TPU v7x, 32 devices: a whole 2x2x4 slice. The times are simulated.
32 devices in a mesh: ctx: 8 (over z, core), fsdp: 4 (over y, x).
Axes of the slice: x: 2, y: 2, z: 4, core: 2. Of those that a mesh axis runs over, the one named last changes fastest.
Arguments:
- tokens: bfloat16 [4, 4096, 1280], P('fsdp', 'ctx'), may hold values from -6 to 6
- lengths: int32 [4], P('fsdp'), may hold values from 1024 to 4096, as said below
- cotangent: bfloat16 [4, 4096, 1280], P('fsdp', 'ctx'), may hold values from -6 to 6
- gain_one: bfloat16 [1280], P('fsdp'), may hold values from 0.5 to 1.5
- query_weight: bfloat16 [1280, 1280], P('fsdp'), may hold values from -0.15625 to 0.15625
- key_matrix: bfloat16 [1280, 320], P('fsdp'), may hold values from -0.15625 to 0.15625
- value_matrix: bfloat16 [1280, 320], P('fsdp'), may hold values from -0.15625 to 0.15625
- out_weight: bfloat16 [1280, 1280], P('fsdp'), may hold values from -4 to 4
- gain_two: bfloat16 [1280], P('fsdp'), may hold values from 0.5 to 1.5
- gate_weight: bfloat16 [1280, 3584], P('fsdp'), may hold values from -0.15625 to 0.15625
- up_weight: bfloat16 [1280, 3584], P('fsdp'), may hold values from -0.15625 to 0.15625
- down_weight: bfloat16 [3584, 1280], P('fsdp'), may hold values from -0.09375 to 0.09375
Outputs:
- output: bfloat16 [4, 4096, 1280], P('fsdp', 'ctx')
- grad_tokens: bfloat16 [4, 4096, 1280], P('fsdp', 'ctx')
- grad_gain_one: float32 [1280], P('fsdp')
- grad_query: float32 [1280, 1280], P('fsdp')
- grad_key: float32 [1280, 320], P('fsdp')
- grad_value: float32 [1280, 320], P('fsdp')
- grad_out: float32 [1280, 1280], P('fsdp')
- grad_gain_two: float32 [1280], P('fsdp')
- grad_gate: float32 [1280, 3584], P('fsdp')
- grad_up: float32 [1280, 3584], P('fsdp')
- grad_down: float32 [3584, 1280], P('fsdp')
Inputs may be any that keep to these rules, and one draw needn't show every extreme that they name: Slot s holds valid tokens at its first lengths[s] positions. One slot of all, chosen by the seed, has length 4096.
All inputs are finite; a program needn't handle non-finite values.
Results may differ from a plain program's by a relative error of at most 0.024.
Values may be sent and summed in bfloat16 or wider, within the bound.
No kernel may reach another device: no remote copies, remote signals or barrier semaphores. Data moves between devices by JAX's collectives and lax.ppermute only.
A program may use at most 192 MiB of HBM per device.

v0:
```python
import math

import jax
import jax.numpy as jnp
from jax import lax
from jax.sharding import PartitionSpec as P

QUERY_HEADS = 20
KEY_VALUE_HEADS = 5
HEAD_SIZE = 64


epsilon = 1e-05


def apply_rotation(vectors, cosine_factor, sine_factor):
    half_size = vectors.shape[-1] // 2
    first_half = vectors[..., :half_size]
    second_half = vectors[..., half_size:]
    return jnp.concatenate(
        [
            first_half * cosine_factor - second_half * sine_factor,
            second_half * cosine_factor + first_half * sine_factor,
        ],
        -1,
    )


def angles(positions):
    exponent = jnp.arange(HEAD_SIZE // 2).astype(jnp.float32) * (2.0 / HEAD_SIZE)
    frequency = jnp.power(10000.0, -exponent)
    phase_angle = positions.astype(jnp.float32)[:, None] * frequency[None, :]
    return (jnp.cos(phase_angle)[:, None, :], jnp.sin(phase_angle)[:, None, :])


def rms_scale(values):
    return lax.rsqrt(jnp.mean(values * values, -1, keepdims=True) + epsilon)


def norm_back(grad_normed, values, scale_rows, gain):
    weighted = grad_normed * gain
    cubed = scale_rows * scale_rows * scale_rows
    return scale_rows * weighted - values * cubed * jnp.mean(weighted * values, -1, keepdims=True)


def split_pairs(block_row_count):
    local_slots, key_total = (block_row_count.shape[0], block_row_count.shape[1])
    key_slice = block_row_count[..., : KEY_VALUE_HEADS * HEAD_SIZE].reshape(
        local_slots, key_total, KEY_VALUE_HEADS, HEAD_SIZE
    )
    value_slice = block_row_count[..., KEY_VALUE_HEADS * HEAD_SIZE :].reshape(
        local_slots, key_total, KEY_VALUE_HEADS, HEAD_SIZE
    )
    return (key_slice, value_slice)


def mask_for(query_pos, key_start, key_total, lengths):
    key_pos = key_start + jnp.arange(key_total, dtype=jnp.int32)
    allowed = (key_pos[None, None, :] <= query_pos[None, :, None]) & (
        key_pos[None, None, :] < lengths[:, None, None]
    )
    return allowed[:, None, None]


def score_grads(
    query_heads,
    grad_heads,
    delta_rows,
    log_total,
    query_pos,
    key_slice,
    value_slice,
    key_start,
    lengths,
    score_scale,
):
    scores = score_scale * jnp.einsum(
        "shgqd,skhd->shgqk", query_heads, key_slice, preferred_element_type=jnp.float32
    )
    allowed = mask_for(query_pos, key_start, key_slice.shape[1], lengths)
    probs_block = jnp.where(allowed, jnp.exp(scores - log_total), 0.0)
    grad_probs = jnp.einsum(
        "shgqd,skhd->shgqk", grad_heads, value_slice, preferred_element_type=jnp.float32
    )
    grad_scores = (probs_block * (grad_probs - delta_rows)).astype(jnp.bfloat16)
    return (grad_scores, probs_block)


def attend_piece(fold_state, piece, query_heads, query_pos, lengths, score_scale):
    key_total = piece.shape[1]
    step_size = math.gcd(key_total, 512)
    steps_total = key_total // step_size
    blocks = jnp.moveaxis(
        piece.reshape(piece.shape[0], steps_total, step_size, piece.shape[2]), 1, 0
    )
    starts = step_size * jnp.arange(steps_total, dtype=jnp.int32)
    last_query = query_pos[-1]

    def one_block(state_now, block_item):
        block_row_count, block_start = block_item

        def one_work(state_in):
            running, row_max, row_total = state_in
            key_slice, value_slice = split_pairs(block_row_count)
            scores = score_scale * jnp.einsum(
                "shgqd,skhd->shgqk", query_heads, key_slice, preferred_element_type=jnp.float32
            )
            allowed = mask_for(query_pos, block_start, step_size, lengths)
            scores = jnp.where(allowed, scores, -1e30)
            new_max = jnp.maximum(row_max, jnp.max(scores, -1, keepdims=True))
            weights = jnp.where(allowed, jnp.exp(scores - new_max), 0.0)
            fading = jnp.exp(row_max - new_max)
            row_total = row_total * fading + jnp.sum(weights, -1, keepdims=True)
            running = running * fading + jnp.einsum(
                "shgqk,skhd->shgqd",
                weights.astype(jnp.bfloat16),
                value_slice,
                preferred_element_type=jnp.float32,
            )
            return (running, new_max, row_total)

        def one_keep(state_in):
            return state_in

        return (lax.cond(block_start <= last_query, one_work, one_keep, state_now), None)

    fold_state, unused = lax.scan(one_block, fold_state, (blocks, starts))
    return fold_state


def local(
    tokens,
    lengths,
    cotangent,
    gain_one,
    query_weight,
    key_matrix,
    value_matrix,
    out_weight,
    gain_two,
    gate_weight,
    up_weight,
    down_weight,
):
    local_slots, block_length, model_width = tokens.shape
    ctx_count = lax.axis_size("ctx")
    group_width = QUERY_HEADS // KEY_VALUE_HEADS
    score_scale = 1.0 / math.sqrt(HEAD_SIZE)
    row_number = local_slots * block_length
    pair_span = 2 * KEY_VALUE_HEADS * HEAD_SIZE
    block_first = lax.axis_index("ctx") * block_length
    query_pos = block_first + jnp.arange(block_length, dtype=jnp.int32)
    last_query = query_pos[-1]
    cosine_factor, sine_factor = angles(query_pos)
    attn_full = (
        lax.all_gather(gain_one, "fsdp", axis=0, tiled=True),
        lax.all_gather(query_weight, "fsdp", axis=0, tiled=True),
        lax.all_gather(key_matrix, "fsdp", axis=0, tiled=True),
        lax.all_gather(value_matrix, "fsdp", axis=0, tiled=True),
        lax.all_gather(out_weight, "fsdp", axis=0, tiled=True),
    )
    ffn_full = (
        lax.all_gather(gain_two, "fsdp", axis=0, tiled=True),
        lax.all_gather(gate_weight, "fsdp", axis=0, tiled=True),
        lax.all_gather(up_weight, "fsdp", axis=0, tiled=True),
        lax.all_gather(down_weight, "fsdp", axis=0, tiled=True),
    )
    gain_first, query_full, key_full, value_full, out_full = attn_full
    gain_second, gate_full, up_full, down_full = ffn_full
    gain_first = gain_first.astype(jnp.float32)
    gain_second = gain_second.astype(jnp.float32)
    token_rows = tokens.reshape(row_number, model_width).astype(jnp.float32)
    scale_one = rms_scale(token_rows)
    normalized_input = (token_rows * scale_one * gain_first).astype(jnp.bfloat16)
    query_pre = jnp.dot(normalized_input, query_full, preferred_element_type=jnp.float32).reshape(
        local_slots, block_length, QUERY_HEADS, HEAD_SIZE
    )
    rotated_query = apply_rotation(query_pre, cosine_factor, sine_factor).astype(jnp.bfloat16)
    query_heads = jnp.transpose(
        rotated_query.reshape(local_slots, block_length, KEY_VALUE_HEADS, group_width, HEAD_SIZE),
        (0, 2, 3, 1, 4),
    )
    key_pre = jnp.dot(normalized_input, key_full, preferred_element_type=jnp.float32).reshape(
        local_slots, block_length, KEY_VALUE_HEADS, HEAD_SIZE
    )
    key_row_block = (
        apply_rotation(key_pre, cosine_factor, sine_factor)
        .astype(jnp.bfloat16)
        .reshape(local_slots, block_length, KEY_VALUE_HEADS * HEAD_SIZE)
    )
    value_row_block = (
        jnp.dot(normalized_input, value_full, preferred_element_type=jnp.float32)
        .astype(jnp.bfloat16)
        .reshape(local_slots, block_length, KEY_VALUE_HEADS * HEAD_SIZE)
    )
    pairs = jnp.concatenate([key_row_block, value_row_block], -1)
    head_layout = (local_slots, KEY_VALUE_HEADS, group_width, block_length)
    initial = (
        jnp.zeros(head_layout + (HEAD_SIZE,), jnp.float32),
        jnp.full(head_layout + (1,), -1e30, jnp.float32),
        jnp.zeros(head_layout + (1,), jnp.float32),
    )
    fold_state = attend_piece(
        initial,
        lax.all_gather(pairs, "ctx", axis=1, tiled=True),
        query_heads,
        query_pos,
        lengths,
        score_scale,
    )
    running, row_max, row_total = fold_state
    attended_heads = running / row_total
    log_total = row_max + jnp.log(row_total)
    attended = (
        jnp.transpose(attended_heads, (0, 3, 1, 2, 4))
        .reshape(row_number, QUERY_HEADS * HEAD_SIZE)
        .astype(jnp.bfloat16)
    )
    hidden = token_rows + jnp.dot(attended, out_full, preferred_element_type=jnp.float32)
    scale_two = rms_scale(hidden)
    normed_two = (hidden * scale_two * gain_second).astype(jnp.bfloat16)
    gate_pre = jnp.dot(normed_two, gate_full, preferred_element_type=jnp.float32)
    up_pre = jnp.dot(normed_two, up_full, preferred_element_type=jnp.float32)
    sigmoid_gate = jax.nn.sigmoid(gate_pre)
    silu_gate = gate_pre * sigmoid_gate
    inner_act = (silu_gate * up_pre).astype(jnp.bfloat16)
    result = hidden + jnp.dot(inner_act, down_full, preferred_element_type=jnp.float32)
    valid_rows = (query_pos[None, :] < lengths[:, None]).reshape(row_number, 1).astype(jnp.float32)
    output = (
        (valid_rows * result).astype(jnp.bfloat16).reshape(local_slots, block_length, model_width)
    )
    grad_result = valid_rows * cotangent.reshape(row_number, model_width).astype(jnp.float32)
    grad_result_low = grad_result.astype(jnp.bfloat16)
    grad_down = jnp.dot(inner_act.T, grad_result_low, preferred_element_type=jnp.float32)
    grad_inner = jnp.dot(grad_result_low, down_full.T, preferred_element_type=jnp.float32)
    grad_gate_pre = (
        grad_inner * up_pre * sigmoid_gate * (1.0 + gate_pre * (1.0 - sigmoid_gate))
    ).astype(jnp.bfloat16)
    grad_up_pre = (grad_inner * silu_gate).astype(jnp.bfloat16)
    grad_gate = jnp.dot(normed_two.T, grad_gate_pre, preferred_element_type=jnp.float32)
    grad_up = jnp.dot(normed_two.T, grad_up_pre, preferred_element_type=jnp.float32)
    grad_normed_two = jnp.dot(
        grad_gate_pre, gate_full.T, preferred_element_type=jnp.float32
    ) + jnp.dot(grad_up_pre, up_full.T, preferred_element_type=jnp.float32)
    grad_gain_two = jnp.sum(grad_normed_two * hidden * scale_two, 0)
    grad_hidden = grad_result + norm_back(grad_normed_two, hidden, scale_two, gain_second)
    grad_hidden_low = grad_hidden.astype(jnp.bfloat16)
    grad_out = jnp.dot(attended.T, grad_hidden_low, preferred_element_type=jnp.float32)
    attended_gradient = jnp.dot(
        grad_hidden_low, out_full.T, preferred_element_type=jnp.float32
    ).astype(jnp.bfloat16)
    grad_heads = jnp.transpose(
        attended_gradient.reshape(
            local_slots, block_length, KEY_VALUE_HEADS, group_width, HEAD_SIZE
        ),
        (0, 2, 3, 1, 4),
    )
    delta_rows = jnp.sum(grad_heads.astype(jnp.float32) * attended_heads, -1, keepdims=True)
    all_pairs = lax.all_gather(pairs, "ctx", axis=1, tiled=True)
    block_pieces = jnp.moveaxis(
        all_pairs.reshape(local_slots, ctx_count, block_length, pair_span), 1, 0
    )
    block_starts = block_length * jnp.arange(ctx_count, dtype=jnp.int32)
    query_zero = jnp.zeros(head_layout + (HEAD_SIZE,), jnp.float32)

    def back_block(grad_query, block_item):
        block_row_count, block_start = block_item

        def back_work(grad_in):
            key_slice, value_slice = split_pairs(block_row_count)
            grad_scores, probs_block = score_grads(
                query_heads,
                grad_heads,
                delta_rows,
                log_total,
                query_pos,
                key_slice,
                value_slice,
                block_start,
                lengths,
                score_scale,
            )
            grad_in = grad_in + score_scale * jnp.einsum(
                "shgqk,skhd->shgqd", grad_scores, key_slice, preferred_element_type=jnp.float32
            )
            key_gradient_rows = score_scale * jnp.einsum(
                "shgqk,shgqd->skhd", grad_scores, query_heads, preferred_element_type=jnp.float32
            )
            value_gradient_rows = jnp.einsum(
                "shgqk,shgqd->skhd",
                probs_block.astype(jnp.bfloat16),
                grad_heads,
                preferred_element_type=jnp.float32,
            )
            joined = jnp.concatenate(
                [
                    key_gradient_rows.reshape(
                        local_slots, block_length, KEY_VALUE_HEADS * HEAD_SIZE
                    ),
                    value_gradient_rows.reshape(
                        local_slots, block_length, KEY_VALUE_HEADS * HEAD_SIZE
                    ),
                ],
                -1,
            )
            return (grad_in, joined)

        def back_keep(grad_in):
            return (grad_in, jnp.zeros((local_slots, block_length, pair_span), jnp.float32))

        return lax.cond(block_start <= last_query, back_work, back_keep, grad_query)

    grad_query_heads, pair_terms = lax.scan(back_block, query_zero, (block_pieces, block_starts))
    pair_terms = jnp.moveaxis(pair_terms, 0, 1).reshape(
        local_slots, ctx_count * block_length, pair_span
    )
    pair_gradients = lax.psum_scatter(
        pair_terms.astype(jnp.bfloat16), "ctx", scatter_dimension=1, tiled=True
    ).astype(jnp.float32)
    grad_query_rot = jnp.transpose(grad_query_heads, (0, 3, 1, 2, 4)).reshape(
        local_slots, block_length, QUERY_HEADS, HEAD_SIZE
    )
    grad_query_pre = (
        apply_rotation(grad_query_rot, cosine_factor, -sine_factor)
        .astype(jnp.bfloat16)
        .reshape(row_number, QUERY_HEADS * HEAD_SIZE)
    )
    rotated_key_gradient = pair_gradients[..., : KEY_VALUE_HEADS * HEAD_SIZE].reshape(
        local_slots, block_length, KEY_VALUE_HEADS, HEAD_SIZE
    )
    grad_key_pre = (
        apply_rotation(rotated_key_gradient, cosine_factor, -sine_factor)
        .astype(jnp.bfloat16)
        .reshape(row_number, KEY_VALUE_HEADS * HEAD_SIZE)
    )
    value_input_gradient = (
        pair_gradients[..., KEY_VALUE_HEADS * HEAD_SIZE :]
        .reshape(row_number, KEY_VALUE_HEADS * HEAD_SIZE)
        .astype(jnp.bfloat16)
    )
    grad_query = jnp.dot(normalized_input.T, grad_query_pre, preferred_element_type=jnp.float32)
    grad_key = jnp.dot(normalized_input.T, grad_key_pre, preferred_element_type=jnp.float32)
    grad_value = jnp.dot(
        normalized_input.T, value_input_gradient, preferred_element_type=jnp.float32
    )
    grad_normed = jnp.dot(grad_query_pre, query_full.T, preferred_element_type=jnp.float32)
    grad_normed = grad_normed + jnp.dot(
        grad_key_pre, key_full.T, preferred_element_type=jnp.float32
    )
    grad_normed = grad_normed + jnp.dot(
        value_input_gradient, value_full.T, preferred_element_type=jnp.float32
    )
    grad_gain_one = jnp.sum(grad_normed * token_rows * scale_one, 0)
    grad_tokens = (
        (grad_hidden + norm_back(grad_normed, token_rows, scale_one, gain_first))
        .astype(jnp.bfloat16)
        .reshape(local_slots, block_length, model_width)
    )
    shards = (
        lax.psum_scatter(
            grad_gain_one.astype(jnp.bfloat16), "fsdp", scatter_dimension=0, tiled=True
        ).astype(jnp.float32),
        lax.psum_scatter(
            grad_query.astype(jnp.bfloat16), "fsdp", scatter_dimension=0, tiled=True
        ).astype(jnp.float32),
        lax.psum_scatter(
            grad_key.astype(jnp.bfloat16), "fsdp", scatter_dimension=0, tiled=True
        ).astype(jnp.float32),
        lax.psum_scatter(
            grad_value.astype(jnp.bfloat16), "fsdp", scatter_dimension=0, tiled=True
        ).astype(jnp.float32),
        lax.psum_scatter(
            grad_out.astype(jnp.bfloat16), "fsdp", scatter_dimension=0, tiled=True
        ).astype(jnp.float32),
        lax.psum_scatter(
            grad_gain_two.astype(jnp.bfloat16), "fsdp", scatter_dimension=0, tiled=True
        ).astype(jnp.float32),
        lax.psum_scatter(
            grad_gate.astype(jnp.bfloat16), "fsdp", scatter_dimension=0, tiled=True
        ).astype(jnp.float32),
        lax.psum_scatter(
            grad_up.astype(jnp.bfloat16), "fsdp", scatter_dimension=0, tiled=True
        ).astype(jnp.float32),
        lax.psum_scatter(
            grad_down.astype(jnp.bfloat16), "fsdp", scatter_dimension=0, tiled=True
        ).astype(jnp.float32),
    )
    summed = (
        lax.psum(shards[0].astype(jnp.bfloat16), "ctx").astype(jnp.float32),
        lax.psum(shards[1].astype(jnp.bfloat16), "ctx").astype(jnp.float32),
        lax.psum(shards[2].astype(jnp.bfloat16), "ctx").astype(jnp.float32),
        lax.psum(shards[3].astype(jnp.bfloat16), "ctx").astype(jnp.float32),
        lax.psum(shards[4].astype(jnp.bfloat16), "ctx").astype(jnp.float32),
        lax.psum(shards[5].astype(jnp.bfloat16), "ctx").astype(jnp.float32),
        lax.psum(shards[6].astype(jnp.bfloat16), "ctx").astype(jnp.float32),
        lax.psum(shards[7].astype(jnp.bfloat16), "ctx").astype(jnp.float32),
        lax.psum(shards[8].astype(jnp.bfloat16), "ctx").astype(jnp.float32),
    )
    return (
        output,
        grad_tokens,
        summed[0],
        summed[1],
        summed[2],
        summed[3],
        summed[4],
        summed[5],
        summed[6],
        summed[7],
        summed[8],
    )


def solution(mesh):
    return jax.shard_map(
        local,
        mesh=mesh,
        in_specs=(
            P("fsdp", "ctx", None),
            P("fsdp"),
            P("fsdp", "ctx", None),
            P("fsdp"),
            P("fsdp", None),
            P("fsdp", None),
            P("fsdp", None),
            P("fsdp", None),
            P("fsdp"),
            P("fsdp", None),
            P("fsdp", None),
            P("fsdp", None),
        ),
        out_specs=(
            P("fsdp", "ctx", None),
            P("fsdp", "ctx", None),
            P("fsdp"),
            P("fsdp", None),
            P("fsdp", None),
            P("fsdp", None),
            P("fsdp", None),
            P("fsdp"),
            P("fsdp", None),
            P("fsdp", None),
            P("fsdp", None),
        ),
        check_vma=False,
    )
```

profile of v0, /device:TPU:0, one launch (start us, length us, event | category | flops | bytes accessed | tf_op | source)
XLA Modules:
  0.0 1596.8 jit_solution(11342410206617651296)
XLA Ops:
  11.7 11.5 all-reduce.7
  23.2 16.8 %all_gather.32 = bf16[1280,320]{1,0:T(8,128)(2,1)S(1)} all-gather(bf16[320,320]{1,0:T(8,128)(2,1)} %param.25), channel_id=1, replica_groups=mesh['ctx'=8,'fsdp'=4] {'fsdp'}, dimensions={0}, use_global_device_ids=true | all-gather | bytes 1024000 | tf_op jit(solution)/shard_map/all_gather | solution.py:158
  43.6 22.1 %all_gather.33 = bf16[1280,320]{1,0:T(8,128)(2,1)S(1)} all-gather(bf16[320,320]{1,0:T(8,128)(2,1)S(1)} %copy-done.21), channel_id=1, replica_groups=mesh['ctx'=8,'fsdp'=4] {'fsdp'}, dimensions={0}, use_global_device_ids=true | all-gather | bytes 1024000 | tf_op jit(solution)/shard_map/all_gather | solution.py:159
  74.0 5.7 copy.48
  79.6 4.2 convolution_bitcast_fusion
  85.4 43.6 %all-gather.7.cloned.1.call-done = bf16[1,4096,640]{1,2,0:T(8,128)(2,1)} async-done(((bf16[1,512,640]{1,2,0:T(8,128)(2,1)}), bf16[1,4096,640]{1,2,0:T(8,128)(2,1)}) %all-gather.7.cloned.1.call-update) | async-done | bytes 5242896 | tf_op jit(solution)/shard_map/all_gather | solution.py:205
  129.0 5.4 copy.75
  136.3 37.3 %while.31 = (s32[]{:T(128)}, f32[1,5,4,512,64]{3,4,2,1,0:T(8,128)}, f32[1,5,4,512,1]{3,2,1,4,0:T(4,128)S(1)}, f32[1,5,4,512,1]{3,2,1,4,0:T(4,128)S(1)}, s32[8]{0...) while((s32[]{:T(128)}, f32[1,5,4,512,64]{3,4,2,1,0:T(8,128)}, ...), condition=%wide.region_6.7_spmd.clone, body=%wide.region_1.6_spmd.clone.sunk | while | flops 1412202496 | bytes 74462504 | solution.py:127
  138.2 21.7 %conditional.6 = ((f32[1,5,4,512,64]{3,4,2,1,0:T(8,128)}, f32[1,5,4,512,1]{3,2,1,4,0:T(4,128)S(1)}, f32[1,5,4,512,1]{3,2,1,4,0:T(4,128)S(1)})) conditional(s32[]{:T(128)} %convert_element_type.474, (f32[1,5,4,512,64]{3,4,2,1,0:T(8,128)}, f32[1,5,4,512,1]{3,2,1,4,0:T(4,128)S(1)}, f32[1,5,4,512,1]{3,2,1,4,0:T(4,128)S(1)}) %tuple.97, (s32[]{:T(128)}, ...), branch_computations={%region_2.2_spmd, %region_3.5_spmd} | conditional | flops 1412202496 | bytes 74460208 | solution.py:125
  141.7 4.8 fusion.4
  146.6 8.0 bitcast_add_fusion
  154.7 5.2 fusion.5
  173.6 3.2 fusion.80
  176.8 4.8 multiply_reduce_fusion.3
  183.2 87.5 %all-gather.13.cloned.1.call-done = bf16[1280,3584]{1,0:T(8,128)(2,1)} async-done(((bf16[320,3584]{1,0:T(8,128)(2,1)}), bf16[1280,3584]{1,0:T(8,128)(2,1)}) %all-gather.13.cloned.1.call-update) | async-done | bytes 9175056 | tf_op jit(solution)/shard_map/all_gather | solution.py:164
  270.7 12.6 fusion.99
  283.3 83.3 %all-gather.15.cloned.1.call-done = bf16[1280,3584]{1,0:T(8,128)(2,1)} async-done(((bf16[320,3584]{1,0:T(8,128)(2,1)}), bf16[1280,3584]{1,0:T(8,128)(2,1)}) %all-gather.15.cloned.1.call-update) | async-done | bytes 9175056 | tf_op jit(solution)/shard_map/all_gather | solution.py:165
  366.6 12.6 fusion.100
  379.1 83.3 %all-gather.17.cloned.1.call-done = bf16[3584,1280]{1,0:T(8,128)(2,1)} async-done(((bf16[896,1280]{1,0:T(8,128)(2,1)}), bf16[3584,1280]{1,0:T(8,128)(2,1)}) %all-gather.17.cloned.1.call-update) | async-done | bytes 9175056 | tf_op jit(solution)/shard_map/all_gather | solution.py:166
  462.4 15.8 multiply_convert_fusion
  478.3 9.8 fusion.101
  488.1 9.6 multiply_reduce_fusion
  507.8 68.8 %while.32 = (s32[]{:T(128)}, f32[1,5,4,512,64]{3,4,2,1,0:T(8,128)}, bf16[8,1,512,640]{3,2,0,1:T(8,128)(2,1)}, s32[8]{0:T(128)S(1)}, s32[]{:T(128)}, /*index=5*/s...) while((s32[]{:T(128)}, f32[1,5,4,512,64]{3,4,2,1,0:T(8,128)}, ...), condition=%wide.region_13.14_spmd.clone, body=%wide.region_10.13_spmd.clone.sunk | while | flops 3411347456 | bytes 113973336 | solution.py:313
  510.1 43.4 %conditional.7 = (f32[1,5,4,512,64]{3,4,2,1,0:T(8,128)}, bf16[1,1,512,640]{2,3,1,0:T(8,128)(2,1)S(1)}) conditional(s32[]{:T(128)} %convert_element_type.475, f32[1,5,4,512,64]{3,4,2,1,0:T(8,128)} %get-tuple-element.674, (s32[]{:T(128)}, s32[]{:T(128)}, s32[1]{0:T(128)}, bf16[8,1,512,640]{2,3,1,0:T(8,128)(2,1)}, s32[]{:T(128)}, ...), branch_computations={%region_11.11_spmd, %region_12.12_spmd} | conditional | flops 3411347456 | bytes 111348768 | solution.py:311
  511.3 9.9 fusion.27
  523.2 11.1 fusion.18
  534.3 5.2 bitcast_add_fusion.2
  539.5 9.4 fusion.20
  548.8 4.6 fusion.32
  581.0 3.8 convolution_convert_fusion.4
  586.0 5.2 convolution_convert_fusion.3
  591.4 348.2 %reduce-scatter.9.cloned.1.call-done = bf16[1,512,640]{2,1,0:T(8,128)(2,1)} async-done(((bf16[1,4096,640]{2,1,0:T(8,128)(2,1)}), bf16[1,512,640]{2,1,0:T(8,128)(2,1)}) %reduce-scatter.9.cloned.1.call-update) | async-done | bytes 655376 | tf_op jit(solution)/shard_map/reduce_scatter | solution.py:317
  945.1 11.0 convolution_convert_fusion.1
  956.4 11.2 convolution_convert_fusion
  968.2 11.0 convolution_convert_fusion.2
  979.5 6.6 reduce-scatter.11.cloned.1.call-done
  986.1 48.1 %reduce-scatter.17.cloned.1.call-done = bf16[320,1280]{1,0:T(8,128)(2,1)} async-done(((bf16[1280,1280]{1,0:T(8,128)(2,1)}), bf16[320,1280]{1,0:T(8,128)(2,1)}) %reduce-scatter.17.cloned.1.call-update) | async-done | bytes 819216 | tf_op jit(solution)/shard_map/reduce_scatter | solution.py:372
  1034.2 30.7 %reduce-scatter.13.cloned.1.call-done = bf16[320,320]{1,0:T(8,128)(2,1)} async-done(((bf16[1280,320]{1,0:T(8,128)(2,1)}), bf16[320,320]{1,0:T(8,128)(2,1)}) %reduce-scatter.13.cloned.1.call-update) | async-done | bytes 204816 | tf_op jit(solution)/shard_map/reduce_scatter | solution.py:366
  1064.8 30.8 %reduce-scatter.15.cloned.1.call-done = bf16[320,320]{1,0:T(8,128)(2,1)} async-done(((bf16[1280,320]{1,0:T(8,128)(2,1)}), bf16[320,320]{1,0:T(8,128)(2,1)}) %reduce-scatter.15.cloned.1.call-update) | async-done | bytes 204816 | tf_op jit(solution)/shard_map/reduce_scatter | solution.py:369
  1095.7 95.9 %reduce-scatter.19.cloned.1.call-done = bf16[320,3584]{1,0:T(8,128)(2,1)} async-done(((bf16[1280,3584]{1,0:T(8,128)(2,1)}), bf16[320,3584]{1,0:T(8,128)(2,1)}) %reduce-scatter.19.cloned.1.call-update) | async-done | bytes 2293776 | tf_op jit(solution)/shard_map/reduce_scatter | solution.py:378
  1191.6 96.0 %reduce-scatter.21.cloned.1.call-done = bf16[320,3584]{1,0:T(8,128)(2,1)} async-done(((bf16[1280,3584]{1,0:T(8,128)(2,1)}), bf16[320,3584]{1,0:T(8,128)(2,1)}) %reduce-scatter.21.cloned.1.call-update) | async-done | bytes 2293776 | tf_op jit(solution)/shard_map/reduce_scatter | solution.py:381
  1287.6 95.9 %reduce-scatter.23.cloned.1.call-done = bf16[896,1280]{1,0:T(8,128)(2,1)} async-done(((bf16[3584,1280]{1,0:T(8,128)(2,1)}), bf16[896,1280]{1,0:T(8,128)(2,1)}) %reduce-scatter.23.cloned.1.call-update) | async-done | bytes 2293776 | tf_op jit(solution)/shard_map/reduce_scatter | solution.py:384
  1384.2 4.4 fusion.102
  1388.6 10.1 fusion.45
  1402.7 8.6 all-reduce.6
  1411.5 15.6 all-reduce.4
  1428.2 4.4 fusion.60
  1432.6 144.0 %all-reduce.10.cloned.1.call-done = (bf16[320,1280]{1,0:T(8,128)(2,1)}, bf16[320,320]{1,0:T(8,128)(2,1)}, bf16[320,320]{1,0:T(8,128)(2,1)}, bf16[320,1280]{1,0:T...) async-done(((bf16[320,1280]{1,0:T(8,128)(2,1)}, bf16[320,320]{1,0:T(8,128)(2,1)}, bf16[320,320]{1,0:T(8,128)(2,1)}, ...) | async-done | bytes 8929296 | tf_op jit(solution)/shard_map/psum | solution.py:390
  (275 shorter events, 88.1 us)
Async XLA Ops:
  7.2 33.5 %copy-start.2 = (bf16[1,512,1280]{2,1,0:T(8,128)(2,1)S(1)}, bf16[1,512,1280]{2,1,0:T(8,128)(2,1)}, u32[]{:S(2)}) copy-start(bf16[1,512,1280]{2,1,0:T(8,128)(2,1)} %param.20) | copy-start | bytes 3932164
  7.2 66.8 %all-gather.9.cloned.1.call-start = ((), (), s32[]{:S(2)}) async-start(), calls=%async_computation.9 | async-start | bytes 4096000 | tf_op jit(solution)/shard_map/all_gather | solution.py:157
  7.9 121.1 %all-gather.7.cloned.1.call-start = ((), (), s32[]{:S(2)}) async-start(), calls=%async_computation.8 | async-start | bytes 5898240 | tf_op jit(solution)/shard_map/all_gather | solution.py:205
  23.2 56.4 %copy-start.25 = (f32[1280]{0:T(1024)}, f32[1280]{0:T(1024)S(1)}, u32[]{:S(2)}) copy-start(f32[1280]{0:T(1024)S(1)} %convert_element_type.287) | copy-start | bytes 15364
  40.0 3.2 copy-start.7
  41.6 38.0 %copy-start.27 = (f32[512]{0:T(512)}, f32[512]{0:T(512)S(1)}, u32[]{:S(2)}) copy-start(f32[512]{0:T(512)S(1)} %get-tuple-element.462) | copy-start | bytes 6148
  42.6 41.2 %copy-start.15 = (f32[512,32]{0,1:T(8,128)}, f32[512,32]{0,1:T(8,128)S(1)}, u32[]{:S(2)}) copy-start(f32[512,32]{0,1:T(8,128)S(1)} %get-tuple-element.460) | copy-start | bytes 196612
  68.4 108.3 %all-gather.11.cloned.1.call-start = ((), (), s32[]{:S(2)}) async-start(), calls=%async_computation.10 | async-start | bytes 4096000 | tf_op jit(solution)/shard_map/all_gather | solution.py:160
  69.2 201.5 %all-gather.13.cloned.1.call-start = ((), (), s32[]{:S(2)}) async-start(), calls=%async_computation.11 | async-start | bytes 11468800 | tf_op jit(solution)/shard_map/all_gather | solution.py:164
  69.8 296.8 %all-gather.15.cloned.1.call-start = ((), (), s32[]{:S(2)}) async-start(), calls=%async_computation.12 | async-start | bytes 11468800 | tf_op jit(solution)/shard_map/all_gather | solution.py:165
  70.3 392.1 %all-gather.17.cloned.1.call-start = ((), (), s32[]{:S(2)}) async-start(), calls=%async_computation.13 | async-start | bytes 11468800 | tf_op jit(solution)/shard_map/all_gather | solution.py:166
  70.9 868.6 %reduce-scatter.9.cloned.1.call-start = ((), (), s32[]{:S(2)}) async-start(), calls=%async_computation.14 | async-start | bytes 5898240 | tf_op jit(solution)/shard_map/reduce_scatter | solution.py:317
  176.8 4.8 copy-start.24
  181.6 316.1 %copy-start = (f32[512,1280]{1,0:T(8,128)}, f32[512,1280]{1,0:T(8,128)S(1)}, u32[]{:S(2)}) copy-start(f32[512,1280]{1,0:T(8,128)S(1)} %get-tuple-element.468) | copy-start | bytes 7864324
  283.3 179.2 %copy-start.30 = (f32[512]{0:T(512)S(1)}, f32[512]{0:T(512)}, u32[]{:S(2)}) copy-start(f32[512]{0:T(512)} %compare_convert_fusion) | copy-start | bytes 6148
  478.2 9.8 copy-start.36
  488.0 9.6 copy-start.17
  497.7 2.3 copy-start.4
  508.2 1.8 copy-start.33
  554.7 1.8 copy-start.33
  557.8 1.8 copy-start.33
  561.0 1.8 copy-start.33
  567.2 1.8 copy-start.33
  570.3 1.8 copy-start.33
  573.5 1.8 copy-start.33
  576.7 409.4 %reduce-scatter.11.cloned.1.call-start = ((), (), s32[]{:S(2)}) async-start(), calls=%async_computation.15 | async-start | bytes 4096000 | tf_op jit(solution)/shard_map/reduce_scatter | solution.py:363
  577.5 3.4 copy-start.3
  577.5 3.4 copy-start.26
  577.5 3.4 copy-start.28
  584.8 449.4 %reduce-scatter.17.cloned.1.call-start = ((), (), s32[]{:S(2)}) async-start(), calls=%async_computation.18 | async-start | bytes 4096000 | tf_op jit(solution)/shard_map/reduce_scatter | solution.py:372
  591.3 473.5 %reduce-scatter.13.cloned.1.call-start = ((), (), s32[]{:S(2)}) async-start(), calls=%async_computation.16 | async-start | bytes 1228800 | tf_op jit(solution)/shard_map/reduce_scatter | solution.py:366
  941.0 2.1 copy-start.14
  943.0 152.7 %reduce-scatter.15.cloned.1.call-start = ((), (), s32[]{:S(2)}) async-start(), calls=%async_computation.17 | async-start | bytes 1228800 | tf_op jit(solution)/shard_map/reduce_scatter | solution.py:369
  945.1 246.5 %reduce-scatter.19.cloned.1.call-start = ((), (), s32[]{:S(2)}) async-start(), calls=%async_computation.19 | async-start | bytes 11468800 | tf_op jit(solution)/shard_map/reduce_scatter | solution.py:378
  956.1 331.5 %reduce-scatter.21.cloned.1.call-start = ((), (), s32[]{:S(2)}) async-start(), calls=%async_computation.20 | async-start | bytes 11468800 | tf_op jit(solution)/shard_map/reduce_scatter | solution.py:381
  967.5 416.0 %reduce-scatter.23.cloned.1.call-start = ((), (), s32[]{:S(2)}) async-start(), calls=%async_computation.21 | async-start | bytes 11468800 | tf_op jit(solution)/shard_map/reduce_scatter | solution.py:384
  979.2 597.4 %all-reduce.10.cloned.1.call-start = ((), (), s32[]{:S(2)}) async-start(), calls=%async_computation.22 | async-start | bytes 18022400 | tf_op jit(solution)/shard_map/psum | solution.py:390
  1384.2 4.4 copy-start.1
  1384.2 4.4 copy-start.35
  1388.6 10.1 copy-start.8
  1399.9 2.8 copy-start.32
  1399.9 28.3 %copy-start.29 = (f32[512]{0:T(512)S(1)}, f32[512]{0:T(512)}, u32[]{:S(2)}) copy-start(f32[512]{0:T(512)} %get-tuple-element.461) | copy-start | bytes 6148
  1576.6 2.6 copy-start.23
  1576.6 3.4 copy-start.22
  1576.6 4.2 copy-start.19
  1576.6 5.5 copy-start.13
  1582.1 2.7 copy-start.12
  1584.8 2.7 copy-start.11
  (18 other events, 21.1 us)
Sparse Core Ops, SparseCore 0:
  9.9 60.8 all-gather.8
  72.9 56.0 all-gather.6
  130.9 43.8 all-gather.10
  176.5 94.1 all-gather.12
  272.4 94.1 all-gather.14
  368.2 94.1 all-gather.16
  576.8 362.7 reduce-scatter.8
  942.6 43.4 reduce-scatter.10
  989.1 45.0 reduce-scatter.16
  1037.5 27.2 reduce-scatter.12
  1068.4 27.2 reduce-scatter.14
  1098.7 92.8 reduce-scatter.18
  1194.8 92.8 reduce-scatter.20
  1290.7 92.8 reduce-scatter.22
  1386.3 190.2 all-reduce.9
where the time goes:
time: 1600 us
  waiting for transfers between devices  1200 us (75%)
  matrix products  190 us (12%)
  blocking collectives  74.6 us (5%)
  local copies, waits for them, and re-layouts  50.5 us (3%)
  other arithmetic  44.9 us (3%)
  loops' own time  21.6 us (1%)
  between operations  16.6 us (1%)
    reduce_scatter x1, waiting for transfers between devices, local(): lax.psum_scatter(pair_terms.astype(jnp.bfloat16), 'ctx', scatter_dimensio...  348 us
    psum x1, waiting for transfers between devices, local(): lax.psum(shards[1].astype(jnp.bfloat16), 'ctx').astype(jnp.float32)  144 us
    reduce_scatter x1, waiting for transfers between devices, local(): lax.psum_scatter(grad_up.astype(jnp.bfloat16), 'fsdp', scatter_dimension=...  96 us
    reduce_scatter x1, waiting for transfers between devices, local(): lax.psum_scatter(grad_down.astype(jnp.bfloat16), 'fsdp', scatter_dimensio...  95.9 us
    reduce_scatter x1, waiting for transfers between devices, local(): lax.psum_scatter(grad_gate.astype(jnp.bfloat16), 'fsdp', scatter_dimensio...  95.9 us
    all_gather x1, waiting for transfers between devices, local(): lax.all_gather(gate_weight, 'fsdp', axis=0, tiled=True)  87.5 us
    all_gather x1, waiting for transfers between devices, local(): lax.all_gather(down_weight, 'fsdp', axis=0, tiled=True)  83.3 us
    all_gather x1, waiting for transfers between devices, local(): lax.all_gather(up_weight, 'fsdp', axis=0, tiled=True)  83.3 us
  transfers between devices with their start and end apart: 15, of which 13 were waited for; matrix products, arithmetic and copies ran while one was open for 10% of the time, Pallas kernels for 0%

commit v1 on v0

v1 whole, which is shorter than its diff:
```python
import functools
import math

import jax
import jax.numpy as jnp
from jax import lax
from jax.experimental import pallas as pl
from jax.experimental.pallas import tpu as pltpu
from jax.sharding import PartitionSpec as P

QUERY_HEADS = 20
KEY_VALUE_HEADS = 5
GROUP = QUERY_HEADS // KEY_VALUE_HEADS
HEAD_SIZE = 64
PAIR = 2 * HEAD_SIZE
HALF_HEAD = HEAD_SIZE // 2
epsilon = 1e-05
LOG2E = math.log2(math.e)
SCORE_SCALE = 1.0 / math.sqrt(HEAD_SIZE)
NEGATIVE = -1e30
EXTRA = 16
f32 = jnp.float32
bf16 = jnp.bfloat16


def rms_scale(values):
    return lax.rsqrt(jnp.mean(values * values, -1, keepdims=True) + epsilon)


def norm_back(grad_normed, values, scale_rows, gain):
    weighted = grad_normed * gain
    cubed = scale_rows * scale_rows * scale_rows
    return scale_rows * weighted - values * cubed * jnp.mean(weighted * values, -1, keepdims=True)


def swap_halves(x):
    lane = lax.broadcasted_iota(jnp.int32, x.shape, 1)
    ahead = pltpu.roll(x, PAIR - HALF_HEAD, 1)
    behind = pltpu.roll(x, HALF_HEAD, 1)
    return jnp.where(lane % HEAD_SIZE < HALF_HEAD, ahead, behind)


def project_kernel(x_ref, w_ref, cos_ref, sin_ref, q_ref, kv_ref):
    step = pl.program_id(0)
    width = w_ref.shape[1]
    product = jnp.dot(x_ref[...], w_ref[...], preferred_element_type=f32)
    is_pair = step == pl.num_programs(0) - 1
    lane = lax.broadcasted_iota(jnp.int32, cos_ref.shape, 1)
    plain = jnp.logical_and(is_pair, lane >= HEAD_SIZE)
    cos = jnp.where(plain, 1.0, cos_ref[...])
    sin = jnp.where(plain, 0.0, sin_ref[...])
    pieces = []
    for at in range(0, width, PAIR):
        part = product[:, at : at + PAIR]
        pieces.append((part * cos + swap_halves(part) * sin).astype(bf16))

    @pl.when(is_pair)
    def _():
        for i, piece in enumerate(pieces):
            kv_ref[:, i * PAIR : (i + 1) * PAIR] = piece

    @pl.when(jnp.logical_not(is_pair))
    def _():
        for i, piece in enumerate(pieces):
            q_ref[:, i * PAIR : (i + 1) * PAIR] = piece


def project(normed, weights, cos, sin):
    rows, model = normed.shape
    width = KEY_VALUE_HEADS * PAIR
    steps = weights.shape[1] // width
    return pl.pallas_call(
        project_kernel,
        grid=(steps,),
        in_specs=[
            pl.BlockSpec((rows, model), lambda i: (0, 0)),
            pl.BlockSpec((model, width), lambda i: (0, i)),
            pl.BlockSpec((rows, PAIR), lambda i: (0, 0)),
            pl.BlockSpec((rows, PAIR), lambda i: (0, 0)),
        ],
        out_specs=[
            pl.BlockSpec((rows, width), lambda i: (0, jnp.minimum(i, steps - 2))),
            pl.BlockSpec((rows, width), lambda i: (0, 0)),
        ],
        out_shape=[
            jax.ShapeDtypeStruct((rows, width * (steps - 1)), bf16),
            jax.ShapeDtypeStruct((rows, width), bf16),
        ],
        compiler_params=pltpu.CompilerParams(vmem_limit_bytes=40 << 20),
        cost_estimate=pl.CostEstimate(
            flops=2 * rows * model * width * steps,
            bytes_accessed=2 * model * width * steps + 4 * rows * model,
            transcendentals=0,
        ),
        name="project",
    )(normed, weights, cos, sin)


def unrotate_kernel(x_ref, cos_ref, sin_ref, out_ref):
    lane = lax.broadcasted_iota(jnp.int32, cos_ref.shape, 1)
    cos = jnp.where(lane >= HEAD_SIZE, 1.0, cos_ref[...])
    sin = jnp.where(lane >= HEAD_SIZE, 0.0, sin_ref[...])
    for at in range(0, x_ref.shape[1], PAIR):
        part = x_ref[:, at : at + PAIR].astype(f32)
        out_ref[:, at : at + PAIR] = (part * cos - swap_halves(part) * sin).astype(bf16)


def unrotate(x, cos, sin):
    return pl.pallas_call(
        unrotate_kernel, out_shape=jax.ShapeDtypeStruct(x.shape, bf16), name="unrotate"
    )(x, cos, sin)


def block_row(block, blocks, half):
    device = jnp.minimum(block, blocks - 1 - block)
    return pl.multiple_of(device * (2 * half) + (block % 2) * half, half)


def two_blocks(ref, step, blocks, half):
    first = ref[pl.ds(block_row(2 * step, blocks, half), half), :]
    second = ref[pl.ds(block_row(2 * step + 1, blocks, half), half), :]
    return jnp.concatenate([first, second], 0)


def one_head(ref, rows, head, low):
    part = ref[rows, (head // 2) * PAIR : (head // 2 + 1) * PAIR].astype(f32)
    lane = lax.broadcasted_iota(jnp.int32, part.shape, 1)
    if (head % 2 == 0) != low:
        part = pltpu.roll(part, HEAD_SIZE, 1)
    keep = lane < HEAD_SIZE if low else lane >= HEAD_SIZE
    return jnp.where(keep, part, 0.0).astype(bf16)


def allowed_keys(step, block, length, half):
    shape = (2 * half, half)
    key_pos = lax.broadcasted_iota(jnp.int32, shape, 0) + step * (2 * half)
    query_pos = lax.broadcasted_iota(jnp.int32, shape, 1) + block * half
    return key_pos <= jnp.minimum(query_pos, length - 1)


def key_steps(block, length, half):
    keys = jnp.minimum((block + 1) * half, length)
    return (keys + 2 * half - 1) // (2 * half)


LAST = (((1,), (1,)), ((), ()))


def forward_kernel(blocks, info_ref, q_ref, kv_ref, o_ref, lse_ref, q_sc, m_sc, l_sc, acc_sc):
    half = q_ref.shape[0] // 2
    length = info_ref[0]
    for slot in range(2):
        block = info_ref[1 + slot]
        rows = slice(slot * half, (slot + 1) * half)
        for head in range(GROUP):
            q_sc[head] = one_head(q_ref, rows, head, True)
        m_sc[...] = jnp.full_like(m_sc, NEGATIVE)
        l_sc[...] = jnp.zeros_like(l_sc)
        acc_sc[...] = jnp.zeros_like(acc_sc)

        def work(step, masked):
            pair = two_blocks(kv_ref, step, blocks, half)
            pair_t = pair.T
            if masked:
                allowed = allowed_keys(step, block, length, half)
            for head in range(GROUP):
                scores = lax.dot_general(pair, q_sc[head], LAST, preferred_element_type=f32)
                scores = scores * (SCORE_SCALE * LOG2E)
                if masked:
                    scores = jnp.where(allowed, scores, NEGATIVE)
                m_old = m_sc[head]
                m_new = jnp.maximum(m_old, jnp.max(scores, 0, keepdims=True))
                weights = jnp.exp2(scores - m_new)
                fading = jnp.exp2(m_old - m_new)
                m_sc[head] = m_new
                l_sc[head] = l_sc[head] * fading + jnp.sum(weights, 0, keepdims=True)
                acc_sc[head] = acc_sc[head] * fading + jnp.dot(
                    pair_t, weights.astype(bf16), preferred_element_type=f32
                )

        steps = key_steps(block, length, half)

        @pl.loop(0, steps - 1)
        def _(step):
            work(step, False)

        work(steps - 1, True)
        for at in range(0, GROUP, 2):
            two = [
                acc_sc[head][HEAD_SIZE:, :] / l_sc[head] for head in (at, at + 1)
            ]
            o_ref[rows, at * HEAD_SIZE : (at + 2) * HEAD_SIZE] = (
                jnp.concatenate(two, 0).T.astype(bf16)
            )
        for head in range(GROUP):
            lse_ref[0, head : head + 1, rows] = m_sc[head] + jnp.log2(l_sc[head])


def attend(q, pairs, info):
    rows, keys = q.shape[0], pairs.shape[0]
    half = rows // 2
    width = GROUP * HEAD_SIZE
    work = QUERY_HEADS * rows * (keys // 2)
    return pl.pallas_call(
        functools.partial(forward_kernel, keys // half),
        grid_spec=pltpu.PrefetchScalarGridSpec(
            num_scalar_prefetch=1,
            grid=(KEY_VALUE_HEADS,),
            in_specs=[
                pl.BlockSpec((rows, width), lambda g, info: (0, g)),
                pl.BlockSpec((keys, PAIR), lambda g, info: (0, g)),
            ],
            out_specs=[
                pl.BlockSpec((rows, width), lambda g, info: (0, g)),
                pl.BlockSpec((1, GROUP, rows), lambda g, info: (g, 0, 0)),
            ],
            scratch_shapes=[
                pltpu.VMEM((GROUP, half, PAIR), bf16),
                pltpu.VMEM((GROUP, 1, half), f32),
                pltpu.VMEM((GROUP, 1, half), f32),
                pltpu.VMEM((GROUP, PAIR, half), f32),
            ],
        ),
        out_shape=[
            jax.ShapeDtypeStruct(q.shape, bf16),
            jax.ShapeDtypeStruct((KEY_VALUE_HEADS, GROUP, rows), f32),
        ],
        compiler_params=pltpu.CompilerParams(vmem_limit_bytes=40 << 20),
        cost_estimate=pl.CostEstimate(
            flops=16 * work * HEAD_SIZE, bytes_accessed=2 * keys * 640, transcendentals=work
        ),
        name="attend",
    )(info, q, pairs)


def backward_kernel(
    blocks, info_ref, q_ref, do_ref, o_ref, lse_ref, kv_ref, cos_ref, sin_ref,
    dq_ref, dkv_ref, both_sc, delta_sc, dq_sc, dkv_sc, terms_sc,
):
    half = q_ref.shape[0] // 2
    length = info_ref[0]
    dkv_sc[...] = jnp.zeros_like(dkv_sc)
    for slot in range(2):
        block = info_ref[1 + slot]
        rows = slice(slot * half, (slot + 1) * half)
        for head in range(GROUP):
            both_sc[2 * head] = one_head(q_ref, rows, head, True)
            both_sc[2 * head + 1] = one_head(do_ref, rows, head, False)
        for at in range(0, GROUP, 2):
            lanes = slice(at * HEAD_SIZE, (at + 2) * HEAD_SIZE)
            product = (do_ref[rows, lanes].astype(f32) * o_ref[rows, lanes].astype(f32)).T
            for i in range(2):
                delta_sc[at + i] = jnp.sum(
                    product[i * HEAD_SIZE : (i + 1) * HEAD_SIZE], 0, keepdims=True
                )
        dq_sc[...] = jnp.zeros_like(dq_sc)

        def work(step, masked):
            pair = two_blocks(kv_ref, step, blocks, half)
            pair_t = pair.T
            if masked:
                allowed = allowed_keys(step, block, length, half)
            for head in range(GROUP):
                scores = lax.dot_general(pair, both_sc[2 * head], LAST, preferred_element_type=f32)
                lse = lse_ref[0, head : head + 1, rows]
                probs = jnp.exp2(scores * (SCORE_SCALE * LOG2E) - lse)
                if masked:
                    probs = jnp.where(allowed, probs, 0.0)
                grad_probs = lax.dot_general(
                    pair, both_sc[2 * head + 1], LAST, preferred_element_type=f32
                )
                grad_scores = (probs * (grad_probs - delta_sc[head])).astype(bf16)
                terms_sc[:, 2 * head * half : (2 * head + 1) * half] = grad_scores
                terms_sc[:, (2 * head + 1) * half : (2 * head + 2) * half] = probs.astype(bf16)
                dq_sc[head] += jnp.dot(pair_t, grad_scores, preferred_element_type=f32)
            update = jnp.dot(
                terms_sc[...],
                both_sc[...].reshape(2 * GROUP * half, PAIR),
                preferred_element_type=f32,
            )
            for i in range(2):
                at = pl.ds(block_row(2 * step + i, blocks, half), half)
                dkv_sc[at, :] += update[i * half : (i + 1) * half]

        steps = key_steps(block, length, half)

        @pl.loop(0, steps - 1)
        def _(step):
            work(step, False)

        work(steps - 1, True)
        for at in range(0, GROUP, 2):
            two = [dq_sc[head][:HEAD_SIZE, :] for head in (at, at + 1)]
            grad = jnp.concatenate(two, 0).T * SCORE_SCALE
            grad = grad * cos_ref[rows, :] - swap_halves(grad) * sin_ref[rows, :]
            dq_ref[rows, at * HEAD_SIZE : (at + 2) * HEAD_SIZE] = grad.astype(bf16)
    lane = lax.broadcasted_iota(jnp.int32, dkv_sc.shape, 1)
    dkv_ref[...] = jnp.where(lane < HEAD_SIZE, dkv_sc[...] * SCORE_SCALE, dkv_sc[...]).astype(bf16)


def attend_back(q, grad, attended, lse, pairs, cos, sin, info):
    rows, keys = q.shape[0], pairs.shape[0]
    half = rows // 2
    width = GROUP * HEAD_SIZE
    work = QUERY_HEADS * rows * (keys // 2)
    head_block = pl.BlockSpec((rows, width), lambda g, info: (0, g))
    key_block = pl.BlockSpec((keys, PAIR), lambda g, info: (0, g))
    table = pl.BlockSpec((rows, PAIR), lambda g, info: (0, 0))
    return pl.pallas_call(
        functools.partial(backward_kernel, keys // half),
        grid_spec=pltpu.PrefetchScalarGridSpec(
            num_scalar_prefetch=1,
            grid=(KEY_VALUE_HEADS,),
            in_specs=[
                head_block,
                head_block,
                head_block,
                pl.BlockSpec((1, GROUP, rows), lambda g, info: (g, 0, 0)),
                key_block,
                table,
                table,
            ],
            out_specs=[head_block, key_block],
            scratch_shapes=[
                pltpu.VMEM((2 * GROUP, half, PAIR), bf16),
                pltpu.VMEM((GROUP, 1, half), f32),
                pltpu.VMEM((GROUP, PAIR, half), f32),
                pltpu.VMEM((keys, PAIR), f32),
                pltpu.VMEM((2 * half, 2 * GROUP * half), bf16),
            ],
        ),
        out_shape=[
            jax.ShapeDtypeStruct(q.shape, bf16),
            jax.ShapeDtypeStruct(pairs.shape, bf16),
        ],
        compiler_params=pltpu.CompilerParams(vmem_limit_bytes=48 << 20),
        cost_estimate=pl.CostEstimate(
            flops=40 * work * HEAD_SIZE, bytes_accessed=8 * keys * 640, transcendentals=work
        ),
        name="attend_back",
    )(info, q, grad, attended, lse, pairs, cos, sin)


def place_kernel(count, spots_ref, *refs):
    out_ref, sems = refs[count], refs[count + 1]
    copies = []
    for i, ref in enumerate(refs[:count]):
        start = pl.multiple_of(spots_ref[i], 16)
        copy = pltpu.make_async_copy(ref, out_ref.at[pl.ds(start, ref.shape[0])], sems.at[i])
        copy.start()
        copies.append(copy)
    for copy in copies:
        copy.wait()


def place(pieces, spots, rows):
    count = len(pieces)
    anywhere = pl.BlockSpec(memory_space=pl.ANY)
    width = pieces[0].shape[1]
    return pl.pallas_call(
        functools.partial(place_kernel, count),
        grid_spec=pltpu.PrefetchScalarGridSpec(
            num_scalar_prefetch=1,
            grid=(1,),
            in_specs=[anywhere] * count,
            out_specs=pl.BlockSpec((rows, width), lambda i, spots: (0, 0)),
            scratch_shapes=[pltpu.SemaphoreType.DMA((count,))],
        ),
        out_shape=jax.ShapeDtypeStruct((rows, width), pieces[0].dtype),
        compiler_params=pltpu.CompilerParams(vmem_limit_bytes=24 << 20),
        cost_estimate=pl.CostEstimate(
            flops=0, bytes_accessed=4 * rows * width, transcendentals=0
        ),
        name="place",
    )(jnp.stack(spots).astype(jnp.int32), *pieces)


def split_kernel(parts, core_ref, gate_ref, up_ref, out_ref):
    width = gate_ref.shape[1] // parts // 2
    for core in range(2):

        @pl.when(core_ref[0] == core)
        def _():
            taken = []
            for ref in (gate_ref, up_ref):
                for i in range(parts):
                    at = (2 * i + core) * width
                    taken.append(ref[:, at : at + width])
            out_ref[...] = jnp.concatenate(taken, 1)


def split_columns(core, gate, up, parts):
    rows, width = gate.shape
    block = rows // 2
    spec = pl.BlockSpec((block, width), lambda i, core: (i, 0))
    return pl.pallas_call(
        functools.partial(split_kernel, parts),
        grid_spec=pltpu.PrefetchScalarGridSpec(
            num_scalar_prefetch=1, grid=(2,), in_specs=[spec, spec], out_specs=spec
        ),
        out_shape=jax.ShapeDtypeStruct((rows, width), gate.dtype),
        cost_estimate=pl.CostEstimate(
            flops=0, bytes_accessed=6 * rows * width, transcendentals=0
        ),
        name="split_columns",
    )(core, gate, up)


def merge_kernel(parts, core_ref, own_ref, other_ref, gate_ref, up_ref):
    width = gate_ref.shape[1] // parts // 2
    for core in range(2):

        @pl.when(core_ref[0] == core)
        def _():
            by_core = (own_ref, other_ref) if core == 0 else (other_ref, own_ref)
            for n, out_ref in enumerate((gate_ref, up_ref)):
                taken = []
                for i in range(parts):
                    at = (n * parts + i) * width
                    for ref in by_core:
                        taken.append(ref[:, at : at + width].astype(f32))
                out_ref[...] = jnp.concatenate(taken, 1)


def merge_columns(core, own, other, parts):
    rows, width = own.shape
    block = rows // 4 if rows % 64 == 0 else rows // 2
    spec = pl.BlockSpec((block, width), lambda i, core: (i, 0))
    out = jax.ShapeDtypeStruct((rows, width), f32)
    return pl.pallas_call(
        functools.partial(merge_kernel, parts),
        grid_spec=pltpu.PrefetchScalarGridSpec(
            num_scalar_prefetch=1,
            grid=(rows // block,),
            in_specs=[spec, spec],
            out_specs=[spec, spec],
        ),
        out_shape=[out, out],
        compiler_params=pltpu.CompilerParams(vmem_limit_bytes=24 << 20),
        cost_estimate=pl.CostEstimate(
            flops=0, bytes_accessed=12 * rows * width, transcendentals=0
        ),
        name="merge_columns",
    )(core, own, other)


def after(value, *others):
    return lax.optimization_barrier((value,) + others)[0]


class Moves:
    def __init__(self):
        self.ctx, self.fsdp = lax.axis_size("ctx"), lax.axis_size("fsdp")
        self.me, self.where = lax.axis_index("fsdp"), lax.axis_index("ctx")
        self.core = self.where % 2
        self.square = self.fsdp == 4
        self.line = self.ctx == 8

    def across(self, value, bit):
        return lax.ppermute(value, "fsdp", [(i, i ^ bit) for i in range(self.fsdp)])

    def swap(self, value):
        return lax.ppermute(value, "ctx", [(i, i ^ 1) for i in range(self.ctx)])

    def pick(self, low, high):
        return jnp.where(self.core == 0, low, high)

    def owner(self, half):
        return half if half < self.ctx else 2 * self.ctx - 1 - half

    def balance(self, rows):
        half = rows.shape[0] // 2
        return jnp.concatenate(
            [
                lax.ppermute(
                    rows[i * half : (i + 1) * half],
                    "ctx",
                    [(d, self.owner(2 * d + i)) for d in range(self.ctx)],
                )
                for i in range(2)
            ],
            0,
        )

    def restore(self, rows):
        half = rows.shape[0] // 2
        return jnp.concatenate(
            [
                lax.ppermute(
                    rows[i * half : (i + 1) * half],
                    "ctx",
                    [(self.owner(2 * d + i), d) for d in range(self.ctx)],
                )
                for i in range(2)
            ],
            0,
        )

    def gather(self, own, gate=None):
        if not self.square:
            whole = lax.all_gather(own, "fsdp", axis=0, tiled=True)
            return whole, None
        if gate is not None:
            own = after(own, *gate)
        rows = own.shape[0]
        half = rows // 32 * 16
        by_x, by_y = self.across(own, 1), self.across(own, 2)
        top, bottom = self.across(by_x[:half], 2), self.across(by_y[half:], 1)
        me = self.me
        spots = [me * rows, (me ^ 1) * rows, (me ^ 2) * rows, (me ^ 3) * rows, (me ^ 3) * rows + half]
        whole = place([own, by_x, by_y, top, bottom], spots, 4 * rows)
        return whole, (by_x, by_y)

    def scatter(self, whole):
        if not self.square:
            rows = whole.shape[1]
            return lax.psum_scatter(
                whole.reshape(self.fsdp * rows, -1), "fsdp", scatter_dimension=0, tiled=True
            )
        part = lambda bit: lax.dynamic_index_in_dim(whole, self.me ^ bit, 0, keepdims=False)
        rows = whole.shape[1]
        half = rows // 32 * 16
        far = part(3)
        top, bottom = self.across(far[:half], 1), self.across(far[half:], 2)
        near_x, near_y = part(1), part(2)
        to_x = jnp.concatenate([near_x[:half], near_x[half:] + bottom], 0)
        to_y = jnp.concatenate([near_y[:half] + top, near_y[half:]], 0)
        return part(0) + self.across(to_x, 1) + self.across(to_y, 2)

    def total(self, part):
        if not self.line:
            groups = [list(range(c, self.ctx, 2)) for c in range(2)]
            return lax.psum(part, "ctx", axis_index_groups=groups)
        move = lambda value, pairs: lax.ppermute(
            value, "ctx", [(2 * a + c, 2 * b + c) for a, b in pairs for c in range(2)]
        )
        inner = part + move(part, [(0, 1), (3, 2)])
        summed = lax.optimization_barrier(inner + move(inner, [(1, 2), (2, 1)]))
        outer = move(summed, [(1, 0), (2, 3)])
        z = self.where // 2
        return jnp.where((z == 0) | (z == 3), outer, summed)

    def both_cores(self, part):
        other = self.swap(part)
        return self.pick(part, other), self.pick(other, part)

    def gather_rows(self, own, gate=None):
        rows, width = own.shape
        half = rows // 2
        mine = self.pick(own[:half], own[half:])
        whole, token = self.gather(mine, gate)
        low, high = self.both_cores(whole)
        shape = (self.fsdp, half, width)
        full = jnp.stack([low.reshape(shape), high.reshape(shape)], 1)
        return full.reshape(self.fsdp * rows, width), token

    def reduce_rows(self, grad, extra=None):
        rows = grad.shape[0] // self.fsdp
        parts = grad.reshape(self.fsdp, 2, rows // 2, grad.shape[1])
        if extra is not None:
            parts = jnp.concatenate([parts, extra], 2)
        send = lax.dynamic_index_in_dim(parts, 1 - self.core, 1, keepdims=False)
        keep = lax.dynamic_index_in_dim(parts, self.core, 1, keepdims=False)
        part = self.total(self.scatter(keep + self.swap(send)))
        return self.both_cores(part)


def local(
    tokens,
    lengths,
    cotangent,
    gain_one,
    query_weight,
    key_matrix,
    value_matrix,
    out_weight,
    gain_two,
    gate_weight,
    up_weight,
    down_weight,
):
    slots, block_length, model = tokens.shape
    moves = Moves()
    fsdp = moves.fsdp
    half = block_length // 2
    shard = model // fsdp
    attention_width = QUERY_HEADS * HEAD_SIZE
    pair_width = KEY_VALUE_HEADS * PAIR
    length = lengths[0]

    ctx = moves.where
    last = 2 * moves.ctx - 1
    block_a = jnp.where(ctx % 2 == 0, ctx, last - ctx).astype(jnp.int32)
    block_b = last - block_a
    info = jnp.stack([length, block_a, block_b]).astype(jnp.int32)
    within = jnp.arange(half, dtype=jnp.int32)
    position = jnp.concatenate([block_a * half + within, block_b * half + within])
    exponent = jnp.arange(HALF_HEAD).astype(f32) * (2.0 / HEAD_SIZE)
    phase = position.astype(f32)[:, None] * jnp.power(10000.0, -exponent)[None, :]
    cos, sin = jnp.cos(phase), jnp.sin(phase)
    cos = jnp.concatenate([cos, cos, cos, cos], -1)
    sin = jnp.concatenate([-sin, sin, -sin, sin], -1)
    valid = (position < length).astype(f32)[:, None]

    by_head = lambda w: w.reshape(shard, KEY_VALUE_HEADS, HEAD_SIZE)
    pair_weight = jnp.concatenate([by_head(key_matrix), by_head(value_matrix)], -1)
    weight_in = jnp.concatenate([query_weight, pair_weight.reshape(shard, pair_width)], 1)
    gains = jnp.concatenate([gain_one, gain_two])[None, :]
    gains = jnp.pad(gains, ((0, EXTRA - 1), (0, weight_in.shape[1] - 2 * shard)))
    in_half = shard // 2
    mine = jnp.concatenate([moves.pick(weight_in[:in_half], weight_in[in_half:]), gains], 0)
    whole_in, token = moves.gather(mine)
    whole_in = whole_in.reshape(fsdp, in_half + EXTRA, -1)
    gain_rows = whole_in[:, in_half, : 2 * shard].astype(f32)
    gain_first = gain_rows[:, :shard].reshape(1, model)
    gain_second = gain_rows[:, shard:].reshape(1, model)
    low, high = moves.both_cores(whole_in[:, :in_half])
    full_in = jnp.stack([low, high], 1).reshape(model, -1)
    full_out, token = moves.gather_rows(out_weight, token)
    ff_half = gate_weight.shape[1] // fsdp // 2
    core = moves.core.astype(jnp.int32)[None]
    own_wide = split_columns(core, gate_weight, up_weight, fsdp)
    full_wide, token = moves.gather(own_wide, token)
    own_down = moves.pick(down_weight[:ff_half], down_weight[ff_half:])
    full_down, token = moves.gather(own_down, token)
    ff_core = ff_half * fsdp

    x = moves.balance(tokens.reshape(block_length, model)).astype(f32)
    scale_one = rms_scale(x)
    normed = (x * scale_one * gain_first).astype(bf16)
    queries, pairs = project(normed, full_in, cos, sin)
    all_pairs = lax.all_gather(pairs, "ctx", axis=0, tiled=True)
    attended, log_total = attend(queries, all_pairs, info)
    hidden = x + jnp.dot(attended, full_out, preferred_element_type=f32)
    scale_two = rms_scale(hidden)
    normed_two = (hidden * scale_two * gain_second).astype(bf16)

    grad_result = valid * moves.balance(cotangent.reshape(block_length, model)).astype(f32)
    grad_low = grad_result.astype(bf16)
    both_grad = jnp.concatenate([grad_low, moves.swap(grad_low)], 0)
    both_normed = jnp.concatenate([normed_two, moves.swap(normed_two)], 0)
    wide = jnp.dot(both_normed, full_wide, preferred_element_type=f32)
    gate_pre, up_pre = wide[:, :ff_core], wide[:, ff_core:]
    sigmoid = jax.nn.sigmoid(gate_pre)
    silu = gate_pre * sigmoid
    inner = (silu * up_pre).astype(bf16)
    grad_inner = lax.dot_general(both_grad, full_down, LAST, preferred_element_type=f32)
    grad_gate_pre = grad_inner * up_pre * sigmoid * (1.0 + gate_pre * (1.0 - sigmoid))
    grad_up_pre = grad_inner * silu
    grad_wide = jnp.concatenate([grad_gate_pre.astype(bf16), grad_up_pre.astype(bf16)], 1)
    partial = lax.dot_general(grad_wide, full_wide, LAST, preferred_element_type=f32)
    grad_normed_two = partial[:block_length] + moves.swap(partial[block_length:].astype(bf16))
    partial_out = jnp.dot(inner, full_down, preferred_element_type=f32)
    result = hidden + (
        partial_out[:block_length] + moves.swap(partial_out[block_length:].astype(bf16))
    )
    output = moves.restore((valid * result).astype(bf16))
    grad_gain_two = jnp.sum(grad_normed_two * hidden * scale_two, 0)
    grad_hidden = grad_result + norm_back(grad_normed_two, hidden, scale_two, gain_second)
    hidden_low = grad_hidden.astype(bf16)
    first = (((0,), (0,)), ((), ()))
    outer = lambda a, b: lax.dot_general(a, b, first, preferred_element_type=f32).astype(bf16)
    grad_wide_weight = outer(both_normed, grad_wide).reshape(fsdp, shard, -1)
    grad_down_weight = outer(inner, both_grad).reshape(fsdp, ff_half, model)

    grad_attended = lax.dot_general(
        hidden_low, full_out, LAST, preferred_element_type=f32
    ).astype(bf16)
    grad_query_pre, pair_terms = attend_back(
        queries, grad_attended, attended, log_total, all_pairs, cos, sin, info
    )
    pair_sum = lax.psum_scatter(pair_terms, "ctx", scatter_dimension=0, tiled=True)
    grad_pair_pre = unrotate(pair_sum, cos, sin)
    grad_normed = lax.dot_general(
        grad_query_pre, full_in[:, :attention_width], LAST, preferred_element_type=f32
    ) + lax.dot_general(
        grad_pair_pre, full_in[:, attention_width:], LAST, preferred_element_type=f32
    )
    grad_gain_one = jnp.sum(grad_normed * x * scale_one, 0)
    grad_tokens = moves.restore(
        (grad_hidden + norm_back(grad_normed, x, scale_one, gain_first)).astype(bf16)
    )

    wide_part = moves.total(moves.scatter(grad_wide_weight))
    grad_gate, grad_up = merge_columns(core, wide_part, moves.swap(wide_part), fsdp)
    down_low, down_high = moves.both_cores(moves.total(moves.scatter(grad_down_weight)))
    out_parts = moves.reduce_rows(outer(attended, hidden_low))
    query_parts = moves.reduce_rows(outer(normed, grad_query_pre))
    gain_grads = jnp.stack([grad_gain_one.reshape(fsdp, shard), grad_gain_two.reshape(fsdp, shard)], 1)
    gain_grads = jnp.pad(
        gain_grads[:, :, None].astype(bf16),
        ((0, 0), (0, 0), (0, EXTRA - 1), (0, pair_width - shard)),
    )
    pair_parts = moves.reduce_rows(outer(normed, grad_pair_pre), gain_grads)

    below = lambda parts: jnp.concatenate(parts, 0).astype(f32)
    pair_grad = below([part[:in_half] for part in pair_parts])
    pair_grad = pair_grad.reshape(shard, KEY_VALUE_HEADS, PAIR)
    return (
        output.reshape(slots, block_length, model),
        grad_tokens.reshape(slots, block_length, model),
        pair_parts[0][in_half, :shard].astype(f32),
        below(query_parts),
        pair_grad[:, :, :HEAD_SIZE].reshape(shard, -1),
        pair_grad[:, :, HEAD_SIZE:].reshape(shard, -1),
        below(out_parts),
        pair_parts[1][in_half, :shard].astype(f32),
        grad_gate,
        grad_up,
        below([down_low, down_high]),
    )


def solution(mesh):
    rows, whole = P("fsdp", None), P("fsdp", "ctx", None)
    return jax.shard_map(
        local,
        mesh=mesh,
        in_specs=(
            whole, P("fsdp"), whole, P("fsdp"), rows, rows, rows, rows, P("fsdp"), rows, rows, rows,
        ),
        out_specs=(
            whole, whole, P("fsdp"), rows, rows, rows, rows, P("fsdp"), rows, rows, rows,
        ),
        check_vma=False,
    )
```

time: 1600 us -> 917 us (0.57)
  waiting for transfers between devices: 1200 us -> 326 us
  starting transfers between devices: 1.77 us -> 224 us
  Pallas kernels: 0 us -> 127 us
  matrix products: 190 us -> 91.5 us
  blocking collectives: 74.6 us -> 0 us
  other arithmetic: 44.9 us -> 75.8 us
  loops' own time: 21.6 us -> 0 us
    reduce_scatter x8 -> x1, waiting for transfers between devices: 752 us -> 0.01 us  [local(): lax.psum_scatter(pair_terms, 'ctx', scatter_dimension=0, tiled=True)]
    ppermute x0 -> x73, waiting for transfers between devices: none -> 326 us  [the longest x15 181 us: total(): lax.ppermute(value, 'ctx', [(2 * a + c, 2 * b + c) for a, b in pairs for...]
    all_gather x6 -> x1, waiting for transfers between devices: 298 us -> 0.01 us  [local(): all_pairs = lax.all_gather(pairs, 'ctx', axis=0, tiled=True)]
    ppermute x0 -> x73, starting transfers between devices: none -> 224 us  [the longest x36 141 us: across(): return lax.ppermute(value, 'fsdp', [(i, i ^ bit) for i in range(self.fsdp)])]
    psum x1 -> x0, waiting for transfers between devices: 144 us -> none  [local(): lax.psum(shards[1].astype(jnp.bfloat16), 'ctx').astype(jnp.float32)]
    pallas_call x0 -> x10, Pallas kernels: none -> 127 us  [the longest x1 56 us: attend_back(): pl.pallas_call(functools.partial(backward_kernel, keys // half), grid_spe...]
    dot_general x28 -> x13, matrix products: 190 us -> 91.5 us  [the longest x5 27.1 us: local(): lax.dot_general(a, b, first, preferred_element_type=f32).astype(bf16)]
    all_gather x2 -> x0, blocking collectives: 38.9 us -> none  [the longest x1 22.1 us: local(): lax.all_gather(value_matrix, 'fsdp', axis=0, tiled=True)]
  transfers between devices with their start and end apart: 15 -> 75, of which waited for: 13 -> 31; matrix products, arithmetic and copies ran while one was open for 10% -> 15% of each run, Pallas kernels for 0% -> 13%
where the time goes in v1:
time: 917 us; the launch traced here: 909 us
  waiting for transfers between devices  326 us (36%)
  starting transfers between devices  224 us (24%)
  Pallas kernels  127 us (14%)
  matrix products  91.5 us (10%)
  other arithmetic  75.8 us (8%)
  local copies, waits for them, and re-layouts  49.1 us (5%)
  between operations  16.3 us (2%)
    ppermute x15, waiting for transfers between devices, total(): lax.ppermute(value, 'ctx', [(2 * a + c, 2 * b + c) for a, b in pairs for...  181 us
    ppermute x36, starting transfers between devices, across(): return lax.ppermute(value, 'fsdp', [(i, i ^ bit) for i in range(self.fsdp)])  141 us
    ppermute x36, waiting for transfers between devices, across(): return lax.ppermute(value, 'fsdp', [(i, i ^ bit) for i in range(self.fsdp)])  133 us
    pallas_call x1, Pallas kernels, attend_back(): pl.pallas_call(functools.partial(backward_kernel, keys // half), grid_spe...  56 us
    pallas_call x1, Pallas kernels, attend(): pl.pallas_call(functools.partial(forward_kernel, keys // half), grid_spec...  45.9 us
    ppermute x15, starting transfers between devices, total(): lax.ppermute(value, 'ctx', [(2 * a + c, 2 * b + c) for a, b in pairs for...  38.7 us
    unnamed x140, local copies, waits for them, and re-layouts  30.8 us
    dot_general x5, matrix products, local(): lax.dot_general(a, b, first, preferred_element_type=f32).astype(bf16)  27.1 us
  transfers between devices with their start and end apart: 75, of which 31 were waited for; matrix products, arithmetic and copies ran while one was open for 15% of the time, Pallas kernels for 13%

profile of v1, /device:TPU:0, one launch (start us, length us, event | category | flops | bytes accessed | tf_op | source)
XLA Modules:
  0.0 909.4 jit_solution(13749698607629159588)
XLA Ops:
  15.4 13.7 %collective-permute-done.3.refs_2_ = bf16[176,1920]{1,0:T(8,128)(2,1)S(1)} collective-permute-done((bf16[176,1920]{1,0:T(8,128)(2,1)S(1)}, bf16[176,1920]{1,0:T(8,128)(2,1)S(1)}, u32[]{:S(2)}, u32[]{:S(2)}) %collective-permute-start.3) | collective-permute-done | bytes 675872 | tf_op jit(solution)/shard_map/ppermute | solution.py:460
  33.4 6.3 collective-permute-done.4.refs_3_
  50.1 6.5 collective-permute-start
  58.2 10.0 %collective-permute-done.1 = bf16[256,1280]{1,0:T(8,128)(2,1)} collective-permute-done((bf16[256,1280]{1,0:T(8,128)(2,1)}, bf16[256,1280]{1,0:T(8,128)(2,1)}, u32[]{:S(2)}, u32[]{:S(2)}) %collective-permute-start.1) | collective-permute-done | bytes 655392 | tf_op jit(solution)/shard_map/ppermute | solution.py:475
  75.5 6.3 project.1
  85.8 5.4 collective-permute-done.7.refs_1_
  100.4 11.7 %collective-permute-start.11 = (bf16[640,1280]{1,0:T(8,128)(2,1)S(1)}, bf16[640,1280]{1,0:T(8,128)(2,1)}, u32[]{:S(2)}, u32[]{:S(2)}) collective-permute-start(bf16[640,1280]{1,0:T(8,128)(2,1)S(1)} %place.5), channel_id=1, source_target_pairs={{0,4},{4,0},{8,12},{12,8},{16,20},{20,16},{24,28},{28,24},{1,5},{5... | collective-permute-start | bytes 4915208 | tf_op jit(solution)/shard_map/ppermute | solution.py:463
  112.2 3.6 split_columns.1.refs_0_
  124.2 43.7 %collective-permute-done.13.refs_1_ = bf16[320,3584]{1,0:T(8,128)(2,1)} collective-permute-done((bf16[320,3584]{1,0:T(8,128)(2,1)}, bf16[320,3584]{1,0:T(8,128)(2,1)}, u32[]{:S(2)}, u32[]{:S(2)}) %collective-permute-start.13) | collective-permute-done | bytes 2293792 | tf_op jit(solution)/shard_map/ppermute | solution.py:460
  174.3 45.9 %attend.1 = (bf16[512,1280]{1,0:T(8,128)(2,1)S(1)}, f32[5,4,512]{2,1,0:T(4,128)S(1)}) custom-call(s32[3]{0:T(128)S(1)} %pad_add_fusion.1.info_ref, bf16[512,1280]{1,0:T(8,128)(2,1)S(1)} %copy-done.27, bf16[4096,640]{1,0:T(8,128)(2,1)S(1)} %copy-done.25), custom_call_target="tpu_custom_call" | custom-call | flops 21474836480 | bytes 5242880 | tf_op jit(solution)/shard_map/attend/pallas_call | solution.py:204
  220.2 3.7 multiply_reduce_fusion.2
  227.5 6.8 collective-permute-start.24
  239.0 35.0 %collective-permute-start.15 = (bf16[160,3584]{1,0:T(8,128)(2,1)}, bf16[160,3584]{1,0:T(8,128)(2,1)}, u32[]{:S(2)}, u32[]{:S(2)}) collective-permute-start(bf16[160,3584]{1,0:T(8,128)(2,1)} %slice.428), channel_id=1, source_target_pairs={{0,2},{1,3},{2,0},{3,1},{4,6},{5,7},{6,4},{7,5},{8,10},{9,11},{10,... | collective-permute-start | bytes 3440648 | tf_op jit(solution)/shard_map/ppermute | solution.py:460
  275.8 9.1 collective-permute-start.19
  286.5 11.1 %collective-permute-done.15.refs_3_ = bf16[160,3584]{1,0:T(8,128)(2,1)} collective-permute-done((bf16[160,3584]{1,0:T(8,128)(2,1)}, bf16[160,3584]{1,0:T(8,128)(2,1)}, u32[]{:S(2)}, u32[]{:S(2)}) %collective-permute-start.15) | collective-permute-done | bytes 1146912 | tf_op jit(solution)/shard_map/ppermute | solution.py:460
  297.6 5.6 collective-permute-start.26
  305.5 3.6 place.6
  316.0 14.3 %fusion.22 = f32[1024,3584]{1,0:T(8,128)} fusion(bf16[1280,3584]{1,0:T(8,128)(2,1)S(1)} %place.6, bf16[512,1280]{1,0:T(8,128)(2,1)} %collective-permute-done.12, bf16[512,1280]{1,0:T(8,128)(2,1)} %multiply_convert_fusion.3), kind=kOutput, calls=%fused_computation.62 | convolution fusion | flops 9400483840 | bytes 26476544 | tf_op jit(solution)/shard_map/dot_general | solution.py:642
  330.3 14.9 %multiply_convert_fusion.1 = (bf16[1024,1792]{1,0:T(8,128)(2,1)}, bf16[1024,1792]{1,0:T(8,128)(2,1)}, bf16[1024,1792]{1,0:T(8,128)(2,1)}) fusion(f32[1024,3584]{1,0:T(8,128)} %fusion.22, bf16[1792,1280]{1,0:T(8,128)(2,1)} %copy-done.4, bf16[512,1280]{1,0:T(8,128)(2,1)} %collective-permute-done.26, bf16[512,1280]{1,0:T(8,128)(2,1)S(1)} %fusion.18), kind=kOutput, calls=%fused_computation.6 | convolution fusion | flops 4730388480 | bytes 32899072 | tf_op jit(solution)/shard_map/dot_general | solution.py:647
  345.2 13.4 %fusion.1 = f32[1024,1280]{1,0:T(8,128)} fusion(bf16[1280,3584]{1,0:T(8,128)(2,1)S(1)} %place.6, bf16[1024,1792]{1,0:T(8,128)(2,1)} %get-tuple-element.60, bf16[1024,1792]{1,0:T(8,128)(2,1)} %get-tuple-element.59), kind=kOutput, calls=%fused_computation.17 | convolution fusion | flops 9409921024 | bytes 21757952 | tf_op jit(solution)/shard_map/dot_general | solution.py:651
  358.6 14.0 %convolution_convert_fusion = bf16[1280,3584]{1,0:T(8,128)(2,1)S(1)} fusion(bf16[1024,1792]{1,0:T(8,128)(2,1)} %get-tuple-element.60, bf16[1024,1792]{1,0:T(8,128)(2,1)} %get-tuple-element.59, bf16[512,1280]{1,0:T(8,128)(2,1)} %collective-permute-done.12, bf16[512,1280]{1,0:T(8,128)(2,1)} %multiply_convert_fusion.3), kind=kOutput, calls=%fused_computation | convolution fusion | flops 9419751424 | bytes 19136512 | tf_op jit(solution)/shard_map/dot_general | solution.py:662
  374.9 3.7 copy-done.61
  378.6 8.1 convolution_convert_fusion.1
  387.1 3.3 copy-done.62
  390.4 4.9 fusion.57
  397.7 16.8 %collective-permute-done.65 = bf16[224,1280]{1,0:T(8,128)(2,1)S(1)} collective-permute-done((bf16[224,1280]{1,0:T(8,128)(2,1)S(1)}, bf16[224,1280]{1,0:T(8,128)(2,1)S(1)}, u32[]{:S(2)}, u32[]{:S(2)}) %collective-permute-start.65) | collective-permute-done | bytes 573472 | tf_op jit(solution)/shard_map/ppermute | solution.py:460
  419.4 3.6 fusion.26
  424.4 4.1 subtract_add_fusion
  431.3 56.0 %attend_back.1 = (bf16[512,1280]{1,0:T(8,128)(2,1)S(1)}, bf16[4096,640]{1,0:T(8,128)(2,1)}) custom-call(s32[3]{0:T(128)S(1)} %pad_add_fusion.1.info_ref, bf16[512,1280]{1,0:T(8,128)(2,1)S(1)} %copy-done.28, bf16[512,1280]{1,0:T(8,128)(2,1)S(1)} %convolution_convert_fusion.5.do_ref, bf16[512,1280]{1,0:T(8,128)(2,1)S(1)} %copy-done.30, ...), custom_call_target="tpu_custom_call" | custom-call | flops 53687091200 | bytes 20971520 | tf_op jit(solution)/shard_map/attend_back/pallas_call | solution.py:309
  493.7 4.3 fusion.27
  498.0 19.2 %collective-permute-start.69 = (bf16[448,1280]{1,0:T(8,128)(2,1)}, bf16[448,1280]{1,0:T(8,128)(2,1)}, u32[]{:S(2)}, u32[]{:S(2)}) collective-permute-start(bf16[448,1280]{1,0:T(8,128)(2,1)} %fusion.27), channel_id=1, source_target_pairs={{0,8},{4,12},{24,16},{28,20},{1,9},{5,13},{25,17},{29,21},{2,10},{... | collective-permute-start | bytes 3440648 | tf_op jit(solution)/shard_map/ppermute | solution.py:534
  520.2 29.1 %collective-permute-start.60 = (bf16[320,3584]{1,0:T(8,128)(2,1)}, bf16[320,3584]{1,0:T(8,128)(2,1)}, u32[]{:S(2)}, u32[]{:S(2)}) collective-permute-start(bf16[320,3584]{1,0:T(8,128)(2,1)} %pad_maximum_fusion.8), channel_id=1, source_target_pairs={{0,2},{1,3},{2,0},{3,1},{4,6},{5,7},{6,4},{7,5},{8,10},{9,11},{10,... | collective-permute-start | bytes 6881288 | tf_op jit(solution)/shard_map/ppermute | solution.py:460
  551.2 3.1 add.292
  557.8 36.7 %collective-permute-start.40 = (bf16[80,1280]{1,0:T(8,128)(2,1)S(1)}, bf16[80,1280]{1,0:T(8,128)(2,1)S(1)}, u32[]{:S(2)}, u32[]{:S(2)}) collective-permute-start(bf16[80,1280]{1,0:T(8,128)(2,1)S(1)} %get-tuple-element.89), channel_id=1, source_target_pairs={{0,2},{1,3},{2,0},{3,1},{4,6},{5,7},{6,4},{7,5},{8,10},{9,11},{10,... | collective-permute-start | bytes 614408 | tf_op jit(solution)/shard_map/ppermute | solution.py:460
  596.2 8.0 collective-permute-done.40
  607.8 3.3 collective-permute-done.49
  615.0 4.2 fusion.19
  624.9 5.4 collective-permute-done.52
  633.4 46.3 %collective-permute-done.44 = bf16[160,1280]{1,0:T(8,128)(2,1)S(1)} collective-permute-done((bf16[160,1280]{1,0:T(8,128)(2,1)S(1)}, bf16[160,1280]{1,0:T(8,128)(2,1)S(1)}, u32[]{:S(2)}, u32[]{:S(2)}) %collective-permute-start.44) | collective-permute-done | bytes 409632 | tf_op jit(solution)/shard_map/ppermute | solution.py:534
  682.4 4.0 collective-permute-done.53
  687.1 6.5 collective-permute-start.22
  699.4 5.3 fusion.3
  716.6 6.1 collective-permute-done.46
  722.8 25.1 %collective-permute-done.55 = bf16[160,1280]{1,0:T(8,128)(2,1)S(1)} collective-permute-done((bf16[160,1280]{1,0:T(8,128)(2,1)S(1)}, bf16[160,1280]{1,0:T(8,128)(2,1)S(1)}, u32[]{:S(2)}, u32[]{:S(2)}) %collective-permute-start.55) | collective-permute-done | bytes 409632 | tf_op jit(solution)/shard_map/ppermute | solution.py:534
  757.4 5.9 fusion.14
  765.0 62.6 %collective-permute-done.63 = bf16[320,3584]{1,0:T(8,128)(2,1)} collective-permute-done((bf16[320,3584]{1,0:T(8,128)(2,1)}, bf16[320,3584]{1,0:T(8,128)(2,1)}, u32[]{:S(2)}, u32[]{:S(2)}) %collective-permute-start.63) | collective-permute-done | bytes 2293792 | tf_op jit(solution)/shard_map/ppermute | solution.py:534
  856.4 35.6 %collective-permute-done.37 = bf16[176,640]{1,0:T(8,128)(2,1)S(1)} collective-permute-done((bf16[176,640]{1,0:T(8,128)(2,1)S(1)}, bf16[176,640]{1,0:T(8,128)(2,1)S(1)}, u32[]{:S(2)}, u32[]{:S(2)}) %collective-permute-start.37) | collective-permute-done | bytes 225312 | tf_op jit(solution)/shard_map/ppermute | solution.py:534
  893.3 4.0 merge_columns.1
  (394 shorter events, 193.5 us)
Async XLA Ops:
  7.2 163.3 %all-gather.2.cloned.1.call-start = ((), (), s32[]{:S(2)}) async-start(), calls=%async_computation.1 | async-start | bytes 5898240 | tf_op jit(solution)/shard_map/all_gather | solution.py:632
  48.4 23.9 %collective-permute-start.6 = (bf16[4,160,1920]{2,1,0:T(8,128)(2,1)}, bf16[4,160,1920]{2,1,0:T(8,128)(2,1)}, u32[]{:S(2)}, u32[]{:S(2)}) collective-permute-start(bf16[4,160,1920]{2,1,0:T(8,128)(2,1)} %slice.424), channel_id=1, source_target_pairs={{0,4},{4,0},{8,12},{12,8},{16,20},{20,16},{24,28},{28,24},{1,5},{5... | collective-permute-start | bytes 7372808 | tf_op jit(solution)/shard_map/ppermute | solution.py:463
  82.9 672.0 %reduce-scatter.2.cloned.1.call-start = ((), (), s32[]{:S(2)}) async-start(), calls=%async_computation.2 | async-start | bytes 5898240 | tf_op jit(solution)/shard_map/reduce_scatter | solution.py:672
  100.4 19.8 %collective-permute-start.11 = (bf16[640,1280]{1,0:T(8,128)(2,1)S(1)}, bf16[640,1280]{1,0:T(8,128)(2,1)}, u32[]{:S(2)}, u32[]{:S(2)}) collective-permute-start(bf16[640,1280]{1,0:T(8,128)(2,1)S(1)} %place.5), channel_id=1, source_target_pairs={{0,4},{4,0},{8,12},{12,8},{16,20},{20,16},{24,28},{28,24},{1,5},{5... | collective-permute-start | bytes 4915208 | tf_op jit(solution)/shard_map/ppermute | solution.py:463
  115.7 52.1 %collective-permute-start.13 = (bf16[320,3584]{1,0:T(8,128)(2,1)}, bf16[320,3584]{1,0:T(8,128)(2,1)}, u32[]{:S(2)}, u32[]{:S(2)}) collective-permute-start(bf16[320,3584]{1,0:T(8,128)(2,1)} %split_columns.1.refs_0_), channel_id=1, source_target_pairs={{0,1},{1,0},{2,3},{3,2},{4,5},{5,4},{6,7},{7,6},{8,9},{9,8},{10,11... | collective-permute-start | bytes 6881288 | tf_op jit(solution)/shard_map/ppermute | solution.py:460
  116.7 51.9 %collective-permute-start.14 = (bf16[320,3584]{1,0:T(8,128)(2,1)}, bf16[320,3584]{1,0:T(8,128)(2,1)}, u32[]{:S(2)}, u32[]{:S(2)}) collective-permute-start(bf16[320,3584]{1,0:T(8,128)(2,1)} %split_columns.1.refs_0_), channel_id=1, source_target_pairs={{0,2},{1,3},{2,0},{3,1},{4,6},{5,7},{6,4},{7,5},{8,10},{9,11},{10,... | collective-permute-start | bytes 6881288 | tf_op jit(solution)/shard_map/ppermute | solution.py:460
  168.6 70.4 %collective-permute-start.17 = (bf16[448,1280]{1,0:T(8,128)(2,1)S(1)}, bf16[448,1280]{1,0:T(8,128)(2,1)S(1)}, u32[]{:S(2)}, u32[]{:S(2)}) collective-permute-start(bf16[448,1280]{1,0:T(8,128)(2,1)S(1)} %slice_select_fusion.refs_0_), channel_id=1, source_target_pairs={{0,1},{1,0},{2,3},{3,2},{4,5},{5,4},{6,7},{7,6},{8,9},{9,8},{10,11... | collective-permute-start | bytes 3440648 | tf_op jit(solution)/shard_map/ppermute | solution.py:460
  169.6 104.4 %collective-permute-start.18 = (bf16[448,1280]{1,0:T(8,128)(2,1)S(1)}, bf16[448,1280]{1,0:T(8,128)(2,1)S(1)}, u32[]{:S(2)}, u32[]{:S(2)}) collective-permute-start(bf16[448,1280]{1,0:T(8,128)(2,1)S(1)} %slice_select_fusion.refs_0_), channel_id=1, source_target_pairs={{0,2},{1,3},{2,0},{3,1},{4,6},{5,7},{6,4},{7,5},{8,10},{9,11},{10,... | collective-permute-start | bytes 3440648 | tf_op jit(solution)/shard_map/ppermute | solution.py:460
  225.3 90.6 %collective-permute-start.12 = (bf16[512,1280]{1,0:T(8,128)(2,1)}, bf16[512,1280]{1,0:T(8,128)(2,1)}, u32[]{:S(2)}, u32[]{:S(2)}) collective-permute-start(bf16[512,1280]{1,0:T(8,128)(2,1)} %multiply_convert_fusion.3), channel_id=1, source_target_pairs={{0,4},{4,0},{8,12},{12,8},{16,20},{20,16},{24,28},{28,24},{1,5},{5... | collective-permute-start | bytes 3932168 | tf_op jit(solution)/shard_map/ppermute | solution.py:463
  227.5 48.3 %collective-permute-start.25 = (bf16[256,1280]{1,0:T(8,128)(2,1)}, bf16[256,1280]{1,0:T(8,128)(2,1)}, u32[]{:S(2)}, u32[]{:S(2)}) collective-permute-start(bf16[256,1280]{1,0:T(8,128)(2,1)} %get-tuple-element.99), channel_id=1, source_target_pairs={{0,4},{4,12},{8,20},{12,28},{16,24},{20,16},{24,8},{28,0},{1,5},{5... | collective-permute-start | bytes 1966088 | tf_op jit(solution)/shard_map/ppermute | solution.py:475
  227.5 57.4 %collective-permute-start.24 = (bf16[256,1280]{1,0:T(8,128)(2,1)}, bf16[256,1280]{1,0:T(8,128)(2,1)}, u32[]{:S(2)}, u32[]{:S(2)}) collective-permute-start(bf16[256,1280]{1,0:T(8,128)(2,1)} %get-tuple-element.98), channel_id=1, source_target_pairs={{0,0},{4,8},{8,16},{12,24},{16,28},{20,20},{24,12},{28,4},{1,1},{5... | collective-permute-start | bytes 1966088 | tf_op jit(solution)/shard_map/ppermute | solution.py:475
  239.0 58.7 %collective-permute-start.15 = (bf16[160,3584]{1,0:T(8,128)(2,1)}, bf16[160,3584]{1,0:T(8,128)(2,1)}, u32[]{:S(2)}, u32[]{:S(2)}) collective-permute-start(bf16[160,3584]{1,0:T(8,128)(2,1)} %slice.428), channel_id=1, source_target_pairs={{0,2},{1,3},{2,0},{3,1},{4,6},{5,7},{6,4},{7,5},{8,10},{9,11},{10,... | collective-permute-start | bytes 3440648 | tf_op jit(solution)/shard_map/ppermute | solution.py:460
  274.0 29.2 %collective-permute-start.16 = (bf16[160,3584]{1,0:T(8,128)(2,1)}, bf16[160,3584]{1,0:T(8,128)(2,1)S(1)}, u32[]{:S(2)}, u32[]{:S(2)}) collective-permute-start(bf16[160,3584]{1,0:T(8,128)(2,1)} %slice.429), channel_id=1, source_target_pairs={{0,1},{1,0},{2,3},{3,2},{4,5},{5,4},{6,7},{7,6},{8,9},{9,8},{10,11... | collective-permute-start | bytes 3440648 | tf_op jit(solution)/shard_map/ppermute | solution.py:460
  275.8 34.0 %collective-permute-start.19 = (bf16[224,1280]{1,0:T(8,128)(2,1)S(1)}, bf16[224,1280]{1,0:T(8,128)(2,1)S(1)}, u32[]{:S(2)}, u32[]{:S(2)}) collective-permute-start(bf16[224,1280]{1,0:T(8,128)(2,1)S(1)} %slice.432), channel_id=1, source_target_pairs={{0,2},{1,3},{2,0},{3,1},{4,6},{5,7},{6,4},{7,5},{8,10},{9,11},{10,... | collective-permute-start | bytes 1720328 | tf_op jit(solution)/shard_map/ppermute | solution.py:460
  284.9 27.5 %collective-permute-start.20 = (bf16[224,1280]{1,0:T(8,128)(2,1)S(1)}, bf16[224,1280]{1,0:T(8,128)(2,1)S(1)}, u32[]{:S(2)}, u32[]{:S(2)}) collective-permute-start(bf16[224,1280]{1,0:T(8,128)(2,1)S(1)} %slice.433), channel_id=1, source_target_pairs={{0,1},{1,0},{2,3},{3,2},{4,5},{5,4},{6,7},{7,6},{8,9},{9,8},{10,11... | collective-permute-start | bytes 1720328 | tf_op jit(solution)/shard_map/ppermute | solution.py:460
  297.6 32.7 %collective-permute-start.26 = (bf16[512,1280]{1,0:T(8,128)(2,1)S(1)}, bf16[512,1280]{1,0:T(8,128)(2,1)}, u32[]{:S(2)}, u32[]{:S(2)}) collective-permute-start(bf16[512,1280]{1,0:T(8,128)(2,1)S(1)} %fusion.18), channel_id=1, source_target_pairs={{0,4},{4,0},{8,12},{12,8},{16,20},{20,16},{24,28},{28,24},{1,5},{5... | collective-permute-start | bytes 3932168 | tf_op jit(solution)/shard_map/ppermute | solution.py:463
  374.9 44.5 %collective-permute-start.57 = (bf16[160,3584]{1,0:T(8,128)(2,1)}, bf16[160,3584]{1,0:T(8,128)(2,1)}, u32[]{:S(2)}, u32[]{:S(2)}) collective-permute-start(bf16[160,3584]{1,0:T(8,128)(2,1)} %get-tuple-element.63), channel_id=1, source_target_pairs={{0,2},{1,3},{2,0},{3,1},{4,6},{5,7},{6,4},{7,5},{8,10},{9,11},{10,... | collective-permute-start | bytes 3440648 | tf_op jit(solution)/shard_map/ppermute | solution.py:460
  374.9 44.5 %collective-permute-start.59 = (bf16[160,3584]{1,0:T(8,128)(2,1)}, bf16[160,3584]{1,0:T(8,128)(2,1)}, u32[]{:S(2)}, u32[]{:S(2)}) collective-permute-start(bf16[160,3584]{1,0:T(8,128)(2,1)} %get-tuple-element.65), channel_id=1, source_target_pairs={{0,1},{1,0},{2,3},{3,2},{4,5},{5,4},{6,7},{7,6},{8,9},{9,8},{10,11... | collective-permute-start | bytes 3440648 | tf_op jit(solution)/shard_map/ppermute | solution.py:460
  386.9 27.6 %collective-permute-start.65 = (bf16[224,1280]{1,0:T(8,128)(2,1)S(1)}, bf16[224,1280]{1,0:T(8,128)(2,1)S(1)}, u32[]{:S(2)}, u32[]{:S(2)}) collective-permute-start(bf16[224,1280]{1,0:T(8,128)(2,1)S(1)} %get-tuple-element.71), channel_id=1, source_target_pairs={{0,2},{1,3},{2,0},{3,1},{4,6},{5,7},{6,4},{7,5},{8,10},{9,11},{10,... | collective-permute-start | bytes 1720328 | tf_op jit(solution)/shard_map/ppermute | solution.py:460
  387.0 28.4 %collective-permute-start.67 = (bf16[224,1280]{1,0:T(8,128)(2,1)S(1)}, bf16[224,1280]{1,0:T(8,128)(2,1)S(1)}, u32[]{:S(2)}, u32[]{:S(2)}) collective-permute-start(bf16[224,1280]{1,0:T(8,128)(2,1)S(1)} %get-tuple-element.73), channel_id=1, source_target_pairs={{0,1},{1,0},{2,3},{3,2},{4,5},{5,4},{6,7},{7,6},{8,9},{9,8},{10,11... | collective-permute-start | bytes 1720328 | tf_op jit(solution)/shard_map/ppermute | solution.py:460
  395.5 27.6 %collective-permute-start.27 = (bf16[512,1280]{1,0:T(8,128)(2,1)S(1)}, bf16[512,1280]{1,0:T(8,128)(2,1)S(1)}, u32[]{:S(2)}, u32[]{:S(2)}) collective-permute-start(bf16[512,1280]{1,0:T(8,128)(2,1)S(1)} %slice.503), channel_id=1, source_target_pairs={{0,4},{4,0},{8,12},{12,8},{16,20},{20,16},{24,28},{28,24},{1,5},{5... | collective-permute-start | bytes 3932168 | tf_op jit(solution)/shard_map/ppermute | solution.py:463
  416.8 76.8 %collective-permute-start.68 = (bf16[448,1280]{1,0:T(8,128)(2,1)}, bf16[448,1280]{1,0:T(8,128)(2,1)}, u32[]{:S(2)}, u32[]{:S(2)}) collective-permute-start(bf16[448,1280]{1,0:T(8,128)(2,1)} %pad_maximum_fusion.16), channel_id=1, source_target_pairs={{0,2},{1,3},{2,0},{3,1},{4,6},{5,7},{6,4},{7,5},{8,10},{9,11},{10,... | collective-permute-start | bytes 3440648 | tf_op jit(solution)/shard_map/ppermute | solution.py:460
  419.4 74.3 %collective-permute-start.66 = (bf16[448,1280]{1,0:T(8,128)(2,1)}, bf16[448,1280]{1,0:T(8,128)(2,1)}, u32[]{:S(2)}, u32[]{:S(2)}) collective-permute-start(bf16[448,1280]{1,0:T(8,128)(2,1)} %pad_maximum_fusion.15), channel_id=1, source_target_pairs={{0,1},{1,0},{2,3},{3,2},{4,5},{5,4},{6,7},{7,6},{8,9},{9,8},{10,11... | collective-permute-start | bytes 3440648 | tf_op jit(solution)/shard_map/ppermute | solution.py:460
  491.4 64.7 %collective-permute-start.39 = (bf16[4,160,1280]{2,1,0:T(8,128)(2,1)}, bf16[4,160,1280]{2,1,0:T(8,128)(2,1)}, u32[]{:S(2)}, u32[]{:S(2)}) collective-permute-start(bf16[4,160,1280]{2,1,0:T(8,128)(2,1)} %dynamic-slice_bitcast_fusion.1), channel_id=1, source_target_pairs={{0,4},{4,0},{8,12},{12,8},{16,20},{20,16},{24,28},{28,24},{1,5},{5... | collective-permute-start | bytes 4915208 | tf_op jit(solution)/shard_map/ppermute | solution.py:463
  498.0 53.2 %collective-permute-start.69 = (bf16[448,1280]{1,0:T(8,128)(2,1)}, bf16[448,1280]{1,0:T(8,128)(2,1)}, u32[]{:S(2)}, u32[]{:S(2)}) collective-permute-start(bf16[448,1280]{1,0:T(8,128)(2,1)} %fusion.27), channel_id=1, source_target_pairs={{0,8},{4,12},{24,16},{28,20},{1,9},{5,13},{25,17},{29,21},{2,10},{... | collective-permute-start | bytes 3440648 | tf_op jit(solution)/shard_map/ppermute | solution.py:534
  518.5 76.0 %collective-permute-start.48 = (bf16[4,160,1280]{2,1,0:T(8,128)(2,1)}, bf16[4,160,1280]{2,1,0:T(8,128)(2,1)}, u32[]{:S(2)}, u32[]{:S(2)}) collective-permute-start(bf16[4,160,1280]{2,1,0:T(8,128)(2,1)} %dynamic-slice_bitcast_fusion), channel_id=1, source_target_pairs={{0,4},{4,0},{8,12},{12,8},{16,20},{20,16},{24,28},{28,24},{1,5},{5... | collective-permute-start | bytes 4915208 | tf_op jit(solution)/shard_map/ppermute | solution.py:463
  520.2 94.0 %collective-permute-start.60 = (bf16[320,3584]{1,0:T(8,128)(2,1)}, bf16[320,3584]{1,0:T(8,128)(2,1)}, u32[]{:S(2)}, u32[]{:S(2)}) collective-permute-start(bf16[320,3584]{1,0:T(8,128)(2,1)} %pad_maximum_fusion.8), channel_id=1, source_target_pairs={{0,2},{1,3},{2,0},{3,1},{4,6},{5,7},{6,4},{7,5},{8,10},{9,11},{10,... | collective-permute-start | bytes 6881288 | tf_op jit(solution)/shard_map/ppermute | solution.py:460
  551.1 63.9 %collective-permute-start.58 = (bf16[320,3584]{1,0:T(8,128)(2,1)S(1)}, bf16[320,3584]{1,0:T(8,128)(2,1)S(1)}, u32[]{:S(2)}, u32[]{:S(2)}) collective-permute-start(bf16[320,3584]{1,0:T(8,128)(2,1)S(1)} %pad_maximum_fusion.7), channel_id=1, source_target_pairs={{0,1},{1,0},{2,3},{3,2},{4,5},{5,4},{6,7},{7,6},{8,9},{9,8},{10,11... | collective-permute-start | bytes 6881288 | tf_op jit(solution)/shard_map/ppermute | solution.py:460
  554.3 143.8 %collective-permute-start.70 = (bf16[448,1280]{1,0:T(8,128)(2,1)}, bf16[448,1280]{1,0:T(8,128)(2,1)}, u32[]{:S(2)}, u32[]{:S(2)}) collective-permute-start(bf16[448,1280]{1,0:T(8,128)(2,1)} %add.292), channel_id=1, source_target_pairs={{8,16},{12,20},{16,8},{20,12},{9,17},{13,21},{17,9},{21,13},{10,18... | collective-permute-start | bytes 3440648 | tf_op jit(solution)/shard_map/ppermute | solution.py:534
  557.8 46.4 %collective-permute-start.40 = (bf16[80,1280]{1,0:T(8,128)(2,1)S(1)}, bf16[80,1280]{1,0:T(8,128)(2,1)S(1)}, u32[]{:S(2)}, u32[]{:S(2)}) collective-permute-start(bf16[80,1280]{1,0:T(8,128)(2,1)S(1)} %get-tuple-element.89), channel_id=1, source_target_pairs={{0,2},{1,3},{2,0},{3,1},{4,6},{5,7},{6,4},{7,5},{8,10},{9,11},{10,... | collective-permute-start | bytes 614408 | tf_op jit(solution)/shard_map/ppermute | solution.py:460
  619.2 87.5 %collective-permute-start.61 = (bf16[320,3584]{1,0:T(8,128)(2,1)}, bf16[320,3584]{1,0:T(8,128)(2,1)}, u32[]{:S(2)}, u32[]{:S(2)}) collective-permute-start(bf16[320,3584]{1,0:T(8,128)(2,1)} %fusion.19), channel_id=1, source_target_pairs={{0,8},{4,12},{24,16},{28,20},{1,9},{5,13},{25,17},{29,21},{2,10},{... | collective-permute-start | bytes 6881288 | tf_op jit(solution)/shard_map/ppermute | solution.py:534
  623.6 56.2 %collective-permute-start.44 = (bf16[160,1280]{1,0:T(8,128)(2,1)S(1)}, bf16[160,1280]{1,0:T(8,128)(2,1)S(1)}, u32[]{:S(2)}, u32[]{:S(2)}) collective-permute-start(bf16[160,1280]{1,0:T(8,128)(2,1)S(1)} %fusion.36), channel_id=1, source_target_pairs={{0,8},{4,12},{24,16},{28,20},{1,9},{5,13},{25,17},{29,21},{2,10},{... | collective-permute-start | bytes 1228808 | tf_op jit(solution)/shard_map/ppermute | solution.py:534
  632.1 54.3 %collective-permute-start.53 = (bf16[160,1280]{1,0:T(8,128)(2,1)S(1)}, bf16[160,1280]{1,0:T(8,128)(2,1)S(1)}, u32[]{:S(2)}, u32[]{:S(2)}) collective-permute-start(bf16[160,1280]{1,0:T(8,128)(2,1)S(1)} %fusion.35), channel_id=1, source_target_pairs={{0,8},{4,12},{24,16},{28,20},{1,9},{5,13},{25,17},{29,21},{2,10},{... | collective-permute-start | bytes 1228808 | tf_op jit(solution)/shard_map/ppermute | solution.py:534
  682.4 28.4 %collective-permute-start.23 = (bf16[256,1280]{1,0:T(8,128)(2,1)}, bf16[256,1280]{1,0:T(8,128)(2,1)}, u32[]{:S(2)}, u32[]{:S(2)}) collective-permute-start(bf16[256,1280]{1,0:T(8,128)(2,1)} %get-tuple-element.101), channel_id=1, source_target_pairs={{4,0},{12,4},{20,8},{28,12},{24,16},{16,20},{8,24},{0,28},{5,1},{1... | collective-permute-start | bytes 1966088 | tf_op jit(solution)/shard_map/ppermute | solution.py:489
  687.1 24.5 %collective-permute-start.22 = (bf16[256,1280]{1,0:T(8,128)(2,1)}, bf16[256,1280]{1,0:T(8,128)(2,1)}, u32[]{:S(2)}, u32[]{:S(2)}) collective-permute-start(bf16[256,1280]{1,0:T(8,128)(2,1)} %get-tuple-element.100), channel_id=1, source_target_pairs={{0,0},{8,4},{16,8},{24,12},{28,16},{20,20},{12,24},{4,28},{1,1},{9... | collective-permute-start | bytes 1966088 | tf_op jit(solution)/shard_map/ppermute | solution.py:489
  695.5 18.6 %collective-permute-start.54 = (bf16[160,1280]{1,0:T(8,128)(2,1)}, bf16[160,1280]{1,0:T(8,128)(2,1)}, u32[]{:S(2)}, u32[]{:S(2)}) collective-permute-start(bf16[160,1280]{1,0:T(8,128)(2,1)} %add.280), channel_id=1, source_target_pairs={{8,16},{12,20},{16,8},{20,12},{9,17},{13,21},{17,9},{21,13},{10,18... | collective-permute-start | bytes 1228808 | tf_op jit(solution)/shard_map/ppermute | solution.py:534
  698.1 24.6 %collective-permute-start.46 = (bf16[160,1280]{1,0:T(8,128)(2,1)S(1)}, bf16[160,1280]{1,0:T(8,128)(2,1)S(1)}, u32[]{:S(2)}, u32[]{:S(2)}) collective-permute-start(bf16[160,1280]{1,0:T(8,128)(2,1)S(1)} %add.274), channel_id=1, source_target_pairs={{8,0},{12,4},{16,24},{20,28},{9,1},{13,5},{17,25},{21,29},{10,2},{... | collective-permute-start | bytes 1228808 | tf_op jit(solution)/shard_map/ppermute | solution.py:534
  706.6 41.4 %collective-permute-start.71 = (bf16[448,1280]{1,0:T(8,128)(2,1)S(1)}, bf16[448,1280]{1,0:T(8,128)(2,1)S(1)}, u32[]{:S(2)}, u32[]{:S(2)}) collective-permute-start(bf16[448,1280]{1,0:T(8,128)(2,1)S(1)} %add.293), channel_id=1, source_target_pairs={{8,0},{12,4},{16,24},{20,28},{9,1},{13,5},{17,25},{21,29},{10,2},{... | collective-permute-start | bytes 3440648 | tf_op jit(solution)/shard_map/ppermute | solution.py:534
  710.8 38.0 %collective-permute-start.62 = (bf16[320,3584]{1,0:T(8,128)(2,1)S(1)}, bf16[320,3584]{1,0:T(8,128)(2,1)S(1)}, u32[]{:S(2)}, u32[]{:S(2)}) collective-permute-start(bf16[320,3584]{1,0:T(8,128)(2,1)S(1)} %add.286), channel_id=1, source_target_pairs={{8,16},{12,20},{16,8},{20,12},{9,17},{13,21},{17,9},{21,13},{10,18... | collective-permute-start | bytes 6881288 | tf_op jit(solution)/shard_map/ppermute | solution.py:534
  715.3 32.6 %collective-permute-start.55 = (bf16[160,1280]{1,0:T(8,128)(2,1)S(1)}, bf16[160,1280]{1,0:T(8,128)(2,1)S(1)}, u32[]{:S(2)}, u32[]{:S(2)}) collective-permute-start(bf16[160,1280]{1,0:T(8,128)(2,1)S(1)} %add.281), channel_id=1, source_target_pairs={{8,0},{12,4},{16,24},{20,28},{9,1},{13,5},{17,25},{21,29},{10,2},{... | collective-permute-start | bytes 1228808 | tf_op jit(solution)/shard_map/ppermute | solution.py:534
  722.7 26.0 %collective-permute-start.47 = (bf16[160,1280]{1,0:T(8,128)(2,1)S(1)}, bf16[160,1280]{1,0:T(8,128)(2,1)S(1)}, u32[]{:S(2)}, u32[]{:S(2)}) collective-permute-start(bf16[160,1280]{1,0:T(8,128)(2,1)S(1)} %broadcast_select_fusion.7), channel_id=1, source_target_pairs={{0,4},{4,0},{8,12},{12,8},{16,20},{20,16},{24,28},{28,24},{1,5},{5... | collective-permute-start | bytes 1228808 | tf_op jit(solution)/shard_map/ppermute | solution.py:463
  748.2 102.9 %collective-permute-start.72 = (bf16[448,1280]{1,0:T(8,128)(2,1)S(1)}, bf16[448,1280]{1,0:T(8,128)(2,1)}, u32[]{:S(2)}, u32[]{:S(2)}) collective-permute-start(bf16[448,1280]{1,0:T(8,128)(2,1)S(1)} %broadcast_select_fusion.3), channel_id=1, source_target_pairs={{0,4},{4,0},{8,12},{12,8},{16,20},{20,16},{24,28},{28,24},{1,5},{5... | collective-permute-start | bytes 3440648 | tf_op jit(solution)/shard_map/ppermute | solution.py:463
  750.7 76.9 %collective-permute-start.63 = (bf16[320,3584]{1,0:T(8,128)(2,1)}, bf16[320,3584]{1,0:T(8,128)(2,1)}, u32[]{:S(2)}, u32[]{:S(2)}) collective-permute-start(bf16[320,3584]{1,0:T(8,128)(2,1)} %add.287), channel_id=1, source_target_pairs={{8,0},{12,4},{16,24},{20,28},{9,1},{13,5},{17,25},{21,29},{10,2},{... | collective-permute-start | bytes 6881288 | tf_op jit(solution)/shard_map/ppermute | solution.py:534
  765.0 64.9 %collective-permute-start.30 = (bf16[4,176,640]{2,1,0:T(8,128)(2,1)S(1)}, bf16[4,176,640]{2,1,0:T(8,128)(2,1)S(1)}, u32[]{:S(2)}, u32[]{:S(2)}) collective-permute-start(bf16[4,176,640]{2,1,0:T(8,128)(2,1)S(1)} %dynamic-slice_bitcast_fusion.8), channel_id=1, source_target_pairs={{0,4},{4,0},{8,12},{12,8},{16,20},{20,16},{24,28},{28,24},{1,5},{5... | collective-permute-start | bytes 2703368 | tf_op jit(solution)/shard_map/ppermute | solution.py:463
  829.7 63.5 %collective-permute-start.64 = (bf16[320,3584]{1,0:T(8,128)(2,1)S(1)}, bf16[320,3584]{1,0:T(8,128)(2,1)S(1)}, u32[]{:S(2)}, u32[]{:S(2)}) collective-permute-start(bf16[320,3584]{1,0:T(8,128)(2,1)S(1)} %broadcast_select_fusion.own_ref), channel_id=1, source_target_pairs={{0,4},{4,0},{8,12},{12,8},{16,20},{20,16},{24,28},{28,24},{1,5},{5... | collective-permute-start | bytes 6881288 | tf_op jit(solution)/shard_map/ppermute | solution.py:463
  846.9 45.2 %collective-permute-start.29 = (bf16[256,1280]{1,0:T(8,128)(2,1)S(1)}, bf16[256,1280]{1,0:T(8,128)(2,1)S(1)}, u32[]{:S(2)}, u32[]{:S(2)}) collective-permute-start(bf16[256,1280]{1,0:T(8,128)(2,1)S(1)} %get-tuple-element.97), channel_id=1, source_target_pairs={{4,0},{12,4},{20,8},{28,12},{24,16},{16,20},{8,24},{0,28},{5,1},{1... | collective-permute-start | bytes 1966088 | tf_op jit(solution)/shard_map/ppermute | solution.py:489
  848.3 43.8 %collective-permute-start.28 = (bf16[256,1280]{1,0:T(8,128)(2,1)S(1)}, bf16[256,1280]{1,0:T(8,128)(2,1)S(1)}, u32[]{:S(2)}, u32[]{:S(2)}) collective-permute-start(bf16[256,1280]{1,0:T(8,128)(2,1)S(1)} %get-tuple-element.96), channel_id=1, source_target_pairs={{0,0},{8,4},{16,8},{24,12},{28,16},{20,20},{12,24},{4,28},{1,1},{9... | collective-permute-start | bytes 1966088 | tf_op jit(solution)/shard_map/ppermute | solution.py:489
  852.6 39.4 %collective-permute-start.37 = (bf16[176,640]{1,0:T(8,128)(2,1)S(1)}, bf16[176,640]{1,0:T(8,128)(2,1)S(1)}, u32[]{:S(2)}, u32[]{:S(2)}) collective-permute-start(bf16[176,640]{1,0:T(8,128)(2,1)S(1)} %add.267), channel_id=1, source_target_pairs={{8,0},{12,4},{16,24},{20,28},{9,1},{13,5},{17,25},{21,29},{10,2},{... | collective-permute-start | bytes 675848 | tf_op jit(solution)/shard_map/ppermute | solution.py:534
  (94 other events, 1129.8 us)
Sparse Core Ops, SparseCore 0:
  83.0 70.1 all-gather.1
  549.5 59.8 reduce-scatter.1

commit v2 on v1

v2 whole, which is shorter than its diff:
```python
import functools
import math

import jax
import jax.numpy as jnp
from jax import lax
from jax.experimental import pallas as pl
from jax.experimental.pallas import tpu as pltpu
from jax.sharding import PartitionSpec as P

QUERY_HEADS = 20
KEY_VALUE_HEADS = 5
GROUP = QUERY_HEADS // KEY_VALUE_HEADS
HEAD_SIZE = 64
PAIR = 2 * HEAD_SIZE
HALF_HEAD = HEAD_SIZE // 2
epsilon = 1e-05
LOG2E = math.log2(math.e)
SCORE_SCALE = 1.0 / math.sqrt(HEAD_SIZE)
NEGATIVE = -1e30
EXTRA = 16
f32 = jnp.float32
bf16 = jnp.bfloat16


def rms_scale(values):
    return lax.rsqrt(jnp.mean(values * values, -1, keepdims=True) + epsilon)


def norm_back(grad_normed, values, scale_rows, gain):
    weighted = grad_normed * gain
    cubed = scale_rows * scale_rows * scale_rows
    return scale_rows * weighted - values * cubed * jnp.mean(weighted * values, -1, keepdims=True)


def swap_halves(x):
    lane = lax.broadcasted_iota(jnp.int32, x.shape, 1)
    ahead = pltpu.roll(x, PAIR - HALF_HEAD, 1)
    behind = pltpu.roll(x, HALF_HEAD, 1)
    return jnp.where(lane % HEAD_SIZE < HALF_HEAD, ahead, behind)


def project_kernel(is_pair, x_ref, w_ref, cos_ref, sin_ref, out_ref):
    product = jnp.dot(x_ref[...], w_ref[...], preferred_element_type=f32)
    cos, sin = cos_ref[...], sin_ref[...]
    if is_pair:
        lane = lax.broadcasted_iota(jnp.int32, cos.shape, 1)
        cos = jnp.where(lane >= HEAD_SIZE, 1.0, cos)
        sin = jnp.where(lane >= HEAD_SIZE, 0.0, sin)
    for at in range(0, w_ref.shape[1], PAIR):
        part = product[:, at : at + PAIR]
        out_ref[:, at : at + PAIR] = (part * cos + swap_halves(part) * sin).astype(bf16)


def project(is_pair, normed, weights, cos, sin, deps=()):
    rows, model = normed.shape
    width = weights.shape[1]
    block = KEY_VALUE_HEADS * PAIR
    return pl.pallas_call(
        ignoring(functools.partial(project_kernel, is_pair), 0, len(deps)),
        grid=(width // block,),
        in_specs=anywhere(deps)
        + [
            pl.BlockSpec((rows, model), lambda i: (0, 0)),
            pl.BlockSpec((model, block), lambda i: (0, i)),
            pl.BlockSpec((rows, PAIR), lambda i: (0, 0)),
            pl.BlockSpec((rows, PAIR), lambda i: (0, 0)),
        ],
        out_specs=pl.BlockSpec((rows, block), lambda i: (0, i)),
        out_shape=jax.ShapeDtypeStruct((rows, width), bf16),
        compiler_params=pltpu.CompilerParams(vmem_limit_bytes=16 << 20),
        cost_estimate=takes(3),
        name="project",
    )(*deps, normed, weights, cos, sin)


def unrotate_kernel(x_ref, cos_ref, sin_ref, out_ref):
    lane = lax.broadcasted_iota(jnp.int32, cos_ref.shape, 1)
    cos = jnp.where(lane >= HEAD_SIZE, 1.0, cos_ref[...])
    sin = jnp.where(lane >= HEAD_SIZE, 0.0, sin_ref[...])
    for at in range(0, x_ref.shape[1], PAIR):
        part = x_ref[:, at : at + PAIR].astype(f32)
        out_ref[:, at : at + PAIR] = (part * cos - swap_halves(part) * sin).astype(bf16)


def unrotate(x, cos, sin, deps=()):
    whole = lambda v: pl.BlockSpec(v.shape, lambda i: (0, 0))
    return pl.pallas_call(
        ignoring(unrotate_kernel, 0, len(deps)),
        grid=(1,),
        in_specs=anywhere(deps) + [whole(x), whole(cos), whole(sin)],
        out_specs=whole(x),
        out_shape=jax.ShapeDtypeStruct(x.shape, bf16),
        cost_estimate=takes(3),
        name="unrotate",
    )(*deps, x, cos, sin)


def copy_kernel(core_ref, x_ref, out_ref):
    out_ref[...] = x_ref[...]


def core_rows(core, x, deps=()):
    rows, width = x.shape
    return pl.pallas_call(
        ignoring(copy_kernel, 1, len(deps)),
        grid_spec=pltpu.PrefetchScalarGridSpec(
            num_scalar_prefetch=1,
            grid=(1,),
            in_specs=anywhere(deps) + [pl.BlockSpec((rows // 2, width), lambda i, core: (core[0], 0))],
            out_specs=pl.BlockSpec((rows // 2, width), lambda i, core: (0, 0)),
        ),
        out_shape=jax.ShapeDtypeStruct((rows // 2, width), x.dtype),
        cost_estimate=takes(1),
        name="core_rows",
    )(core, *deps, x)


def block_row(block, blocks, half):
    device = jnp.minimum(block, blocks - 1 - block)
    return pl.multiple_of(device * (2 * half) + (block % 2) * half, half)


def two_blocks(ref, step, blocks, half):
    first = ref[pl.ds(block_row(2 * step, blocks, half), half), :]
    second = ref[pl.ds(block_row(2 * step + 1, blocks, half), half), :]
    return jnp.concatenate([first, second], 0)


def one_head(ref, rows, head, low):
    part = ref[rows, (head // 2) * PAIR : (head // 2 + 1) * PAIR].astype(f32)
    lane = lax.broadcasted_iota(jnp.int32, part.shape, 1)
    if (head % 2 == 0) != low:
        part = pltpu.roll(part, HEAD_SIZE, 1)
    keep = lane < HEAD_SIZE if low else lane >= HEAD_SIZE
    return jnp.where(keep, part, 0.0).astype(bf16)


def allowed_keys(step, block, length, half):
    shape = (2 * half, half)
    key_pos = lax.broadcasted_iota(jnp.int32, shape, 0) + step * (2 * half)
    query_pos = lax.broadcasted_iota(jnp.int32, shape, 1) + block * half
    return key_pos <= jnp.minimum(query_pos, length - 1)


def key_steps(block, length, half):
    keys = jnp.minimum((block + 1) * half, length)
    return (keys + 2 * half - 1) // (2 * half)


LAST = (((1,), (1,)), ((), ()))


def ignoring(kernel, scalars, count):
    def body(*refs):
        return kernel(*refs[:scalars], *refs[scalars + count :])

    return body


def anywhere(deps):
    return [pl.BlockSpec(memory_space=pl.ANY)] * len(deps)


def takes(microseconds):
    return pl.CostEstimate(
        flops=int(microseconds * 0.45e9 * 1.1535), bytes_accessed=0, transcendentals=0
    )


def copy_all_kernel(x_ref, out_ref):
    out_ref[...] = x_ref[...]


def copy_later(x, deps):
    whole = pl.BlockSpec(x.shape, lambda i: (0, 0))
    return pl.pallas_call(
        ignoring(copy_all_kernel, 0, len(deps)),
        grid=(1,),
        in_specs=anywhere(deps) + [whole],
        out_specs=whole,
        out_shape=jax.ShapeDtypeStruct(x.shape, x.dtype),
        cost_estimate=takes(1),
        name="copy_later",
    )(*deps, x)


def nothing_kernel(*refs):
    pass


def gate(values, *deps):
    values = tuple(values)
    count = len(deps)
    return pl.pallas_call(
        nothing_kernel,
        in_specs=anywhere(deps) + anywhere(values),
        out_specs=anywhere(values),
        out_shape=[jax.ShapeDtypeStruct(v.shape, v.dtype) for v in values],
        input_output_aliases={count + i: i for i in range(len(values))},
        cost_estimate=takes(0),
        name="gate",
    )(*deps, *values)


def forward_kernel(blocks, info_ref, q_ref, kv_ref, o_ref, lse_ref, q_sc, m_sc, l_sc, acc_sc):
    half = q_ref.shape[0] // 2
    wide = GROUP * half
    length = info_ref[0]
    scale = SCORE_SCALE * LOG2E
    for slot in range(2):
        block = info_ref[1 + slot]
        rows = slice(slot * half, (slot + 1) * half)
        for head in range(GROUP):
            q_sc[:, head * half : (head + 1) * half] = one_head(q_ref, rows, head, True).T
        m_sc[...] = jnp.full_like(m_sc, NEGATIVE)
        l_sc[...] = jnp.zeros_like(l_sc)
        acc_sc[...] = jnp.zeros_like(acc_sc)

        def work(step, masked):
            pair = two_blocks(kv_ref, step, blocks, half)
            values_t = pair.T[HEAD_SIZE:]
            if masked:
                allowed = allowed_keys(step, block, length, half)
                allowed = jnp.concatenate([allowed, allowed], 1)
            sides = [slice(i * wide // 2, (i + 1) * wide // 2) for i in range(2)]
            both = [jnp.dot(pair, q_sc[:, at], preferred_element_type=f32) for at in sides]
            for at, scores in zip(sides, both):
                if masked:
                    scores = jnp.where(allowed, scores, NEGATIVE)
                m_old = m_sc[:1, at]
                m_new = jnp.maximum(m_old, jnp.max(scores, 0, keepdims=True) * scale)
                weights = jnp.exp2(scores * scale - m_new)
                fading = jnp.exp2(m_old - m_new)
                m_sc[:1, at] = m_new
                sums = jnp.sum(weights.reshape(2 * half // 8, 8, wide // 2), 0)
                l_sc[:, at] = l_sc[:, at] * fading + sums
                acc_sc[:, at] = acc_sc[:, at] * fading + jnp.dot(
                    values_t, weights.astype(bf16), preferred_element_type=f32
                )

        steps = key_steps(block, length, half)

        @pl.loop(0, steps - 1)
        def _(step):
            work(step, False)

        work(steps - 1, True)
        total = jnp.sum(l_sc[...], 0, keepdims=True)
        result = acc_sc[...] / total
        lse = m_sc[:1] + jnp.log2(total)
        for at in range(0, GROUP, 2):
            two = [result[:, head * half : (head + 1) * half] for head in (at, at + 1)]
            o_ref[rows, at * HEAD_SIZE : (at + 2) * HEAD_SIZE] = (
                jnp.concatenate(two, 0).T.astype(bf16)
            )
        for head in range(GROUP):
            lse_ref[0, head : head + 1, rows] = lse[:, head * half : (head + 1) * half]


def attend(head, count, grown, q, pairs, info, deps=()):
    rows, keys = q.shape[0], pairs.shape[0]
    half = rows // 2
    wide = GROUP * half
    width = GROUP * HEAD_SIZE
    aliases = {1 + i: i for i in range(len(grown))}
    deps = tuple(grown) + tuple(deps)
    return pl.pallas_call(
        ignoring(functools.partial(forward_kernel, keys // half), 1, len(deps)),
        grid_spec=pltpu.PrefetchScalarGridSpec(
            num_scalar_prefetch=1,
            grid=(count,),
            in_specs=anywhere(deps)
            + [
                pl.BlockSpec((rows, width), lambda g, info: (0, head + g)),
                pl.BlockSpec((keys, PAIR), lambda g, info: (0, head + g)),
            ],
            out_specs=[
                pl.BlockSpec((rows, width), lambda g, info: (0, head + g)),
                pl.BlockSpec((1, GROUP, rows), lambda g, info: (head + g, 0, 0)),
            ],
            scratch_shapes=[
                pltpu.VMEM((PAIR, wide), bf16),
                pltpu.VMEM((8, wide), f32),
                pltpu.VMEM((8, wide), f32),
                pltpu.VMEM((HEAD_SIZE, wide), f32),
            ],
        ),
        out_shape=[
            jax.ShapeDtypeStruct(q.shape, bf16),
            jax.ShapeDtypeStruct((KEY_VALUE_HEADS, GROUP, rows), f32),
        ],
        input_output_aliases=aliases,
        compiler_params=pltpu.CompilerParams(vmem_limit_bytes=20 << 20),
        cost_estimate=takes(10 * count),
        name="attend",
    )(info, *deps, q, pairs)


def backward_kernel(
    blocks, info_ref, q_ref, do_ref, o_ref, lse_ref, kv_ref, cos_ref, sin_ref,
    dq_ref, same_ref, other_ref, both_sc, q_sc, do_sc, row_sc, dq_sc, dkv_sc, terms_sc,
):
    half = q_ref.shape[0] // 2
    wide = GROUP * half
    length = info_ref[0]
    dkv_sc[...] = jnp.zeros_like(dkv_sc)
    for slot in range(2):
        block = info_ref[1 + slot]
        rows = slice(slot * half, (slot + 1) * half)
        for head in range(GROUP):
            at = slice(head * half, (head + 1) * half)
            query = one_head(q_ref, rows, head, True)
            grad = one_head(do_ref, rows, head, False)
            both_sc[head * half : (head + 1) * half] = query
            both_sc[wide + head * half : wide + (head + 1) * half] = grad
            q_sc[:, at] = query.T
            do_sc[:, at] = grad.T
            row_sc[1:2, at] = lse_ref[0, head : head + 1, rows]
        for at in range(0, GROUP, 2):
            lanes = slice(at * HEAD_SIZE, (at + 2) * HEAD_SIZE)
            product = (do_ref[rows, lanes].astype(f32) * o_ref[rows, lanes].astype(f32)).T
            for i in range(2):
                row_sc[:1, (at + i) * half : (at + i + 1) * half] = jnp.sum(
                    product[i * HEAD_SIZE : (i + 1) * HEAD_SIZE], 0, keepdims=True
                )
        dq_sc[...] = jnp.zeros_like(dq_sc)

        def work(step, masked):
            pair = two_blocks(kv_ref, step, blocks, half)
            keys_t = pair.T[:HEAD_SIZE]
            if masked:
                allowed = allowed_keys(step, block, length, half)
            sides = [slice(head * half, (head + 1) * half) for head in range(GROUP)]

            def products(at):
                return (
                    jnp.dot(pair, q_sc[:, at], preferred_element_type=f32),
                    jnp.dot(pair, do_sc[:, at], preferred_element_type=f32),
                )

            coming = products(sides[0])
            for head, at in enumerate(sides):
                scores, grad_probs = coming
                if head + 1 < GROUP:
                    coming = products(sides[head + 1])
                probs = jnp.exp2(scores * (SCORE_SCALE * LOG2E) - row_sc[1:2, at])
                if masked:
                    probs = jnp.where(allowed, probs, 0.0)
                grad_scores = (probs * (grad_probs - row_sc[:1, at])).astype(bf16)
                terms_sc[:, at] = grad_scores
                terms_sc[:, wide + head * half : wide + (head + 1) * half] = probs.astype(bf16)
                dq_sc[:, at] += jnp.dot(keys_t, grad_scores, preferred_element_type=f32)
            update = jnp.dot(terms_sc[...], both_sc[...], preferred_element_type=f32)
            for i in range(2):
                at = pl.ds(block_row(2 * step + i, blocks, half), half)
                dkv_sc[at, :] += update[i * half : (i + 1) * half]

        steps = key_steps(block, length, half)

        @pl.loop(0, steps - 1)
        def _(step):
            work(step, False)

        work(steps - 1, True)
        for at in range(0, GROUP, 2):
            two = [dq_sc[:, head * half : (head + 1) * half] for head in (at, at + 1)]
            grad = jnp.concatenate(two, 0).T * SCORE_SCALE
            grad = grad * cos_ref[rows, :] - swap_halves(grad) * sin_ref[rows, :]
            dq_ref[rows, at * HEAD_SIZE : (at + 2) * HEAD_SIZE] = grad.astype(bf16)
    lane = lax.broadcasted_iota(jnp.int32, (2 * half, PAIR), 1)
    scale = jnp.where(lane < HEAD_SIZE, SCORE_SCALE, 1.0)
    core = info_ref[3]
    for i in range(blocks // 4):
        rows = slice(i * 2 * half, (i + 1) * 2 * half)
        for ref, side in ((same_ref, core), (other_ref, 1 - core)):
            at = pl.ds(pl.multiple_of((2 * i + side) * 2 * half, 2 * half), 2 * half)
            ref[rows, :] = (dkv_sc[at, :] * scale).astype(bf16)


def attend_back(head, span, grown, q, grad, attended, lse, pairs, cos, sin, info, deps=()):
    rows, keys = q.shape[0], pairs.shape[0]
    half = rows // 2
    wide = GROUP * half
    width = GROUP * HEAD_SIZE
    filled = [at for at, value in enumerate(grown) if value is not None]
    aliases = {1 + i: at for i, at in enumerate(filled)}
    deps = tuple(grown[at] for at in filled) + tuple(deps)
    head_block = pl.BlockSpec((rows, width), lambda g, info: (0, head))
    half_block = pl.BlockSpec((keys // 2, PAIR), lambda g, info: (0, head - span[0]))
    table = pl.BlockSpec((rows, PAIR), lambda g, info: (0, 0))
    half_shape = jax.ShapeDtypeStruct((keys // 2, span[1] * PAIR), bf16)
    return pl.pallas_call(
        ignoring(functools.partial(backward_kernel, keys // half), 1, len(deps)),
        grid_spec=pltpu.PrefetchScalarGridSpec(
            num_scalar_prefetch=1,
            grid=(1,),
            in_specs=anywhere(deps)
            + [
                head_block,
                head_block,
                head_block,
                pl.BlockSpec((1, GROUP, rows), lambda g, info: (head, 0, 0)),
                pl.BlockSpec((keys, PAIR), lambda g, info: (0, head)),
                table,
                table,
            ],
            out_specs=[head_block, half_block, half_block],
            scratch_shapes=[
                pltpu.VMEM((2 * wide, PAIR), bf16),
                pltpu.VMEM((PAIR, wide), bf16),
                pltpu.VMEM((PAIR, wide), bf16),
                pltpu.VMEM((8, wide), f32),
                pltpu.VMEM((HEAD_SIZE, wide), f32),
                pltpu.VMEM((keys, PAIR), f32),
                pltpu.VMEM((2 * half, 2 * wide), bf16),
            ],
        ),
        out_shape=[jax.ShapeDtypeStruct(q.shape, bf16), half_shape, half_shape],
        input_output_aliases=aliases,
        compiler_params=pltpu.CompilerParams(vmem_limit_bytes=24 << 20),
        cost_estimate=takes(16),
        name="attend_back",
    )(info, *deps, q, grad, attended, lse, pairs, cos, sin)


def outer_kernel(parts, core_ref, a_ref, b_ref, keep_ref, send_ref, at_sc):
    @pl.when(pl.program_id(0) == 0)
    def _():
        at_sc[...] = a_ref[...].T

    rows = at_sc.shape[0] // parts // 2
    for i in range(parts):
        for side, ref in enumerate((keep_ref, send_ref)):
            half = jnp.bitwise_xor(core_ref[0], side)
            start = pl.multiple_of((2 * i + half) * rows, 16)
            ref[i] = jnp.dot(
                at_sc[pl.ds(start, rows), :], b_ref[...], preferred_element_type=f32
            ).astype(bf16)


def outer_rows(core, a, b, parts, deps=()):
    tokens, model = a.shape
    width = b.shape[1]
    block = KEY_VALUE_HEADS * PAIR
    rows = model // parts // 2
    out = jax.ShapeDtypeStruct((parts, rows, width), bf16)
    spec = pl.BlockSpec((parts, rows, block), lambda i, core: (0, 0, i))
    return pl.pallas_call(
        ignoring(functools.partial(outer_kernel, parts), 1, len(deps)),
        grid_spec=pltpu.PrefetchScalarGridSpec(
            num_scalar_prefetch=1,
            grid=(width // block,),
            in_specs=anywhere(deps)
            + [
                pl.BlockSpec((tokens, model), lambda i, core: (0, 0)),
                pl.BlockSpec((tokens, block), lambda i, core: (0, i)),
            ],
            out_specs=[spec, spec],
            scratch_shapes=[pltpu.VMEM((model, tokens), bf16)],
        ),
        out_shape=[out, out],
        compiler_params=pltpu.CompilerParams(vmem_limit_bytes=20 << 20),
        cost_estimate=takes(3),
        name="outer_rows",
    )(core, *deps, a, b)


def place_kernel(count, spots_ref, *refs):
    out_ref, sems = refs[count], refs[count + 1]
    copies = []
    for i, ref in enumerate(refs[:count]):
        start = pl.multiple_of(spots_ref[i], 16)
        copy = pltpu.make_async_copy(ref, out_ref.at[pl.ds(start, ref.shape[0])], sems.at[i])
        copy.start()
        copies.append(copy)
    for copy in copies:
        copy.wait()


def place(pieces, spots, rows):
    count = len(pieces)
    width = pieces[0].shape[1]
    return pl.pallas_call(
        functools.partial(place_kernel, count),
        grid_spec=pltpu.PrefetchScalarGridSpec(
            num_scalar_prefetch=1,
            grid=(1,),
            in_specs=anywhere(pieces),
            out_specs=pl.BlockSpec((rows, width), lambda i, spots: (0, 0)),
            scratch_shapes=[pltpu.SemaphoreType.DMA((count,))],
        ),
        out_shape=jax.ShapeDtypeStruct((rows, width), pieces[0].dtype),
        compiler_params=pltpu.CompilerParams(vmem_limit_bytes=24 << 20),
        cost_estimate=takes(3),
        name="place",
    )(jnp.stack(spots).astype(jnp.int32), *pieces)


def split_kernel(parts, core_ref, gate_ref, up_ref, out_ref):
    width = gate_ref.shape[1] // parts // 2
    for core in range(2):

        @pl.when(core_ref[0] == core)
        def _():
            taken = []
            for ref in (gate_ref, up_ref):
                for i in range(parts):
                    at = (2 * i + core) * width
                    taken.append(ref[:, at : at + width])
            out_ref[...] = jnp.concatenate(taken, 1)


def split_columns(core, gate, up, parts, deps=()):
    rows, width = gate.shape
    block = rows // 2
    spec = pl.BlockSpec((block, width), lambda i, core: (i, 0))
    return pl.pallas_call(
        ignoring(functools.partial(split_kernel, parts), 1, len(deps)),
        grid_spec=pltpu.PrefetchScalarGridSpec(
            num_scalar_prefetch=1,
            grid=(2,),
            in_specs=anywhere(deps) + [spec, spec],
            out_specs=spec,
        ),
        out_shape=jax.ShapeDtypeStruct((rows, width), gate.dtype),
        cost_estimate=takes(3.5),
        name="split_columns",
    )(core, *deps, gate, up)


def merge_kernel(parts, core_ref, own_ref, other_ref, out_ref):
    width = own_ref.shape[1] // parts
    for core in range(2):

        @pl.when(core_ref[0] == core)
        def _():
            taken = []
            for i in range(parts):
                for ref in (own_ref, other_ref) if core == 0 else (other_ref, own_ref):
                    taken.append(ref[:, i * width : (i + 1) * width].astype(f32))
            out_ref[...] = jnp.concatenate(taken, 1)


def merge_columns(core, own, other, parts):
    rows, width = own.shape
    block = rows // 4 if rows % 64 == 0 else rows // 2
    spec = pl.BlockSpec((block, width), lambda i, core: (i, 0))
    return pl.pallas_call(
        functools.partial(merge_kernel, parts),
        grid_spec=pltpu.PrefetchScalarGridSpec(
            num_scalar_prefetch=1,
            grid=(rows // block,),
            in_specs=[spec, spec],
            out_specs=pl.BlockSpec((block, 2 * width), lambda i, core: (i, 0)),
        ),
        out_shape=jax.ShapeDtypeStruct((rows, 2 * width), f32),
        compiler_params=pltpu.CompilerParams(vmem_limit_bytes=24 << 20),
        cost_estimate=takes(2.7),
        name="merge_columns",
    )(core, own, other)


def after(value, *others):
    return lax.optimization_barrier((value,) + others)[0]


class Moves:
    def __init__(self):
        self.ctx, self.fsdp = lax.axis_size("ctx"), lax.axis_size("fsdp")
        self.me, self.where = lax.axis_index("fsdp"), lax.axis_index("ctx")
        self.core = self.where % 2
        self.square = self.fsdp == 4
        self.line = self.ctx == 8

    def across(self, value, bit):
        return lax.ppermute(value, "fsdp", [(i, i ^ bit) for i in range(self.fsdp)])

    def swap(self, value):
        return lax.ppermute(value, "ctx", [(i, i ^ 1) for i in range(self.ctx)])

    def pick(self, low, high):
        return jnp.where(self.core == 0, low, high)

    def owner(self, half):
        return half if half < self.ctx else 2 * self.ctx - 1 - half

    def balance(self, rows):
        half = rows.shape[0] // 2
        return jnp.concatenate(
            [
                lax.ppermute(
                    rows[i * half : (i + 1) * half],
                    "ctx",
                    [(d, self.owner(2 * d + i)) for d in range(self.ctx)],
                )
                for i in range(2)
            ],
            0,
        )

    def restore(self, rows):
        half = rows.shape[0] // 2
        return jnp.concatenate(
            [
                lax.ppermute(
                    rows[i * half : (i + 1) * half],
                    "ctx",
                    [(self.owner(2 * d + i), d) for d in range(self.ctx)],
                )
                for i in range(2)
            ],
            0,
        )

    def gather_all(self, own):
        return lax.all_gather(own, "fsdp", axis=0, tiled=True)

    def gather_first(self, own):
        return (self.across(own, 1), self.across(own, 2)) if self.square else ()

    def gather_last(self, own, arrived):
        if not self.square:
            return self.gather_all(own)
        rows = own.shape[0]
        half = rows // 32 * 16
        by_x, by_y = arrived
        top, bottom = self.across(by_x[:half], 2), self.across(by_y[half:], 1)
        me = self.me
        spots = [me * rows, (me ^ 1) * rows, (me ^ 2) * rows, (me ^ 3) * rows, (me ^ 3) * rows + half]
        return place([own, by_x, by_y, top, bottom], spots, 4 * rows)

    def chip(self, value, bit):
        return lax.ppermute(value, "ctx", [(i, i ^ (2 * bit)) for i in range(self.ctx)])

    def gather_pairs(self, pairs):
        if not self.line:
            return lax.all_gather(pairs, "ctx", axis=0, tiled=True)
        rows = pairs.shape[0]
        pieces, spots = [], []
        for bit in (0, 3, 2, 1):
            piece = pairs if bit == 0 else self.chip(pairs, bit)
            pieces += [piece, self.swap(piece)]
            spots += [(self.where ^ (2 * bit)) * rows, (self.where ^ (2 * bit + 1)) * rows]
        return place(pieces, spots, self.ctx * rows)

    def scatter_pairs(self, kept):
        groups = [list(range(c, self.ctx, 2)) for c in range(2)]
        return lax.psum_scatter(
            kept, "ctx", scatter_dimension=0, axis_index_groups=groups, tiled=True
        )

    def scatter_at_once(self, whole):
        if not self.square:
            rows = whole.shape[1]
            flat = whole.reshape(self.fsdp * rows, -1)
            return lax.psum_scatter(flat, "fsdp", scatter_dimension=0, tiled=True), ()
        part = lambda bit: lax.dynamic_index_in_dim(whole, self.me ^ bit, 0, keepdims=False)
        moved = [self.across(part(bit), bit) for bit in (3, 1, 2)]
        wide = [value.astype(f32) for value in moved]
        total = (part(0).astype(f32) + wide[0]) + (wide[1] + wide[2])
        return total.astype(bf16), tuple(moved)

    def total_at_once(self, part):
        if not self.line:
            return self.over_line(part)
        moved = [part] + [self.chip(part, bit) for bit in (1, 2, 3)]
        z = self.where // 2
        low = lambda a, b: jnp.where(z % 2 == 0, a, b).astype(f32)
        near = low(moved[0], moved[1]) + low(moved[1], moved[0])
        far = low(moved[2], moved[3]) + low(moved[3], moved[2])
        first = jnp.where(z // 2 == 0, near, far)
        second = jnp.where(z // 2 == 0, far, near)
        return (first + second).astype(bf16)

    def over_line(self, part):
        groups = [list(range(c, self.ctx, 2)) for c in range(2)]
        return lax.psum(part, "ctx", axis_index_groups=groups)

    def along(self, value, pairs):
        return lax.ppermute(
            value, "ctx", [(2 * a + c, 2 * b + c) for a, b in pairs for c in range(2)]
        )

    def inward(self, part):
        return (self.along(part, [(0, 1), (3, 2)]),) if self.line else ()

    def crossing(self, part, arrived):
        if not self.line:
            return part, ()
        inner = part + arrived[0]
        return inner, (self.along(inner, [(1, 2), (2, 1)]),)

    def outward(self, inner, arrived):
        if not self.line:
            return inner, ()
        summed = inner + arrived[0]
        return summed, (self.along(summed, [(1, 0), (2, 3)]),)

    def settled(self, summed, arrived):
        if not self.line:
            return self.over_line(summed)
        z = self.where // 2
        return jnp.where((z == 0) | (z == 3), arrived[0], summed)

    def both_cores(self, part):
        other = self.swap(part)
        return self.pick(part, other), self.pick(other, part)


def local(
    tokens,
    lengths,
    cotangent,
    gain_one,
    query_weight,
    key_matrix,
    value_matrix,
    out_weight,
    gain_two,
    gate_weight,
    up_weight,
    down_weight,
):
    slots, block_length, model = tokens.shape
    moves = Moves()
    fsdp = moves.fsdp
    half = block_length // 2
    shard = model // fsdp
    attention_width = QUERY_HEADS * HEAD_SIZE
    pair_width = KEY_VALUE_HEADS * PAIR
    length = lengths[0]

    ctx = moves.where
    last = 2 * moves.ctx - 1
    block_a = jnp.where(ctx % 2 == 0, ctx, last - ctx).astype(jnp.int32)
    block_b = last - block_a
    info = jnp.stack([length, block_a, block_b, moves.core]).astype(jnp.int32)
    within = jnp.arange(half, dtype=jnp.int32)
    position = jnp.concatenate([block_a * half + within, block_b * half + within])
    exponent = jnp.arange(HALF_HEAD).astype(f32) * (2.0 / HEAD_SIZE)
    phase = position.astype(f32)[:, None] * jnp.power(10000.0, -exponent)[None, :]
    cos, sin = jnp.cos(phase), jnp.sin(phase)
    cos = jnp.concatenate([cos, cos, cos, cos], -1)
    sin = jnp.concatenate([-sin, sin, -sin, sin], -1)
    valid = (position < length).astype(f32)[:, None]

    core = moves.core.astype(jnp.int32)[None]
    in_half = shard // 2
    by_head = lambda w: w.reshape(shard, KEY_VALUE_HEADS, HEAD_SIZE)
    pair_weight = jnp.concatenate([by_head(key_matrix), by_head(value_matrix)], -1)
    pair_weight = pair_weight.reshape(shard, pair_width)
    gains = jnp.concatenate([gain_one, gain_two])[None, :]
    gains = jnp.pad(gains, ((0, EXTRA - 1), (0, pair_width - 2 * shard)))
    own_pair = jnp.concatenate([moves.pick(pair_weight[:in_half], pair_weight[in_half:]), gains], 0)
    x = moves.balance(tokens.reshape(block_length, model)).astype(f32)
    arrived = moves.gather_first(own_pair)
    own_query = core_rows(core, query_weight)
    whole_query = moves.gather_all(own_query)
    whole_pair = moves.gather_last(own_pair, arrived)
    whole_pair = whole_pair.reshape(fsdp, in_half + EXTRA, pair_width)
    gain_rows = whole_pair[:, in_half, : 2 * shard].astype(f32)
    gain_first = gain_rows[:, :shard].reshape(1, model)
    gain_second = gain_rows[:, shard:].reshape(1, model)
    beside = lambda two: jnp.stack(two, 1).reshape(model, -1)
    full_pair = beside(moves.both_cores(whole_pair[:, :in_half]))
    own_wide = split_columns(core, gate_weight, up_weight, fsdp)
    wide_arrived = moves.gather_first(own_wide)

    scale_one = rms_scale(x)
    normed = (x * scale_one * gain_first).astype(bf16)
    pairs = project(True, normed, full_pair, cos, sin)
    all_pairs = lax.all_gather(pairs, "ctx", axis=0, tiled=True)
    (whole_query,) = gate((whole_query,), pairs)
    full_query = beside(moves.both_cores(whole_query.reshape(fsdp, in_half, -1)))
    queries = project(False, normed, full_query, cos, sin)
    own_out = core_rows(core, out_weight, (queries,))
    whole_out = moves.gather_all(own_out)
    own_down = core_rows(core, down_weight, (own_out,))
    full_down = moves.gather_all(own_down)
    if wide_arrived:
        wide_arrived = gate(wide_arrived, queries)
    full_wide = moves.gather_last(own_wide, wide_arrived)
    late = copy_later(cotangent.reshape(block_length, model), (all_pairs, queries))
    cotangent_rows = moves.balance(late)
    ff_half = gate_weight.shape[1] // fsdp // 2
    ff_core = ff_half * fsdp
    grown = attend(0, 3, (), queries, all_pairs, info, (own_down, late))
    (whole_out,) = gate((whole_out,), grown[1])
    out_cores = moves.both_cores(whole_out.reshape(fsdp, in_half, model))
    full_out = beside(out_cores)
    attended, log_total = attend(
        3, 2, grown, queries, all_pairs, info, (cotangent_rows, full_wide)
    )
    hidden = x + jnp.dot(attended, full_out, preferred_element_type=f32)
    scale_two = rms_scale(hidden)
    normed_two = (hidden * scale_two * gain_second).astype(bf16)

    grad_result = valid * cotangent_rows.astype(f32)
    grad_low = grad_result.astype(bf16)
    both_grad = jnp.concatenate([grad_low, moves.swap(grad_low)], 0)
    both_normed = jnp.concatenate([normed_two, moves.swap(normed_two)], 0)
    wide = jnp.dot(both_normed, full_wide, preferred_element_type=f32)
    gate_pre, up_pre = wide[:, :ff_core], wide[:, ff_core:]
    sigmoid = jax.nn.sigmoid(gate_pre)
    silu = gate_pre * sigmoid
    inner = (silu * up_pre).astype(bf16)
    grad_inner = lax.dot_general(both_grad, full_down, LAST, preferred_element_type=f32)
    grad_gate_pre = grad_inner * up_pre * sigmoid * (1.0 + gate_pre * (1.0 - sigmoid))
    grad_up_pre = grad_inner * silu
    grad_wide = jnp.concatenate([grad_gate_pre.astype(bf16), grad_up_pre.astype(bf16)], 1)
    first = (((0,), (0,)), ((), ()))
    outer = lambda a, b: lax.dot_general(a, b, first, preferred_element_type=f32).astype(bf16)
    partial = lax.dot_general(grad_wide, full_wide, LAST, preferred_element_type=f32)
    grad_normed_two = partial[:block_length] + moves.swap(partial[block_length:].astype(bf16))
    grad_gain_two = jnp.sum(grad_normed_two * hidden * scale_two, 0)
    grad_hidden = grad_result + norm_back(grad_normed_two, hidden, scale_two, gain_second)
    hidden_low = grad_hidden.astype(bf16)
    shared = lambda grad: lax.psum_scatter(grad, "fsdp", scatter_dimension=0, tiled=True)
    gate_terms = outer(both_normed, grad_wide[:, :ff_core])
    up_terms = outer(both_normed, grad_wide[:, ff_core:])
    gate_shared, up_shared = shared(gate_terms), shared(up_terms)

    grad_attended = lax.dot_general(
        hidden_low, full_out, LAST, preferred_element_type=f32
    ).astype(bf16)

    def back(head, span, grown, *deps):
        return attend_back(
            head, span, grown, queries, grad_attended, attended, log_total, all_pairs, cos, sin,
            info, deps,
        )

    span = (0, KEY_VALUE_HEADS)
    grown = back(0, span, (None, None, None), gate_terms, up_terms)
    (inner,) = gate((inner,), grown[0])
    partial_out = jnp.dot(inner, full_down, preferred_element_type=f32)
    grown = back(1, span, grown, partial_out)
    result = hidden + (
        partial_out[:block_length] + moves.swap(partial_out[block_length:].astype(bf16))
    )
    output = moves.restore((valid * result).astype(bf16))
    down_terms = outer(inner, both_grad)
    down_shared = shared(down_terms)
    gate_in = moves.inward(gate_shared)
    grown = back(2, span, grown, down_terms, gate_shared)
    grown = back(3, span, grown)
    gate_inner, gate_across = moves.crossing(gate_shared, gate_in)
    grown = back(4, span, grown, output, *gate_in)
    grad_query_pre, same, other = grown

    pair_sum = moves.scatter_pairs(same + moves.swap(other))
    up_shared, down_shared = gate((up_shared, down_shared), grad_query_pre)
    up_in = moves.inward(up_shared)
    down_in = moves.inward(down_shared)
    gate_sum, gate_out = moves.outward(gate_inner, gate_across)
    from_out = outer_rows(core, attended, hidden_low, fsdp, (grad_query_pre,))
    from_query = outer_rows(core, normed, grad_query_pre, fsdp)
    square = [jnp.concatenate(two, 2) for two in zip(from_out, from_query)]
    square_shared = shared((square[0] + moves.swap(square[1])).reshape(model // 2, -1))
    by_query = lax.dot_general(grad_query_pre, full_query, LAST, preferred_element_type=f32)

    up_inner, up_across = moves.crossing(up_shared, up_in)
    down_inner, down_across = moves.crossing(down_shared, down_in)
    grad_pair_pre = unrotate(pair_sum, cos, sin, (by_query,) + up_in + down_in + gate_out)
    by_pair = lax.dot_general(grad_pair_pre, full_pair, LAST, preferred_element_type=f32)
    from_pair = outer_rows(core, normed, grad_pair_pre, fsdp)
    grad_normed = by_query + by_pair
    grad_gain_one = jnp.sum(grad_normed * x * scale_one, 0)
    grad_tokens = (grad_hidden + norm_back(grad_normed, x, scale_one, gain_first)).astype(bf16)
    gain_grads = jnp.stack([grad_gain_one.reshape(fsdp, shard), grad_gain_two.reshape(fsdp, shard)], 1)
    gain_grads = jnp.pad(
        gain_grads[:, :, None].astype(bf16),
        ((0, 0), (0, 0), (0, EXTRA - 1), (0, pair_width - shard)),
    )
    mine_too = moves.pick(gain_grads[:, 0], gain_grads[:, 1])
    others_too = moves.pick(gain_grads[:, 1], gain_grads[:, 0])
    keep = jnp.concatenate([from_pair[0], mine_too], 1)
    send = jnp.concatenate([from_pair[1], others_too], 1)
    pair_shared = shared((keep + moves.swap(send)).reshape(fsdp * (in_half + EXTRA), -1))
    pair_part = moves.over_line(pair_shared)
    square_part = moves.over_line(square_shared)
    grad_tokens = moves.restore(grad_tokens)

    gate_part = moves.settled(gate_sum, gate_out)
    gate_other = moves.swap(gate_part)
    up_sum, up_out = moves.outward(up_inner, up_across)
    grad_gate = merge_columns(core, gate_part, gate_other, fsdp)
    up_part = moves.settled(up_sum, up_out)
    grad_up = merge_columns(core, up_part, moves.swap(up_part), fsdp)
    down_sum, down_out = moves.outward(down_inner, down_across)
    down_low, down_high = moves.both_cores(moves.settled(down_sum, down_out))
    pair_parts = moves.both_cores(pair_part)
    square_parts = moves.both_cores(square_part)

    below = lambda parts: jnp.concatenate(parts, 0).astype(f32)
    pair_grad = below([part[:in_half] for part in pair_parts])
    pair_grad = pair_grad.reshape(shard, KEY_VALUE_HEADS, PAIR)
    return (
        output.reshape(slots, block_length, model),
        grad_tokens.reshape(slots, block_length, model),
        pair_parts[0][in_half, :shard].astype(f32),
        below([part[:, model:] for part in square_parts]),
        pair_grad[:, :, :HEAD_SIZE].reshape(shard, -1),
        pair_grad[:, :, HEAD_SIZE:].reshape(shard, -1),
        below([part[:, :model] for part in square_parts]),
        pair_parts[1][in_half, :shard].astype(f32),
        grad_gate,
        grad_up,
        below([down_low, down_high]),
    )


def solution(mesh):
    rows, whole = P("fsdp", None), P("fsdp", "ctx", None)
    return jax.shard_map(
        local,
        mesh=mesh,
        in_specs=(
            whole, P("fsdp"), whole, P("fsdp"), rows, rows, rows, rows, P("fsdp"), rows, rows, rows,
        ),
        out_specs=(
            whole, whole, P("fsdp"), rows, rows, rows, rows, P("fsdp"), rows, rows, rows,
        ),
        check_vma=False,
    )
```

time: 917 us -> 720 us (0.79)
  starting transfers between devices: 224 us -> 70.5 us
  waiting for transfers between devices: 326 us -> 248 us
  local copies, waits for them, and re-layouts: 49.1 us -> 76.3 us
  Pallas kernels: 127 us -> 143 us
  other arithmetic: 75.8 us -> 60.9 us
    ppermute x36 -> x8, starting transfers between devices: 141 us -> 7.78 us  [across(): return lax.ppermute(value, 'fsdp', [(i, i ^ bit) for i in range(self.fsdp)])]
    ppermute x36 -> x8, waiting for transfers between devices: 133 us -> 45.3 us  [across(): return lax.ppermute(value, 'fsdp', [(i, i ^ bit) for i in range(self.fsdp)])]
    ppermute x15 -> x9, waiting for transfers between devices: 181 us -> 94.2 us  [along(): lax.ppermute(value, 'ctx', [(2 * a + c, 2 * b + c) for a, b in pairs for...]
    psum x0 -> x1, waiting for transfers between devices: none -> 64.6 us  [over_line(): return lax.psum(part, 'ctx', axis_index_groups=groups)]
    unnamed x140 -> x197, local copies, waits for them, and re-layouts: 30.8 us -> 63 us
    ppermute x14 -> x15, starting transfers between devices: 21.7 us -> 4.59 us  [swap(): return lax.ppermute(value, 'ctx', [(i, i ^ 1) for i in range(self.ctx)])]
    ppermute x14 -> x15, waiting for transfers between devices: 0.04 us -> 16.8 us  [swap(): return lax.ppermute(value, 'ctx', [(i, i ^ 1) for i in range(self.ctx)])]
    pallas_call x5 -> x23, Pallas kernels: 114 us -> 130 us  [the longest x5 62.5 us: attend_back(): pl.pallas_call(ignoring(functools.partial(backward_kernel, keys // half),...]
  transfers between devices with their start and end apart: 75 -> 51, of which waited for: 31 -> 16; matrix products, arithmetic and copies ran while one was open for 15% -> 21% of each run, Pallas kernels for 13% -> 20%
where the time goes in v2:
time: 720 us; the launch traced here: 710 us
  waiting for transfers between devices  248 us (34%)
  Pallas kernels  143 us (20%)
  matrix products  95.2 us (13%)
  local copies, waits for them, and re-layouts  76.3 us (11%)
  starting transfers between devices  70.5 us (10%)
  other arithmetic  60.9 us (8%)
  between operations  16.4 us (2%)
    ppermute x9, waiting for transfers between devices, along(): lax.ppermute(value, 'ctx', [(2 * a + c, 2 * b + c) for a, b in pairs for...  94.2 us
    psum x1, waiting for transfers between devices, over_line(): return lax.psum(part, 'ctx', axis_index_groups=groups)  64.6 us
    unnamed x197, local copies, waits for them, and re-layouts  63 us
    pallas_call x5, Pallas kernels, attend_back(): pl.pallas_call(ignoring(functools.partial(backward_kernel, keys // half),...  62.5 us
    ppermute x8, waiting for transfers between devices, across(): return lax.ppermute(value, 'fsdp', [(i, i ^ bit) for i in range(self.fsdp)])  45.3 us
    pallas_call x2, Pallas kernels, attend(): pl.pallas_call(ignoring(functools.partial(forward_kernel, keys // half),...  39.1 us
    ppermute x9, starting transfers between devices, along(): lax.ppermute(value, 'ctx', [(2 * a + c, 2 * b + c) for a, b in pairs for...  34.8 us
    dot_general x3, matrix products, local(): lax.dot_general(a, b, first, preferred_element_type=f32).astype(bf16)  26.7 us
  transfers between devices with their start and end apart: 51, of which 16 were waited for; matrix products, arithmetic and copies ran while one was open for 21% of the time, Pallas kernels for 20%

profile of v2, /device:TPU:0, one launch (start us, length us, event | category | flops | bytes accessed | tf_op | source)
XLA Modules:
  0.0 710.5 jit_solution(1938310587535206563)
XLA Ops:
  10.8 3.0 collective-permute-start.3
  24.9 6.3 collective-permute-done.4.refs_3_
  34.8 16.1 %collective-permute-done.1 = bf16[256,1280]{1,0:T(8,128)(2,1)} collective-permute-done((bf16[256,1280]{1,0:T(8,128)(2,1)}, bf16[256,1280]{1,0:T(8,128)(2,1)}, u32[]{:S(2)}, u32[]{:S(2)}) %collective-permute-start.1) | collective-permute-done | bytes 655392 | tf_op jit(solution)/shard_map/ppermute | solution.py:592
  60.1 3.6 split_columns.1.refs_0_
  68.6 3.5 project.3.refs_1_.refs_3_.refs_0_.refs_5_.refs_6_.refs_4_
  77.4 38.6 %collective-permute-done.11.refs_2_ = bf16[320,3584]{1,0:T(8,128)(2,1)S(1)} collective-permute-done((bf16[320,3584]{1,0:T(8,128)(2,1)}, bf16[320,3584]{1,0:T(8,128)(2,1)S(1)}, u32[]{:S(2)}, u32[]{:S(2)}) %collective-permute-start.11) | collective-permute-done | bytes 2293792 | tf_op jit(solution)/shard_map/ppermute | solution.py:577
  129.6 6.7 collective-permute-start.8
  138.9 23.3 %attend.2 = (bf16[512,1280]{1,0:T(8,128)(2,1)S(1)}, f32[5,4,512]{2,1,0:T(4,128)S(1)}) custom-call(s32[4]{0:T(128)S(1)} %pad_add_fusion.1.refs_0_, bf16[448,1280]{1,0:T(8,128)(2,1)S(1)} %copy-done.22, bf16[512,1280]{1,0:T(8,128)(2,1)S(1)} %copy-done.9, bf16[512,1280]{1,0:T(8,128)(2,1)S(1)} %copy-done.1, bf16[4096,640]{1,0:T(8,128)(2,1)S(1)} %copy-done.10), custom_call_target="tpu_custom_call" | custom-call | flops 15572249600 | tf_op jit(solution)/shard_map/attend/pallas_call | solution.py:268
  167.4 3.7 place.3.refs_4_
  174.9 15.7 %attend.3 = (bf16[512,1280]{1,0:T(8,128)(2,1)S(1)}, f32[5,4,512]{2,1,0:T(4,128)S(1)}) custom-call(s32[4]{0:T(128)S(1)} %pad_add_fusion.1.refs_0_, bf16[512,1280]{1,0:T(8,128)(2,1)S(1)} %copy-done.53, f32[5,4,512]{2,1,0:T(4,128)S(1)} %copy-done.45, ...), custom_call_target="tpu_custom_call", output_to_operand_aliasing={{0}: (1, {}), {1}: (2, {})} | custom-call | flops 10381500416 | tf_op jit(solution)/shard_map/attend/pallas_call | solution.py:268
  193.9 3.5 multiply_reduce_fusion.2
  202.0 13.1 %fusion.20 = f32[1024,3584]{1,0:T(8,128)} fusion(bf16[1280,3584]{1,0:T(8,128)(2,1)S(1)} %place.3.refs_4_, bf16[512,1280]{1,0:T(8,128)(2,1)S(1)} %collective-permute-done.15, bf16[512,1280]{1,0:T(8,128)(2,1)S(1)} %multiply_convert_fusion.3), kind=kOutput, calls=%fused_computation.72 | convolution fusion | flops 9400483840 | bytes 26476544 | tf_op jit(solution)/shard_map/dot_general | solution.py:803
  215.1 11.1 %all-gather.11.cloned.1.call-done = bf16[1792,1280]{1,0:T(8,128)(2,1)} async-done(((bf16[448,1280]{1,0:T(8,128)(2,1)}), bf16[1792,1280]{1,0:T(8,128)(2,1)}) %all-gather.11.cloned.1.call-update) | async-done | bytes 4587536 | tf_op jit(solution)/shard_map/all_gather | solution.py:617
  226.2 15.1 %multiply_convert_fusion.1 = (bf16[1024,1792]{1,0:T(8,128)(2,1)}, bf16[1024,1792]{1,0:T(8,128)(2,1)S(1)}, bf16[1024,1792]{1,0:T(8,128)(2,1)}) fusion(f32[1024,3584]{1,0:T(8,128)} %fusion.20, bf16[1792,1280]{1,0:T(8,128)(2,1)} %all-gather.11.cloned.1.call-done, bf16[512,1280]{1,0:T(8,128)(2,1)} %collective-permute-done.16, bf16[512,1280]{1,0:T(8,128)(2,1)} %fusion.18), kind=kOutput, calls=%fused_computation.8 | convolution fusion | flops 4730388480 | bytes 32899072 | tf_op jit(solution)/shard_map/dot_general | solution.py:808
  243.3 6.7 convolution_convert_fusion.2.refs_1_
  250.0 10.0 %convolution_convert_fusion.1.refs_2_ = bf16[1280,1792]{1,0:T(8,128)(2,1)} fusion(bf16[1024,1792]{1,0:T(8,128)(2,1)} %get-tuple-element.110, bf16[512,1280]{1,0:T(8,128)(2,1)} %copy-done.86, bf16[512,1280]{1,0:T(8,128)(2,1)} %copy-done.76), kind=kOutput, calls=%fused_computation.1 | convolution fusion | flops 4705157120 | bytes 10878976 | tf_op jit(solution)/shard_map/dot_general | solution.py:813
  260.1 15.1 %fusion = f32[1024,1280]{1,0:T(8,128)S(1)} fusion(bf16[1280,3584]{1,0:T(8,128)(2,1)} %copy-done.7, bf16[1024,1792]{1,0:T(8,128)(2,1)} %get-tuple-element.110, bf16[1024,1792]{1,0:T(8,128)(2,1)} %copy-done.88), kind=kOutput, calls=%fused_computation.3 | convolution fusion | flops 9409921024 | bytes 21757952 | tf_op jit(solution)/shard_map/dot_general | solution.py:814
  275.4 3.0 collective-permute-done.17
  287.2 12.5 %attend_back.5 = (bf16[512,1280]{1,0:T(8,128)(2,1)S(1)}, bf16[2048,640]{1,0:T(8,128)(2,1)S(1)}, bf16[2048,640]{1,0:T(8,128)(2,1)S(1)}) custom-call(s32[4]{0:T(128)S(1)} %pad_add_fusion.1.refs_0_, bf16[1280,1792]{1,0:T(8,128)(2,1)S(1)} %bitcast.83, bf16[1280,1792]{1,0:T(8,128)(2,1)S(1)} %bitcast.81, bf16[512,1280]{1,0:T(8,128)(2,1)S(1)} %copy-done.1, ...), custom_call_target="tpu_custom_call" | custom-call | flops 8305200128 | tf_op jit(solution)/shard_map/attend_back/pallas_call | solution.py:393
  303.8 10.0 %convolution_convert_fusion.refs_4_ = bf16[1792,1280]{1,0:T(8,128)(2,1)} fusion(bf16[1024,1792]{1,0:T(8,128)(2,1)} %gate.8, bf16[512,1280]{1,0:T(8,128)(2,1)} %collective-permute-done.16, bf16[512,1280]{1,0:T(8,128)(2,1)} %fusion.18), kind=kOutput, calls=%fused_computation | convolution fusion | flops 4705157120 | bytes 10878976 | tf_op jit(solution)/shard_map/dot_general | solution.py:813
  313.8 9.1 %fusion.49.refs_4_ = f32[1024,1280]{1,0:T(8,128)S(1)} fusion(bf16[1024,1792]{1,0:T(8,128)(2,1)} %gate.8, bf16[1792,1280]{1,0:T(8,128)(2,1)} %all-gather.11.cloned.1.call-done), kind=kOutput, calls=%fused_computation.139 | convolution fusion | flops 4697620480 | bytes 13500416 | tf_op jit(solution)/shard_map/dot_general | solution.py:837
  323.2 3.0 collective-permute-done.18
  326.8 5.3 collective-permute-start.20
  335.4 12.7 %attend_back.6 = (bf16[512,1280]{1,0:T(8,128)(2,1)S(1)}, bf16[2048,640]{1,0:T(8,128)(2,1)S(1)}, bf16[2048,640]{1,0:T(8,128)(2,1)S(1)}) custom-call(s32[4]{0:T(128)S(1)} %pad_add_fusion.1.refs_0_, bf16[512,1280]{1,0:T(8,128)(2,1)S(1)} %copy-done.19, bf16[2048,640]{1,0:T(8,128)(2,1)S(1)} %copy-done.24, ...), custom_call_target="tpu_custom_call", output_to_operand_aliasing={{0}: (1, {}), {1}: (2, {}), {2}: (3, {})} | custom-call | flops 8305200128 | tf_op jit(solution)/shard_map/attend_back/pallas_call | solution.py:393
  352.2 12.2 %collective-permute-start.21 = (bf16[320,1792]{1,0:T(8,128)(2,1)}, bf16[320,1792]{1,0:T(8,128)(2,1)S(1)}, u32[]{:S(2)}, u32[]{:S(2)}) collective-permute-start(bf16[320,1792]{1,0:T(8,128)(2,1)} %reduce-scatter.9.cloned.1.call-done.refs_5_), channel_id=1, source_target_pairs={{0,8},{4,12},{24,16},{28,20},{1,9},{5,13},{25,17},{29,21},{2,10},{... | collective-permute-start | bytes 3440648 | tf_op jit(solution)/shard_map/ppermute | solution.py:681
  377.1 12.5 %attend_back.7 = (bf16[512,1280]{1,0:T(8,128)(2,1)S(1)}, bf16[2048,640]{1,0:T(8,128)(2,1)S(1)}, bf16[2048,640]{1,0:T(8,128)(2,1)S(1)}) custom-call(s32[4]{0:T(128)S(1)} %pad_add_fusion.1.refs_0_, bf16[512,1280]{1,0:T(8,128)(2,1)S(1)} %get-tuple-element.49.refs_1_, ...), custom_call_target="tpu_custom_call", output_to_operand_aliasing={{0}: (1, {}), {1}: (2, {}), {2}: (3, {})} | custom-call | flops 8305200128 | tf_op jit(solution)/shard_map/attend_back/pallas_call | solution.py:393
  396.1 12.3 %attend_back.8 = (bf16[512,1280]{1,0:T(8,128)(2,1)S(1)}, bf16[2048,640]{1,0:T(8,128)(2,1)S(1)}, bf16[2048,640]{1,0:T(8,128)(2,1)S(1)}) custom-call(s32[4]{0:T(128)S(1)} %pad_add_fusion.1.refs_0_, bf16[512,1280]{1,0:T(8,128)(2,1)S(1)} %get-tuple-element.52.refs_1_, ...), custom_call_target="tpu_custom_call", output_to_operand_aliasing={{0}: (1, {}), {1}: (2, {}), {2}: (3, {})} | custom-call | flops 8305200128 | tf_op jit(solution)/shard_map/attend_back/pallas_call | solution.py:393
  408.4 12.5 %attend_back.9 = (bf16[512,1280]{1,0:T(8,128)(2,1)S(1)}, bf16[2048,640]{1,0:T(8,128)(2,1)S(1)}, bf16[2048,640]{1,0:T(8,128)(2,1)S(1)}) custom-call(s32[4]{0:T(128)S(1)} %pad_add_fusion.1.refs_0_, bf16[512,1280]{1,0:T(8,128)(2,1)S(1)} %get-tuple-element.55.refs_1_, ...), custom_call_target="tpu_custom_call", output_to_operand_aliasing={{0}: (1, {}), {1}: (2, {}), {2}: (3, {})} | custom-call | flops 8305200128 | tf_op jit(solution)/shard_map/attend_back/pallas_call | solution.py:393
  422.9 4.5 collective-permute-done.26
  427.4 3.9 add.144
  433.9 3.2 outer_rows.4
  437.2 3.2 outer_rows.5
  441.1 5.5 collective-permute-done.31
  453.7 10.5 %collective-permute-start.22 = (bf16[320,1792]{1,0:T(8,128)(2,1)}, bf16[320,1792]{1,0:T(8,128)(2,1)S(1)}, u32[]{:S(2)}, u32[]{:S(2)}) collective-permute-start(bf16[320,1792]{1,0:T(8,128)(2,1)} %get-tuple-element.59), channel_id=1, source_target_pairs={{0,8},{4,12},{24,16},{28,20},{1,9},{5,13},{25,17},{29,21},{2,10},{... | collective-permute-start | bytes 3440648 | tf_op jit(solution)/shard_map/ppermute | solution.py:681
  466.9 2.9 add.143
  471.1 41.9 %collective-permute-done.22.refs_1_ = bf16[320,1792]{1,0:T(8,128)(2,1)S(1)} collective-permute-done((bf16[320,1792]{1,0:T(8,128)(2,1)}, bf16[320,1792]{1,0:T(8,128)(2,1)S(1)}, u32[]{:S(2)}, u32[]{:S(2)}) %collective-permute-start.22) | collective-permute-done | bytes 1146912 | tf_op jit(solution)/shard_map/ppermute | solution.py:681
  516.5 4.8 fusion.50.refs_0_
  521.3 16.0 %collective-permute-done.23.refs_2_ = bf16[448,1280]{1,0:T(8,128)(2,1)} collective-permute-done((bf16[448,1280]{1,0:T(8,128)(2,1)}, bf16[448,1280]{1,0:T(8,128)(2,1)}, u32[]{:S(2)}, u32[]{:S(2)}) %collective-permute-start.23) | collective-permute-done | bytes 1146912 | tf_op jit(solution)/shard_map/ppermute | solution.py:681
  541.6 4.4 collective-permute-done.25.refs_3_
  547.5 3.0 add.150
  551.9 2.8 unrotate.1.refs_2_
  554.7 6.1 fusion.14
  562.9 2.9 add.152
  567.0 4.3 merge_columns.2
  571.3 10.0 %collective-permute-done.35 = bf16[320,1792]{1,0:T(8,128)(2,1)} collective-permute-done((bf16[320,1792]{1,0:T(8,128)(2,1)}, bf16[320,1792]{1,0:T(8,128)(2,1)}, u32[]{:S(2)}, u32[]{:S(2)}) %collective-permute-start.35) | collective-permute-done | bytes 1146912 | tf_op jit(solution)/shard_map/ppermute | solution.py:681
  584.1 21.8 %collective-permute-done.38 = bf16[448,1280]{1,0:T(8,128)(2,1)} collective-permute-done((bf16[448,1280]{1,0:T(8,128)(2,1)}, bf16[448,1280]{1,0:T(8,128)(2,1)}, u32[]{:S(2)}, u32[]{:S(2)}) %collective-permute-start.38) | collective-permute-done | bytes 1146912 | tf_op jit(solution)/shard_map/ppermute | solution.py:681
  611.8 6.5 collective-permute-start.27
  625.3 64.6 %all-reduce.6.cloned.1.call-done = (bf16[176,640]{1,0:T(8,128)(2,1)}, bf16[160,2560]{1,0:T(8,128)(2,1)}) async-done(((bf16[176,640]{1,0:T(8,128)(2,1)}, bf16[160,2560]{1,0:T(8,128)(2,1)}), (bf16[176,640]{1,0:T(8,128)(2,1)}, bf16[160,2560]{1,0:T(8,128)(2,1)})) %all-reduce.6.cloned.1.call-update) | async-done | bytes 1044496 | tf_op jit(solution)/shard_map/psum | solution.py:678
  (391 shorter events, 171.0 us)
Async XLA Ops:
  7.2 52.8 %all-gather.5.cloned.1.call-start = ((), (), s32[]{:S(2)}) async-start(), calls=%async_computation.6 | async-start | bytes 2048000 | tf_op jit(solution)/shard_map/all_gather | solution.py:617
  10.8 12.2 %collective-permute-start.3 = (bf16[176,640]{1,0:T(8,128)(2,1)S(1)}, bf16[176,640]{1,0:T(8,128)(2,1)S(1)}, u32[]{:S(2)}, u32[]{:S(2)}) collective-permute-start(bf16[176,640]{1,0:T(8,128)(2,1)S(1)} %fusion.29.refs_0_), channel_id=1, source_target_pairs={{0,2},{1,3},{2,0},{3,1},{4,6},{5,7},{6,4},{7,5},{8,10},{9,11},{10,... | collective-permute-start | bytes 675848 | tf_op jit(solution)/shard_map/ppermute | solution.py:577
  13.8 10.1 %collective-permute-start.2 = (bf16[176,640]{1,0:T(8,128)(2,1)S(1)}, bf16[176,640]{1,0:T(8,128)(2,1)S(1)}, u32[]{:S(2)}, u32[]{:S(2)}) collective-permute-start(bf16[176,640]{1,0:T(8,128)(2,1)S(1)} %fusion.29.refs_0_), channel_id=1, source_target_pairs={{0,1},{1,0},{2,3},{3,2},{4,5},{5,4},{6,7},{7,6},{8,9},{9,8},{10,11... | collective-permute-start | bytes 675848 | tf_op jit(solution)/shard_map/ppermute | solution.py:577
  17.1 107.4 %all-gather.7.cloned.1.call-start = ((), (), s32[]{:S(2)}) async-start(), calls=%async_computation.7 | async-start | bytes 5898240 | tf_op jit(solution)/shard_map/all_gather | solution.py:773
  18.3 16.5 %collective-permute-start = (bf16[256,1280]{1,0:T(8,128)(2,1)}, bf16[256,1280]{1,0:T(8,128)(2,1)S(1)}, u32[]{:S(2)}, u32[]{:S(2)}) collective-permute-start(bf16[256,1280]{1,0:T(8,128)(2,1)} %get-tuple-element.131), channel_id=1, source_target_pairs={{0,0},{4,8},{8,16},{12,24},{16,28},{20,20},{24,12},{28,4},{1,1},{5... | collective-permute-start | bytes 1966088 | tf_op jit(solution)/shard_map/ppermute | solution.py:592
  20.0 30.8 %collective-permute-start.1 = (bf16[256,1280]{1,0:T(8,128)(2,1)}, bf16[256,1280]{1,0:T(8,128)(2,1)}, u32[]{:S(2)}, u32[]{:S(2)}) collective-permute-start(bf16[256,1280]{1,0:T(8,128)(2,1)} %get-tuple-element.132), channel_id=1, source_target_pairs={{0,4},{4,12},{8,20},{12,28},{16,24},{20,16},{24,8},{28,0},{1,5},{5... | collective-permute-start | bytes 1966088 | tf_op jit(solution)/shard_map/ppermute | solution.py:592
  23.0 8.2 %collective-permute-start.5 = (bf16[96,640]{1,0:T(8,128)(2,1)S(1)}, bf16[96,640]{1,0:T(8,128)(2,1)S(1)}, u32[]{:S(2)}, u32[]{:S(2)}) collective-permute-start(bf16[96,640]{1,0:T(8,128)(2,1)S(1)} %slice.161), channel_id=1, source_target_pairs={{0,1},{1,0},{2,3},{3,2},{4,5},{5,4},{6,7},{7,6},{8,9},{9,8},{10,11... | collective-permute-start | bytes 368648 | tf_op jit(solution)/shard_map/ppermute | solution.py:577
  23.9 7.3 %collective-permute-start.4 = (bf16[80,640]{1,0:T(8,128)(2,1)S(1)}, bf16[80,640]{1,0:T(8,128)(2,1)S(1)}, u32[]{:S(2)}, u32[]{:S(2)}) collective-permute-start(bf16[80,640]{1,0:T(8,128)(2,1)S(1)} %slice.160), channel_id=1, source_target_pairs={{0,2},{1,3},{2,0},{3,1},{4,6},{5,7},{6,4},{7,5},{8,10},{9,11},{10,... | collective-permute-start | bytes 307208 | tf_op jit(solution)/shard_map/ppermute | solution.py:577
  33.1 21.2 %collective-permute-start.6 = (bf16[4,160,640]{2,1,0:T(8,128)(2,1)S(1)}, bf16[4,160,640]{2,1,0:T(8,128)(2,1)}, u32[]{:S(2)}, u32[]{:S(2)}) collective-permute-start(bf16[4,160,640]{2,1,0:T(8,128)(2,1)S(1)} %slice.164), channel_id=1, source_target_pairs={{0,4},{4,0},{8,12},{12,8},{16,20},{20,16},{24,28},{28,24},{1,5},{5... | collective-permute-start | bytes 2457608 | tf_op jit(solution)/shard_map/ppermute | solution.py:580
  59.9 104.0 %all-gather.9.cloned.1.call-start = ((), (), s32[]{:S(2)}) async-start(), calls=%async_computation.8 | async-start | bytes 2048000 | tf_op jit(solution)/shard_map/all_gather | solution.py:617
  60.0 4.7 collective-permute-start.7
  63.6 52.4 %collective-permute-start.11 = (bf16[320,3584]{1,0:T(8,128)(2,1)}, bf16[320,3584]{1,0:T(8,128)(2,1)S(1)}, u32[]{:S(2)}, u32[]{:S(2)}) collective-permute-start(bf16[320,3584]{1,0:T(8,128)(2,1)} %split_columns.1.refs_0_), channel_id=1, source_target_pairs={{0,2},{1,3},{2,0},{3,1},{4,6},{5,7},{6,4},{7,5},{8,10},{9,11},{10,... | collective-permute-start | bytes 6881288 | tf_op jit(solution)/shard_map/ppermute | solution.py:577
  64.1 52.3 %collective-permute-start.10 = (bf16[320,3584]{1,0:T(8,128)(2,1)}, bf16[320,3584]{1,0:T(8,128)(2,1)}, u32[]{:S(2)}, u32[]{:S(2)}) collective-permute-start(bf16[320,3584]{1,0:T(8,128)(2,1)} %split_columns.1.refs_0_), channel_id=1, source_target_pairs={{0,1},{1,0},{2,3},{3,2},{4,5},{5,4},{6,7},{7,6},{8,9},{9,8},{10,11... | collective-permute-start | bytes 6881288 | tf_op jit(solution)/shard_map/ppermute | solution.py:577
  76.6 149.6 %all-gather.11.cloned.1.call-start = ((), (), s32[]{:S(2)}) async-start(), calls=%async_computation.9 | async-start | bytes 5734400 | tf_op jit(solution)/shard_map/all_gather | solution.py:617
  121.1 43.0 %collective-permute-start.13 = (bf16[160,3584]{1,0:T(8,128)(2,1)}, bf16[160,3584]{1,0:T(8,128)(2,1)}, u32[]{:S(2)}, u32[]{:S(2)}) collective-permute-start(bf16[160,3584]{1,0:T(8,128)(2,1)} %slice.134), channel_id=1, source_target_pairs={{0,1},{1,0},{2,3},{3,2},{4,5},{5,4},{6,7},{7,6},{8,9},{9,8},{10,11... | collective-permute-start | bytes 3440648 | tf_op jit(solution)/shard_map/ppermute | solution.py:577
  121.6 42.5 %collective-permute-start.12 = (bf16[160,3584]{1,0:T(8,128)(2,1)}, bf16[160,3584]{1,0:T(8,128)(2,1)}, u32[]{:S(2)}, u32[]{:S(2)}) collective-permute-start(bf16[160,3584]{1,0:T(8,128)(2,1)} %slice.133), channel_id=1, source_target_pairs={{0,2},{1,3},{2,0},{3,1},{4,6},{5,7},{6,4},{7,5},{8,10},{9,11},{10,... | collective-permute-start | bytes 3440648 | tf_op jit(solution)/shard_map/ppermute | solution.py:577
  129.6 43.3 %collective-permute-start.9 = (bf16[256,1280]{1,0:T(8,128)(2,1)}, bf16[256,1280]{1,0:T(8,128)(2,1)}, u32[]{:S(2)}, u32[]{:S(2)}) collective-permute-start(bf16[256,1280]{1,0:T(8,128)(2,1)} %get-tuple-element.129), channel_id=1, source_target_pairs={{0,4},{4,12},{8,20},{12,28},{16,24},{20,16},{24,8},{28,0},{1,5},{5... | collective-permute-start | bytes 1966088 | tf_op jit(solution)/shard_map/ppermute | solution.py:592
  129.6 41.6 %collective-permute-start.8 = (bf16[256,1280]{1,0:T(8,128)(2,1)}, bf16[256,1280]{1,0:T(8,128)(2,1)}, u32[]{:S(2)}, u32[]{:S(2)}) collective-permute-start(bf16[256,1280]{1,0:T(8,128)(2,1)} %get-tuple-element.130), channel_id=1, source_target_pairs={{0,0},{4,8},{8,16},{12,24},{16,28},{20,20},{24,12},{28,4},{1,1},{5... | collective-permute-start | bytes 1966088 | tf_op jit(solution)/shard_map/ppermute | solution.py:592
  163.9 26.8 %collective-permute-start.14 = (bf16[4,160,1280]{2,1,0:T(8,128)(2,1)}, bf16[4,160,1280]{2,1,0:T(8,128)(2,1)}, u32[]{:S(2)}, u32[]{:S(2)}) collective-permute-start(bf16[4,160,1280]{2,1,0:T(8,128)(2,1)} %bitcast.91), channel_id=1, source_target_pairs={{0,4},{4,0},{8,12},{12,8},{16,20},{20,16},{24,28},{28,24},{1,5},{5... | collective-permute-start | bytes 4915208 | tf_op jit(solution)/shard_map/ppermute | solution.py:580
  164.1 188.2 %reduce-scatter.9.cloned.1.call-start = ((), (), s32[]{:S(2)}) async-start(), calls=%async_computation.10 | async-start | bytes 5734400 | tf_op jit(solution)/shard_map/reduce_scatter | solution.py:819
  197.7 3.3 collective-permute-start.15
  199.7 26.5 %collective-permute-start.16 = (bf16[512,1280]{1,0:T(8,128)(2,1)}, bf16[512,1280]{1,0:T(8,128)(2,1)}, u32[]{:S(2)}, u32[]{:S(2)}) collective-permute-start(bf16[512,1280]{1,0:T(8,128)(2,1)} %fusion.18), channel_id=1, source_target_pairs={{0,4},{4,0},{8,12},{12,8},{16,20},{20,16},{24,28},{28,24},{1,5},{5... | collective-permute-start | bytes 3932168 | tf_op jit(solution)/shard_map/ppermute | solution.py:580
  250.0 203.7 %reduce-scatter.11.cloned.1.call-start = ((), (), s32[]{:S(2)}) async-start(), calls=%async_computation.11 | async-start | bytes 5734400 | tf_op jit(solution)/shard_map/reduce_scatter | solution.py:819
  260.0 193.7 %reduce-scatter.13.cloned.1.call-start = ((), (), s32[]{:S(2)}) async-start(), calls=%async_computation.12 | async-start | bytes 5734400 | tf_op jit(solution)/shard_map/reduce_scatter | solution.py:819
  313.8 238.1 %reduce-scatter.15.cloned.1.call-start = ((), (), s32[]{:S(2)}) async-start(), calls=%async_computation.13 | async-start | bytes 3276800 | tf_op jit(solution)/shard_map/reduce_scatter | solution.py:649
  326.8 24.3 %collective-permute-start.20 = (bf16[256,1280]{1,0:T(8,128)(2,1)S(1)}, bf16[256,1280]{1,0:T(8,128)(2,1)S(1)}, u32[]{:S(2)}, u32[]{:S(2)}) collective-permute-start(bf16[256,1280]{1,0:T(8,128)(2,1)S(1)} %get-tuple-element.127), channel_id=1, source_target_pairs={{4,0},{12,4},{20,8},{28,12},{24,16},{16,20},{8,24},{0,28},{5,1},{1... | collective-permute-start | bytes 1966088 | tf_op jit(solution)/shard_map/ppermute | solution.py:606
  332.1 18.9 %collective-permute-start.19 = (bf16[256,1280]{1,0:T(8,128)(2,1)S(1)}, bf16[256,1280]{1,0:T(8,128)(2,1)S(1)}, u32[]{:S(2)}, u32[]{:S(2)}) collective-permute-start(bf16[256,1280]{1,0:T(8,128)(2,1)S(1)} %get-tuple-element.128), channel_id=1, source_target_pairs={{0,0},{8,4},{16,8},{24,12},{28,16},{20,20},{12,24},{4,28},{1,1},{9... | collective-permute-start | bytes 1966088 | tf_op jit(solution)/shard_map/ppermute | solution.py:606
  352.2 56.2 %collective-permute-start.21 = (bf16[320,1792]{1,0:T(8,128)(2,1)}, bf16[320,1792]{1,0:T(8,128)(2,1)S(1)}, u32[]{:S(2)}, u32[]{:S(2)}) collective-permute-start(bf16[320,1792]{1,0:T(8,128)(2,1)} %reduce-scatter.9.cloned.1.call-done.refs_5_), channel_id=1, source_target_pairs={{0,8},{4,12},{24,16},{28,20},{1,9},{5,13},{25,17},{29,21},{2,10},{... | collective-permute-start | bytes 3440648 | tf_op jit(solution)/shard_map/ppermute | solution.py:681
  422.5 4.9 collective-permute-start.26
  431.3 187.0 %reduce-scatter.17.cloned.1.call-start = ((), (), s32[]{:S(2)}) async-start(), calls=%async_computation.14 | async-start | bytes 4096000 | tf_op jit(solution)/shard_map/reduce_scatter | solution.py:819
  440.7 5.9 collective-permute-start.31
  449.1 169.2 %reduce-scatter.19.cloned.1.call-start = ((), (), s32[]{:S(2)}) async-start(), calls=%async_computation.15 | async-start | bytes 1126400
  451.9 15.0 %collective-permute-start.24 = (bf16[320,1792]{1,0:T(8,128)(2,1)}, bf16[320,1792]{1,0:T(8,128)(2,1)}, u32[]{:S(2)}, u32[]{:S(2)}) collective-permute-start(bf16[320,1792]{1,0:T(8,128)(2,1)} %add.142), channel_id=1, source_target_pairs={{8,16},{12,20},{16,8},{20,12},{9,17},{13,21},{17,9},{21,13},{10,18... | collective-permute-start | bytes 3440648 | tf_op jit(solution)/shard_map/ppermute | solution.py:681
  453.7 59.3 %collective-permute-start.22 = (bf16[320,1792]{1,0:T(8,128)(2,1)}, bf16[320,1792]{1,0:T(8,128)(2,1)S(1)}, u32[]{:S(2)}, u32[]{:S(2)}) collective-permute-start(bf16[320,1792]{1,0:T(8,128)(2,1)} %get-tuple-element.59), channel_id=1, source_target_pairs={{0,8},{4,12},{24,16},{28,20},{1,9},{5,13},{25,17},{29,21},{2,10},{... | collective-permute-start | bytes 3440648 | tf_op jit(solution)/shard_map/ppermute | solution.py:681
  464.3 73.0 %collective-permute-start.23 = (bf16[448,1280]{1,0:T(8,128)(2,1)}, bf16[448,1280]{1,0:T(8,128)(2,1)}, u32[]{:S(2)}, u32[]{:S(2)}) collective-permute-start(bf16[448,1280]{1,0:T(8,128)(2,1)} %get-tuple-element.60), channel_id=1, source_target_pairs={{0,8},{4,12},{24,16},{28,20},{1,9},{5,13},{25,17},{29,21},{2,10},{... | collective-permute-start | bytes 3440648 | tf_op jit(solution)/shard_map/ppermute | solution.py:681
  469.8 76.2 %collective-permute-start.25 = (bf16[320,1792]{1,0:T(8,128)(2,1)}, bf16[320,1792]{1,0:T(8,128)(2,1)}, u32[]{:S(2)}, u32[]{:S(2)}) collective-permute-start(bf16[320,1792]{1,0:T(8,128)(2,1)} %add.143), channel_id=1, source_target_pairs={{8,0},{12,4},{16,24},{20,28},{9,1},{13,5},{17,25},{21,29},{10,2},{... | collective-permute-start | bytes 3440648 | tf_op jit(solution)/shard_map/ppermute | solution.py:681
  514.4 33.0 %collective-permute-start.34 = (bf16[320,1792]{1,0:T(8,128)(2,1)}, bf16[320,1792]{1,0:T(8,128)(2,1)}, u32[]{:S(2)}, u32[]{:S(2)}) collective-permute-start(bf16[320,1792]{1,0:T(8,128)(2,1)} %add.149), channel_id=1, source_target_pairs={{8,16},{12,20},{16,8},{20,12},{9,17},{13,21},{17,9},{21,13},{10,18... | collective-permute-start | bytes 3440648 | tf_op jit(solution)/shard_map/ppermute | solution.py:681
  539.9 23.0 %collective-permute-start.37 = (bf16[448,1280]{1,0:T(8,128)(2,1)}, bf16[448,1280]{1,0:T(8,128)(2,1)}, u32[]{:S(2)}, u32[]{:S(2)}) collective-permute-start(bf16[448,1280]{1,0:T(8,128)(2,1)} %add.151), channel_id=1, source_target_pairs={{8,16},{12,20},{16,8},{20,12},{9,17},{13,21},{17,9},{21,13},{10,18... | collective-permute-start | bytes 3440648 | tf_op jit(solution)/shard_map/ppermute | solution.py:681
  547.4 19.7 %collective-permute-start.33 = (bf16[320,1792]{1,0:T(8,128)(2,1)S(1)}, bf16[320,1792]{1,0:T(8,128)(2,1)}, u32[]{:S(2)}, u32[]{:S(2)}) collective-permute-start(bf16[320,1792]{1,0:T(8,128)(2,1)S(1)} %broadcast_select_fusion.4.own_ref), channel_id=1, source_target_pairs={{0,4},{4,0},{8,12},{12,8},{16,20},{20,16},{24,28},{28,24},{1,5},{5... | collective-permute-start | bytes 3440648 | tf_op jit(solution)/shard_map/ppermute | solution.py:580
  550.5 30.9 %collective-permute-start.35 = (bf16[320,1792]{1,0:T(8,128)(2,1)}, bf16[320,1792]{1,0:T(8,128)(2,1)}, u32[]{:S(2)}, u32[]{:S(2)}) collective-permute-start(bf16[320,1792]{1,0:T(8,128)(2,1)} %add.150), channel_id=1, source_target_pairs={{8,0},{12,4},{16,24},{20,28},{9,1},{13,5},{17,25},{21,29},{10,2},{... | collective-permute-start | bytes 3440648 | tf_op jit(solution)/shard_map/ppermute | solution.py:681
  562.6 20.2 %collective-permute-start.29 = (bf16[4,176,640]{2,1,0:T(8,128)(2,1)S(1)}, bf16[4,176,640]{2,1,0:T(8,128)(2,1)S(1)}, u32[]{:S(2)}, u32[]{:S(2)}) collective-permute-start(bf16[4,176,640]{2,1,0:T(8,128)(2,1)S(1)} %pad_maximum_fusion.9), channel_id=1, source_target_pairs={{0,4},{4,0},{8,12},{12,8},{16,20},{20,16},{24,28},{28,24},{1,5},{5... | collective-permute-start | bytes 2703368 | tf_op jit(solution)/shard_map/ppermute | solution.py:580
  565.7 40.1 %collective-permute-start.38 = (bf16[448,1280]{1,0:T(8,128)(2,1)}, bf16[448,1280]{1,0:T(8,128)(2,1)}, u32[]{:S(2)}, u32[]{:S(2)}) collective-permute-start(bf16[448,1280]{1,0:T(8,128)(2,1)} %add.152), channel_id=1, source_target_pairs={{8,0},{12,4},{16,24},{20,28},{9,1},{13,5},{17,25},{21,29},{10,2},{... | collective-permute-start | bytes 3440648 | tf_op jit(solution)/shard_map/ppermute | solution.py:681
  582.7 37.4 %collective-permute-start.36 = (bf16[320,1792]{1,0:T(8,128)(2,1)S(1)}, bf16[320,1792]{1,0:T(8,128)(2,1)S(1)}, u32[]{:S(2)}, u32[]{:S(2)}) collective-permute-start(bf16[320,1792]{1,0:T(8,128)(2,1)S(1)} %broadcast_select_fusion.3.own_ref), channel_id=1, source_target_pairs={{0,4},{4,0},{8,12},{12,8},{16,20},{20,16},{24,28},{28,24},{1,5},{5... | collective-permute-start | bytes 3440648 | tf_op jit(solution)/shard_map/ppermute | solution.py:580
  584.0 105.9 %all-reduce.6.cloned.1.call-start = ((), (), s32[]{:S(2)}) async-start(), calls=%async_computation.16 | async-start | bytes 2088960 | tf_op jit(solution)/shard_map/psum | solution.py:678
  608.2 10.1 %collective-permute-start.39 = (bf16[448,1280]{1,0:T(8,128)(2,1)}, bf16[448,1280]{1,0:T(8,128)(2,1)}, u32[]{:S(2)}, u32[]{:S(2)}) collective-permute-start(bf16[448,1280]{1,0:T(8,128)(2,1)} %broadcast_select_fusion), channel_id=1, source_target_pairs={{0,4},{4,0},{8,12},{12,8},{16,20},{20,16},{24,28},{28,24},{1,5},{5... | collective-permute-start | bytes 3440648 | tf_op jit(solution)/shard_map/ppermute | solution.py:580
  611.8 78.2 %collective-permute-start.27 = (bf16[256,1280]{1,0:T(8,128)(2,1)}, bf16[256,1280]{1,0:T(8,128)(2,1)}, u32[]{:S(2)}, u32[]{:S(2)}) collective-permute-start(bf16[256,1280]{1,0:T(8,128)(2,1)} %get-tuple-element.125), channel_id=1, source_target_pairs={{0,0},{8,4},{16,8},{24,12},{28,16},{20,20},{12,24},{4,28},{1,1},{9... | collective-permute-start | bytes 1966088 | tf_op jit(solution)/shard_map/ppermute | solution.py:606
  618.3 71.7 %collective-permute-start.28 = (bf16[256,1280]{1,0:T(8,128)(2,1)S(1)}, bf16[256,1280]{1,0:T(8,128)(2,1)}, u32[]{:S(2)}, u32[]{:S(2)}) collective-permute-start(bf16[256,1280]{1,0:T(8,128)(2,1)S(1)} %get-tuple-element.126), channel_id=1, source_target_pairs={{4,0},{12,4},{20,8},{28,12},{24,16},{16,20},{8,24},{0,28},{5,1},{1... | collective-permute-start | bytes 1966088 | tf_op jit(solution)/shard_map/ppermute | solution.py:606
  692.4 6.9 collective-permute-start.32
  (98 other events, 751.8 us)
Sparse Core Ops, SparseCore 0:
  17.2 31.9 all-gather.4
  60.0 56.0 all-gather.6
  118.5 42.8 all-gather.8
  164.2 61.9 all-gather.10
  250.1 56.0 reduce-scatter.8
  309.7 55.9 reduce-scatter.10
  369.3 55.9 reduce-scatter.12
  431.5 82.2 reduce-scatter.14
  517.4 63.3 reduce-scatter.16
  584.2 29.1 reduce-scatter.18
  618.5 71.3 all-reduce.5

commit v3 on v2

--- a/solution.py
+++ b/solution.py
@@ -294,7 +294,7 @@
         compiler_params=pltpu.CompilerParams(vmem_limit_bytes=20 << 20),
         cost_estimate=takes(10 * count),
         name="attend",
-    )(info, *deps, q, pairs)
+    )(info, *deps, q, pltpu.with_memory_space_constraint(pairs, pltpu.HBM))
 
 
 def backward_kernel(
@@ -389,7 +389,7 @@
     head_block = pl.BlockSpec((rows, width), lambda g, info: (0, head))
     half_block = pl.BlockSpec((keys // 2, PAIR), lambda g, info: (0, head - span[0]))
     table = pl.BlockSpec((rows, PAIR), lambda g, info: (0, 0))
-    half_shape = jax.ShapeDtypeStruct((keys // 2, span[1] * PAIR), bf16)
+    half_shape = pltpu.HBM((keys // 2, span[1] * PAIR), bf16)
     return pl.pallas_call(
         ignoring(functools.partial(backward_kernel, keys // half), 1, len(deps)),
         grid_spec=pltpu.PrefetchScalarGridSpec(
@@ -416,12 +416,12 @@
                 pltpu.VMEM((2 * half, 2 * wide), bf16),
             ],
         ),
-        out_shape=[jax.ShapeDtypeStruct(q.shape, bf16), half_shape, half_shape],
+        out_shape=[pltpu.HBM(q.shape, bf16), half_shape, half_shape],
         input_output_aliases=aliases,
         compiler_params=pltpu.CompilerParams(vmem_limit_bytes=24 << 20),
         cost_estimate=takes(16),
         name="attend_back",
-    )(info, *deps, q, grad, attended, lse, pairs, cos, sin)
+    )(info, *deps, q, grad, attended, lse, pltpu.with_memory_space_constraint(pairs, pltpu.HBM), cos, sin)
 
 
 def outer_kernel(parts, core_ref, a_ref, b_ref, keep_ref, send_ref, at_sc):
@@ -619,13 +619,15 @@
     def gather_first(self, own):
         return (self.across(own, 1), self.across(own, 2)) if self.square else ()
 
-    def gather_last(self, own, arrived):
+    def gather_last(self, own, arrived, hold=None):
         if not self.square:
             return self.gather_all(own)
         rows = own.shape[0]
         half = rows // 32 * 16
         by_x, by_y = arrived
         top, bottom = self.across(by_x[:half], 2), self.across(by_y[half:], 1)
+        if hold is not None:
+            top, bottom = gate((top, bottom), hold)
         me = self.me
         spots = [me * rows, (me ^ 1) * rows, (me ^ 2) * rows, (me ^ 3) * rows, (me ^ 3) * rows + half]
         return place([own, by_x, by_y, top, bottom], spots, 4 * rows)
@@ -771,7 +773,7 @@
     normed = (x * scale_one * gain_first).astype(bf16)
     pairs = project(True, normed, full_pair, cos, sin)
     all_pairs = lax.all_gather(pairs, "ctx", axis=0, tiled=True)
-    (whole_query,) = gate((whole_query,), pairs)
+    (whole_query,) = gate((whole_query,), pairs, own_wide)
     full_query = beside(moves.both_cores(whole_query.reshape(fsdp, in_half, -1)))
     queries = project(False, normed, full_query, cos, sin)
     own_out = core_rows(core, out_weight, (queries,))
@@ -780,12 +782,12 @@
     full_down = moves.gather_all(own_down)
     if wide_arrived:
         wide_arrived = gate(wide_arrived, queries)
-    full_wide = moves.gather_last(own_wide, wide_arrived)
     late = copy_later(cotangent.reshape(block_length, model), (all_pairs, queries))
     cotangent_rows = moves.balance(late)
     ff_half = gate_weight.shape[1] // fsdp // 2
     ff_core = ff_half * fsdp
     grown = attend(0, 3, (), queries, all_pairs, info, (own_down, late))
+    full_wide = moves.gather_last(own_wide, wide_arrived, grown[1])
     (whole_out,) = gate((whole_out,), grown[1])
     out_cores = moves.both_cores(whole_out.reshape(fsdp, in_half, model))
     full_out = beside(out_cores)

time: 720 us -> 704 us (0.978)
  local copies, waits for them, and re-layouts: 76.3 us -> 47 us
  Pallas kernels: 143 us -> 154 us
    unnamed x197 -> x145, local copies, waits for them, and re-layouts: 63 us -> 32.8 us
    pallas_call x5, Pallas kernels: 62.5 us -> 72.1 us  [attend_back(): pl.pallas_call(ignoring(functools.partial(backward_kernel, keys // half),...]
  transfers between devices with their start and end apart: 51 -> 51, of which waited for: 16 -> 18; matrix products, arithmetic and copies ran while one was open for 21% -> 21% of each run, Pallas kernels for 20% -> 22%
where the time goes in v3:
time: 704 us; the launch traced here: 694 us
  waiting for transfers between devices  248 us (35%)
  Pallas kernels  154 us (22%)
  matrix products  94.4 us (13%)
  starting transfers between devices  73 us (10%)
  other arithmetic  61.1 us (9%)
  local copies, waits for them, and re-layouts  47 us (7%)
  between operations  16.2 us (2%)
    ppermute x9, waiting for transfers between devices, along(): lax.ppermute(value, 'ctx', [(2 * a + c, 2 * b + c) for a, b in pairs for...  94.9 us
    pallas_call x5, Pallas kernels, attend_back(): pl.pallas_call(ignoring(functools.partial(backward_kernel, keys // half),...  72.1 us
    psum x1, waiting for transfers between devices, over_line(): return lax.psum(part, 'ctx', axis_index_groups=groups)  62.2 us
    ppermute x8, waiting for transfers between devices, across(): return lax.ppermute(value, 'fsdp', [(i, i ^ bit) for i in range(self.fsdp)])  43 us
    pallas_call x2, Pallas kernels, attend(): pl.pallas_call(ignoring(functools.partial(forward_kernel, keys // half),...  40.7 us
    ppermute x9, starting transfers between devices, along(): lax.ppermute(value, 'ctx', [(2 * a + c, 2 * b + c) for a, b in pairs for...  38.2 us
    unnamed x145, local copies, waits for them, and re-layouts  32.8 us
    dot_general x3, matrix products, local(): lax.dot_general(a, b, first, preferred_element_type=f32).astype(bf16)  26.7 us
  transfers between devices with their start and end apart: 51, of which 18 were waited for; matrix products, arithmetic and copies ran while one was open for 21% of the time, Pallas kernels for 22%

profile of v3, /device:TPU:0, one launch (start us, length us, event | category | flops | bytes accessed | tf_op | source)
XLA Modules:
  0.0 693.6 jit_solution(10753918745378058731)
XLA Ops:
  10.8 3.0 collective-permute-start.3
  24.9 6.3 collective-permute-done.4.refs_3_
  34.8 16.1 %collective-permute-done.1 = bf16[256,1280]{1,0:T(8,128)(2,1)} collective-permute-done((bf16[256,1280]{1,0:T(8,128)(2,1)}, bf16[256,1280]{1,0:T(8,128)(2,1)}, u32[]{:S(2)}, u32[]{:S(2)}) %collective-permute-start.1) | collective-permute-done | bytes 655392 | tf_op jit(solution)/shard_map/ppermute | solution.py:592
  60.0 3.6 split_columns.1.refs_1_.refs_0_
  70.7 3.5 project.3.refs_1_.refs_3_.refs_0_.refs_5_.refs_6_.refs_4_
  79.5 36.4 %collective-permute-done.11.refs_2_ = bf16[320,3584]{1,0:T(8,128)(2,1)} collective-permute-done((bf16[320,3584]{1,0:T(8,128)(2,1)S(1)}, bf16[320,3584]{1,0:T(8,128)(2,1)}, u32[]{:S(2)}, u32[]{:S(2)}) %collective-permute-start.11) | collective-permute-done | bytes 2293792 | tf_op jit(solution)/shard_map/ppermute | solution.py:577
  132.0 24.0 %attend.2 = (bf16[512,1280]{1,0:T(8,128)(2,1)S(1)}, f32[5,4,512]{2,1,0:T(4,128)S(1)}) custom-call(s32[4]{0:T(128)S(1)} %pad_add_fusion.1.refs_0_, bf16[448,1280]{1,0:T(8,128)(2,1)S(1)} %copy-done.14, bf16[512,1280]{1,0:T(8,128)(2,1)S(1)} %copy-done.7, bf16[512,1280]{1,0:T(8,128)(2,1)S(1)} %copy-done.1, ...), custom_call_target="tpu_custom_call" | custom-call | flops 15572249600 | tf_op jit(solution)/shard_map/attend/pallas_call | solution.py:268
  163.7 4.0 place.3.refs_4_
  171.5 16.7 %attend.3 = (bf16[512,1280]{1,0:T(8,128)(2,1)S(1)}, f32[5,4,512]{2,1,0:T(4,128)S(1)}) custom-call(s32[4]{0:T(128)S(1)} %pad_add_fusion.1.refs_0_, bf16[512,1280]{1,0:T(8,128)(2,1)S(1)} %copy-done.31, f32[5,4,512]{2,1,0:T(4,128)S(1)} %copy-done.29, ...), custom_call_target="tpu_custom_call", output_to_operand_aliasing={{0}: (1, {}), {1}: (2, {})} | custom-call | flops 10381500416 | tf_op jit(solution)/shard_map/attend/pallas_call | solution.py:268
  191.4 3.4 multiply_reduce_fusion.2
  199.4 13.1 %fusion.20 = f32[1024,3584]{1,0:T(8,128)} fusion(bf16[1280,3584]{1,0:T(8,128)(2,1)S(1)} %place.3.refs_4_, bf16[512,1280]{1,0:T(8,128)(2,1)S(1)} %collective-permute-done.15, bf16[512,1280]{1,0:T(8,128)(2,1)S(1)} %multiply_convert_fusion.3), kind=kOutput, calls=%fused_computation.72 | convolution fusion | flops 9400483840 | bytes 26476544 | tf_op jit(solution)/shard_map/dot_general | solution.py:805
  212.5 11.4 %all-gather.11.cloned.1.call-done = bf16[1792,1280]{1,0:T(8,128)(2,1)} async-done(((bf16[448,1280]{1,0:T(8,128)(2,1)}), bf16[1792,1280]{1,0:T(8,128)(2,1)}) %all-gather.11.cloned.1.call-update) | async-done | bytes 4587536 | tf_op jit(solution)/shard_map/all_gather | solution.py:617
  223.9 15.1 %multiply_convert_fusion.1 = (bf16[1024,1792]{1,0:T(8,128)(2,1)}, bf16[1024,1792]{1,0:T(8,128)(2,1)S(1)}, bf16[1024,1792]{1,0:T(8,128)(2,1)}) fusion(f32[1024,3584]{1,0:T(8,128)} %fusion.20, bf16[1792,1280]{1,0:T(8,128)(2,1)} %all-gather.11.cloned.1.call-done, bf16[512,1280]{1,0:T(8,128)(2,1)} %collective-permute-done.16, bf16[512,1280]{1,0:T(8,128)(2,1)} %fusion.18), kind=kOutput, calls=%fused_computation.8 | convolution fusion | flops 4730388480 | bytes 32899072 | tf_op jit(solution)/shard_map/dot_general | solution.py:810
  240.9 6.7 convolution_convert_fusion.2.refs_1_
  247.6 10.0 %convolution_convert_fusion.1.refs_2_ = bf16[1280,1792]{1,0:T(8,128)(2,1)} fusion(bf16[1024,1792]{1,0:T(8,128)(2,1)} %get-tuple-element.114, bf16[512,1280]{1,0:T(8,128)(2,1)} %copy-done.62, bf16[512,1280]{1,0:T(8,128)(2,1)} %copy-done.52), kind=kOutput, calls=%fused_computation.1 | convolution fusion | flops 4705157120 | bytes 10878976 | tf_op jit(solution)/shard_map/dot_general | solution.py:815
  257.7 15.1 %fusion = f32[1024,1280]{1,0:T(8,128)S(1)} fusion(bf16[1280,3584]{1,0:T(8,128)(2,1)} %copy-done.6, bf16[1024,1792]{1,0:T(8,128)(2,1)} %get-tuple-element.114, bf16[1024,1792]{1,0:T(8,128)(2,1)} %copy-done.64), kind=kOutput, calls=%fused_computation.3 | convolution fusion | flops 9409921024 | bytes 21757952 | tf_op jit(solution)/shard_map/dot_general | solution.py:816
  273.0 3.0 collective-permute-done.17
  282.8 14.4 %attend_back.5 = (bf16[512,1280]{1,0:T(8,128)(2,1)}, bf16[2048,640]{1,0:T(8,128)(2,1)}, bf16[2048,640]{1,0:T(8,128)(2,1)}) custom-call(s32[4]{0:T(128)S(1)} %pad_add_fusion.1.refs_0_, bf16[1280,1792]{1,0:T(8,128)(2,1)S(1)} %bitcast.81, bf16[1280,1792]{1,0:T(8,128)(2,1)S(1)} %bitcast.79, bf16[512,1280]{1,0:T(8,128)(2,1)S(1)} %copy-done.1, ...), custom_call_target="tpu_custom_call" | custom-call | flops 8305200128 | tf_op jit(solution)/shard_map/attend_back/pallas_call | solution.py:393
  297.2 10.0 %convolution_convert_fusion.refs_4_ = bf16[1792,1280]{1,0:T(8,128)(2,1)} fusion(bf16[1024,1792]{1,0:T(8,128)(2,1)} %gate.10, bf16[512,1280]{1,0:T(8,128)(2,1)} %collective-permute-done.16, bf16[512,1280]{1,0:T(8,128)(2,1)} %fusion.18), kind=kOutput, calls=%fused_computation | convolution fusion | flops 4705157120 | bytes 10878976 | tf_op jit(solution)/shard_map/dot_general | solution.py:815
  307.3 8.3 %fusion.49.refs_4_ = f32[1024,1280]{1,0:T(8,128)S(1)} fusion(bf16[1024,1792]{1,0:T(8,128)(2,1)} %gate.10, bf16[1792,1280]{1,0:T(8,128)(2,1)} %all-gather.11.cloned.1.call-done), kind=kOutput, calls=%fused_computation.139 | convolution fusion | flops 4697620480 | bytes 13500416 | tf_op jit(solution)/shard_map/dot_general | solution.py:839
  315.9 3.0 collective-permute-done.18
  319.4 6.1 collective-permute-start.20
  326.2 14.7 %attend_back.6 = (bf16[512,1280]{1,0:T(8,128)(2,1)}, bf16[2048,640]{1,0:T(8,128)(2,1)}, bf16[2048,640]{1,0:T(8,128)(2,1)}) custom-call(s32[4]{0:T(128)S(1)} %pad_add_fusion.1.refs_0_, bf16[512,1280]{1,0:T(8,128)(2,1)} %get-tuple-element.50.refs_0_.refs_1_, ...), custom_call_target="tpu_custom_call", output_to_operand_aliasing={{0}: (1, {}), {1}: (2, {}), {2}: (3, {})} | custom-call | flops 8305200128 | tf_op jit(solution)/shard_map/attend_back/pallas_call | solution.py:393
  341.0 15.7 %collective-permute-start.21 = (bf16[320,1792]{1,0:T(8,128)(2,1)}, bf16[320,1792]{1,0:T(8,128)(2,1)S(1)}, u32[]{:S(2)}, u32[]{:S(2)}) collective-permute-start(bf16[320,1792]{1,0:T(8,128)(2,1)} %reduce-scatter.9.cloned.1.call-done.refs_5_), channel_id=1, source_target_pairs={{0,8},{4,12},{24,16},{28,20},{1,9},{5,13},{25,17},{29,21},{2,10},{... | collective-permute-start | bytes 3440648 | tf_op jit(solution)/shard_map/ppermute | solution.py:683
  363.0 14.4 %attend_back.7 = (bf16[512,1280]{1,0:T(8,128)(2,1)}, bf16[2048,640]{1,0:T(8,128)(2,1)}, bf16[2048,640]{1,0:T(8,128)(2,1)}) custom-call(s32[4]{0:T(128)S(1)} %pad_add_fusion.1.refs_0_, bf16[512,1280]{1,0:T(8,128)(2,1)} %get-tuple-element.53.refs_1_, ...), custom_call_target="tpu_custom_call", output_to_operand_aliasing={{0}: (1, {}), {1}: (2, {}), {2}: (3, {})} | custom-call | flops 8305200128 | tf_op jit(solution)/shard_map/attend_back/pallas_call | solution.py:393
  377.4 14.2 %attend_back.8 = (bf16[512,1280]{1,0:T(8,128)(2,1)}, bf16[2048,640]{1,0:T(8,128)(2,1)}, bf16[2048,640]{1,0:T(8,128)(2,1)}) custom-call(s32[4]{0:T(128)S(1)} %pad_add_fusion.1.refs_0_, bf16[512,1280]{1,0:T(8,128)(2,1)} %get-tuple-element.56.refs_1_, ...), custom_call_target="tpu_custom_call", output_to_operand_aliasing={{0}: (1, {}), {1}: (2, {}), {2}: (3, {})} | custom-call | flops 8305200128 | tf_op jit(solution)/shard_map/attend_back/pallas_call | solution.py:393
  391.6 14.4 %attend_back.9 = (bf16[512,1280]{1,0:T(8,128)(2,1)}, bf16[2048,640]{1,0:T(8,128)(2,1)}, bf16[2048,640]{1,0:T(8,128)(2,1)}) custom-call(s32[4]{0:T(128)S(1)} %pad_add_fusion.1.refs_0_, bf16[512,1280]{1,0:T(8,128)(2,1)} %get-tuple-element.59.refs_1_, ...), custom_call_target="tpu_custom_call", output_to_operand_aliasing={{0}: (1, {}), {1}: (2, {}), {2}: (3, {})} | custom-call | flops 8305200128 | tf_op jit(solution)/shard_map/attend_back/pallas_call | solution.py:393
  406.8 4.7 collective-permute-done.26
  411.5 4.0 add.144
  418.6 3.2 outer_rows.4
  421.8 3.2 outer_rows.5
  425.8 5.5 collective-permute-done.31
  438.4 10.5 %collective-permute-start.22 = (bf16[320,1792]{1,0:T(8,128)(2,1)}, bf16[320,1792]{1,0:T(8,128)(2,1)S(1)}, u32[]{:S(2)}, u32[]{:S(2)}) collective-permute-start(bf16[320,1792]{1,0:T(8,128)(2,1)} %get-tuple-element.63), channel_id=1, source_target_pairs={{0,8},{4,12},{24,16},{28,20},{1,9},{5,13},{25,17},{29,21},{2,10},{... | collective-permute-start | bytes 3440648 | tf_op jit(solution)/shard_map/ppermute | solution.py:683
  451.6 2.9 add.143
  455.9 42.5 %collective-permute-done.22.refs_1_ = bf16[320,1792]{1,0:T(8,128)(2,1)S(1)} collective-permute-done((bf16[320,1792]{1,0:T(8,128)(2,1)}, bf16[320,1792]{1,0:T(8,128)(2,1)S(1)}, u32[]{:S(2)}, u32[]{:S(2)}) %collective-permute-start.22) | collective-permute-done | bytes 1146912 | tf_op jit(solution)/shard_map/ppermute | solution.py:683
  501.8 4.8 fusion.50.refs_0_
  506.6 16.1 %collective-permute-done.23.refs_2_ = bf16[448,1280]{1,0:T(8,128)(2,1)} collective-permute-done((bf16[448,1280]{1,0:T(8,128)(2,1)}, bf16[448,1280]{1,0:T(8,128)(2,1)}, u32[]{:S(2)}, u32[]{:S(2)}) %collective-permute-start.23) | collective-permute-done | bytes 1146912 | tf_op jit(solution)/shard_map/ppermute | solution.py:683
  527.0 4.5 collective-permute-done.25.refs_3_
  533.0 2.9 add.150
  537.4 2.6 unrotate.1.refs_2_
  540.1 6.0 fusion.14
  548.3 2.9 add.152
  552.5 4.3 merge_columns.2
  556.8 10.1 %collective-permute-done.35 = bf16[320,1792]{1,0:T(8,128)(2,1)} collective-permute-done((bf16[320,1792]{1,0:T(8,128)(2,1)}, bf16[320,1792]{1,0:T(8,128)(2,1)}, u32[]{:S(2)}, u32[]{:S(2)}) %collective-permute-start.35) | collective-permute-done | bytes 1146912 | tf_op jit(solution)/shard_map/ppermute | solution.py:683
  569.6 21.8 %collective-permute-done.38 = bf16[448,1280]{1,0:T(8,128)(2,1)} collective-permute-done((bf16[448,1280]{1,0:T(8,128)(2,1)}, bf16[448,1280]{1,0:T(8,128)(2,1)}, u32[]{:S(2)}, u32[]{:S(2)}) %collective-permute-start.38) | collective-permute-done | bytes 1146912 | tf_op jit(solution)/shard_map/ppermute | solution.py:683
  597.3 6.5 collective-permute-start.27
  605.7 2.7 merge_columns.3
  610.9 62.2 %all-reduce.6.cloned.1.call-done = (bf16[176,640]{1,0:T(8,128)(2,1)}, bf16[160,2560]{1,0:T(8,128)(2,1)}) async-done(((bf16[176,640]{1,0:T(8,128)(2,1)}, bf16[160,2560]{1,0:T(8,128)(2,1)}), (bf16[176,640]{1,0:T(8,128)(2,1)}, bf16[160,2560]{1,0:T(8,128)(2,1)})) %all-reduce.6.cloned.1.call-update) | async-done | bytes 1044496 | tf_op jit(solution)/shard_map/psum | solution.py:680
  (339 shorter events, 146.8 us)
Async XLA Ops:
  7.2 56.3 %all-gather.5.cloned.1.call-start = ((), (), s32[]{:S(2)}) async-start(), calls=%async_computation.6 | async-start | bytes 2048000 | tf_op jit(solution)/shard_map/all_gather | solution.py:617
  10.8 12.2 %collective-permute-start.3 = (bf16[176,640]{1,0:T(8,128)(2,1)S(1)}, bf16[176,640]{1,0:T(8,128)(2,1)S(1)}, u32[]{:S(2)}, u32[]{:S(2)}) collective-permute-start(bf16[176,640]{1,0:T(8,128)(2,1)S(1)} %fusion.29.refs_0_), channel_id=1, source_target_pairs={{0,2},{1,3},{2,0},{3,1},{4,6},{5,7},{6,4},{7,5},{8,10},{9,11},{10,... | collective-permute-start | bytes 675848 | tf_op jit(solution)/shard_map/ppermute | solution.py:577
  13.8 10.1 %collective-permute-start.2 = (bf16[176,640]{1,0:T(8,128)(2,1)S(1)}, bf16[176,640]{1,0:T(8,128)(2,1)S(1)}, u32[]{:S(2)}, u32[]{:S(2)}) collective-permute-start(bf16[176,640]{1,0:T(8,128)(2,1)S(1)} %fusion.29.refs_0_), channel_id=1, source_target_pairs={{0,1},{1,0},{2,3},{3,2},{4,5},{5,4},{6,7},{7,6},{8,9},{9,8},{10,11... | collective-permute-start | bytes 675848 | tf_op jit(solution)/shard_map/ppermute | solution.py:577
  17.1 108.2 %all-gather.7.cloned.1.call-start = ((), (), s32[]{:S(2)}) async-start(), calls=%async_computation.7 | async-start | bytes 5898240 | tf_op jit(solution)/shard_map/all_gather | solution.py:775
  18.3 16.5 %collective-permute-start = (bf16[256,1280]{1,0:T(8,128)(2,1)}, bf16[256,1280]{1,0:T(8,128)(2,1)S(1)}, u32[]{:S(2)}, u32[]{:S(2)}) collective-permute-start(bf16[256,1280]{1,0:T(8,128)(2,1)} %get-tuple-element.135), channel_id=1, source_target_pairs={{0,0},{4,8},{8,16},{12,24},{16,28},{20,20},{24,12},{28,4},{1,1},{5... | collective-permute-start | bytes 1966088 | tf_op jit(solution)/shard_map/ppermute | solution.py:592
  20.0 30.8 %collective-permute-start.1 = (bf16[256,1280]{1,0:T(8,128)(2,1)}, bf16[256,1280]{1,0:T(8,128)(2,1)}, u32[]{:S(2)}, u32[]{:S(2)}) collective-permute-start(bf16[256,1280]{1,0:T(8,128)(2,1)} %get-tuple-element.136), channel_id=1, source_target_pairs={{0,4},{4,12},{8,20},{12,28},{16,24},{20,16},{24,8},{28,0},{1,5},{5... | collective-permute-start | bytes 1966088 | tf_op jit(solution)/shard_map/ppermute | solution.py:592
  23.0 8.2 %collective-permute-start.5 = (bf16[96,640]{1,0:T(8,128)(2,1)S(1)}, bf16[96,640]{1,0:T(8,128)(2,1)S(1)}, u32[]{:S(2)}, u32[]{:S(2)}) collective-permute-start(bf16[96,640]{1,0:T(8,128)(2,1)S(1)} %slice.161), channel_id=1, source_target_pairs={{0,1},{1,0},{2,3},{3,2},{4,5},{5,4},{6,7},{7,6},{8,9},{9,8},{10,11... | collective-permute-start | bytes 368648 | tf_op jit(solution)/shard_map/ppermute | solution.py:577
  23.9 7.3 %collective-permute-start.4 = (bf16[80,640]{1,0:T(8,128)(2,1)S(1)}, bf16[80,640]{1,0:T(8,128)(2,1)S(1)}, u32[]{:S(2)}, u32[]{:S(2)}) collective-permute-start(bf16[80,640]{1,0:T(8,128)(2,1)S(1)} %slice.160), channel_id=1, source_target_pairs={{0,2},{1,3},{2,0},{3,1},{4,6},{5,7},{6,4},{7,5},{8,10},{9,11},{10,... | collective-permute-start | bytes 307208 | tf_op jit(solution)/shard_map/ppermute | solution.py:577
  33.1 21.2 %collective-permute-start.6 = (bf16[4,160,640]{2,1,0:T(8,128)(2,1)S(1)}, bf16[4,160,640]{2,1,0:T(8,128)(2,1)}, u32[]{:S(2)}, u32[]{:S(2)}) collective-permute-start(bf16[4,160,640]{2,1,0:T(8,128)(2,1)S(1)} %slice.164), channel_id=1, source_target_pairs={{0,4},{4,0},{8,12},{12,8},{16,20},{20,16},{24,28},{28,24},{1,5},{5... | collective-permute-start | bytes 2457608 | tf_op jit(solution)/shard_map/ppermute | solution.py:580
  59.9 99.3 %all-gather.9.cloned.1.call-start = ((), (), s32[]{:S(2)}) async-start(), calls=%async_computation.8 | async-start | bytes 2048000 | tf_op jit(solution)/shard_map/all_gather | solution.py:617
  63.5 3.8 collective-permute-start.7
  65.2 50.8 %collective-permute-start.11 = (bf16[320,3584]{1,0:T(8,128)(2,1)S(1)}, bf16[320,3584]{1,0:T(8,128)(2,1)}, u32[]{:S(2)}, u32[]{:S(2)}) collective-permute-start(bf16[320,3584]{1,0:T(8,128)(2,1)S(1)} %copy-done.2), channel_id=1, source_target_pairs={{0,2},{1,3},{2,0},{3,1},{4,6},{5,7},{6,4},{7,5},{8,10},{9,11},{10,... | collective-permute-start | bytes 6881288 | tf_op jit(solution)/shard_map/ppermute | solution.py:577
  65.7 50.5 %collective-permute-start.10 = (bf16[320,3584]{1,0:T(8,128)(2,1)S(1)}, bf16[320,3584]{1,0:T(8,128)(2,1)}, u32[]{:S(2)}, u32[]{:S(2)}) collective-permute-start(bf16[320,3584]{1,0:T(8,128)(2,1)S(1)} %copy-done.2), channel_id=1, source_target_pairs={{0,1},{1,0},{2,3},{3,2},{4,5},{5,4},{6,7},{7,6},{8,9},{9,8},{10,11... | collective-permute-start | bytes 6881288 | tf_op jit(solution)/shard_map/ppermute | solution.py:577
  78.7 145.1 %all-gather.11.cloned.1.call-start = ((), (), s32[]{:S(2)}) async-start(), calls=%async_computation.9 | async-start | bytes 5734400 | tf_op jit(solution)/shard_map/all_gather | solution.py:617
  120.9 41.2 %collective-permute-start.13 = (bf16[160,3584]{1,0:T(8,128)(2,1)}, bf16[160,3584]{1,0:T(8,128)(2,1)}, u32[]{:S(2)}, u32[]{:S(2)}) collective-permute-start(bf16[160,3584]{1,0:T(8,128)(2,1)} %slice.134), channel_id=1, source_target_pairs={{0,1},{1,0},{2,3},{3,2},{4,5},{5,4},{6,7},{7,6},{8,9},{9,8},{10,11... | collective-permute-start | bytes 3440648 | tf_op jit(solution)/shard_map/ppermute | solution.py:577
  121.4 40.6 %collective-permute-start.12 = (bf16[160,3584]{1,0:T(8,128)(2,1)}, bf16[160,3584]{1,0:T(8,128)(2,1)}, u32[]{:S(2)}, u32[]{:S(2)}) collective-permute-start(bf16[160,3584]{1,0:T(8,128)(2,1)} %slice.133), channel_id=1, source_target_pairs={{0,2},{1,3},{2,0},{3,1},{4,6},{5,7},{6,4},{7,5},{8,10},{9,11},{10,... | collective-permute-start | bytes 3440648 | tf_op jit(solution)/shard_map/ppermute | solution.py:577
  130.3 39.2 %collective-permute-start.9 = (bf16[256,1280]{1,0:T(8,128)(2,1)}, bf16[256,1280]{1,0:T(8,128)(2,1)}, u32[]{:S(2)}, u32[]{:S(2)}) collective-permute-start(bf16[256,1280]{1,0:T(8,128)(2,1)} %get-tuple-element.133), channel_id=1, source_target_pairs={{0,4},{4,12},{8,20},{12,28},{16,24},{20,16},{24,8},{28,0},{1,5},{5... | collective-permute-start | bytes 1966088 | tf_op jit(solution)/shard_map/ppermute | solution.py:592
  130.3 37.5 %collective-permute-start.8 = (bf16[256,1280]{1,0:T(8,128)(2,1)S(1)}, bf16[256,1280]{1,0:T(8,128)(2,1)}, u32[]{:S(2)}, u32[]{:S(2)}) collective-permute-start(bf16[256,1280]{1,0:T(8,128)(2,1)S(1)} %get-tuple-element.134), channel_id=1, source_target_pairs={{0,0},{4,8},{8,16},{12,24},{16,28},{20,20},{24,12},{28,4},{1,1},{5... | collective-permute-start | bytes 1966088 | tf_op jit(solution)/shard_map/ppermute | solution.py:592
  159.2 29.0 %collective-permute-start.14 = (bf16[4,160,1280]{2,1,0:T(8,128)(2,1)}, bf16[4,160,1280]{2,1,0:T(8,128)(2,1)}, u32[]{:S(2)}, u32[]{:S(2)}) collective-permute-start(bf16[4,160,1280]{2,1,0:T(8,128)(2,1)} %bitcast.91), channel_id=1, source_target_pairs={{0,4},{4,0},{8,12},{12,8},{16,20},{20,16},{24,28},{28,24},{1,5},{5... | collective-permute-start | bytes 4915208 | tf_op jit(solution)/shard_map/ppermute | solution.py:580
  162.0 179.0 %reduce-scatter.9.cloned.1.call-start = ((), (), s32[]{:S(2)}) async-start(), calls=%async_computation.10 | async-start | bytes 5734400 | tf_op jit(solution)/shard_map/reduce_scatter | solution.py:821
  195.2 3.1 collective-permute-start.15
  197.1 26.8 %collective-permute-start.16 = (bf16[512,1280]{1,0:T(8,128)(2,1)}, bf16[512,1280]{1,0:T(8,128)(2,1)}, u32[]{:S(2)}, u32[]{:S(2)}) collective-permute-start(bf16[512,1280]{1,0:T(8,128)(2,1)} %fusion.18), channel_id=1, source_target_pairs={{0,4},{4,0},{8,12},{12,8},{16,20},{20,16},{24,28},{28,24},{1,5},{5... | collective-permute-start | bytes 3932168 | tf_op jit(solution)/shard_map/ppermute | solution.py:580
  247.6 190.8 %reduce-scatter.11.cloned.1.call-start = ((), (), s32[]{:S(2)}) async-start(), calls=%async_computation.11 | async-start | bytes 5734400 | tf_op jit(solution)/shard_map/reduce_scatter | solution.py:821
  257.6 180.8 %reduce-scatter.13.cloned.1.call-start = ((), (), s32[]{:S(2)}) async-start(), calls=%async_computation.12 | async-start | bytes 5734400 | tf_op jit(solution)/shard_map/reduce_scatter | solution.py:821
  307.2 230.2 %reduce-scatter.15.cloned.1.call-start = ((), (), s32[]{:S(2)}) async-start(), calls=%async_computation.13 | async-start | bytes 3276800 | tf_op jit(solution)/shard_map/reduce_scatter | solution.py:651
  319.4 21.5 %collective-permute-start.20 = (bf16[256,1280]{1,0:T(8,128)(2,1)S(1)}, bf16[256,1280]{1,0:T(8,128)(2,1)S(1)}, u32[]{:S(2)}, u32[]{:S(2)}) collective-permute-start(bf16[256,1280]{1,0:T(8,128)(2,1)S(1)} %get-tuple-element.131), channel_id=1, source_target_pairs={{4,0},{12,4},{20,8},{28,12},{24,16},{16,20},{8,24},{0,28},{5,1},{1... | collective-permute-start | bytes 1966088 | tf_op jit(solution)/shard_map/ppermute | solution.py:606
  325.5 15.4 %collective-permute-start.19 = (bf16[256,1280]{1,0:T(8,128)(2,1)S(1)}, bf16[256,1280]{1,0:T(8,128)(2,1)S(1)}, u32[]{:S(2)}, u32[]{:S(2)}) collective-permute-start(bf16[256,1280]{1,0:T(8,128)(2,1)S(1)} %get-tuple-element.132), channel_id=1, source_target_pairs={{0,0},{8,4},{16,8},{24,12},{28,16},{20,20},{12,24},{4,28},{1,1},{9... | collective-permute-start | bytes 1966088 | tf_op jit(solution)/shard_map/ppermute | solution.py:606
  341.0 50.6 %collective-permute-start.21 = (bf16[320,1792]{1,0:T(8,128)(2,1)}, bf16[320,1792]{1,0:T(8,128)(2,1)S(1)}, u32[]{:S(2)}, u32[]{:S(2)}) collective-permute-start(bf16[320,1792]{1,0:T(8,128)(2,1)} %reduce-scatter.9.cloned.1.call-done.refs_5_), channel_id=1, source_target_pairs={{0,8},{4,12},{24,16},{28,20},{1,9},{5,13},{25,17},{29,21},{2,10},{... | collective-permute-start | bytes 3440648 | tf_op jit(solution)/shard_map/ppermute | solution.py:683
  406.0 5.5 collective-permute-start.26
  415.6 188.3 %reduce-scatter.17.cloned.1.call-start = ((), (), s32[]{:S(2)}) async-start(), calls=%async_computation.14 | async-start | bytes 4096000 | tf_op jit(solution)/shard_map/reduce_scatter | solution.py:821
  425.3 6.0 collective-permute-start.31
  433.8 170.1 %reduce-scatter.19.cloned.1.call-start = ((), (), s32[]{:S(2)}) async-start(), calls=%async_computation.15 | async-start | bytes 1126400
  436.7 14.9 %collective-permute-start.24 = (bf16[320,1792]{1,0:T(8,128)(2,1)}, bf16[320,1792]{1,0:T(8,128)(2,1)}, u32[]{:S(2)}, u32[]{:S(2)}) collective-permute-start(bf16[320,1792]{1,0:T(8,128)(2,1)} %add.142), channel_id=1, source_target_pairs={{8,16},{12,20},{16,8},{20,12},{9,17},{13,21},{17,9},{21,13},{10,18... | collective-permute-start | bytes 3440648 | tf_op jit(solution)/shard_map/ppermute | solution.py:683
  438.4 59.9 %collective-permute-start.22 = (bf16[320,1792]{1,0:T(8,128)(2,1)}, bf16[320,1792]{1,0:T(8,128)(2,1)S(1)}, u32[]{:S(2)}, u32[]{:S(2)}) collective-permute-start(bf16[320,1792]{1,0:T(8,128)(2,1)} %get-tuple-element.63), channel_id=1, source_target_pairs={{0,8},{4,12},{24,16},{28,20},{1,9},{5,13},{25,17},{29,21},{2,10},{... | collective-permute-start | bytes 3440648 | tf_op jit(solution)/shard_map/ppermute | solution.py:683
  449.0 73.7 %collective-permute-start.23 = (bf16[448,1280]{1,0:T(8,128)(2,1)}, bf16[448,1280]{1,0:T(8,128)(2,1)}, u32[]{:S(2)}, u32[]{:S(2)}) collective-permute-start(bf16[448,1280]{1,0:T(8,128)(2,1)} %get-tuple-element.64), channel_id=1, source_target_pairs={{0,8},{4,12},{24,16},{28,20},{1,9},{5,13},{25,17},{29,21},{2,10},{... | collective-permute-start | bytes 3440648 | tf_op jit(solution)/shard_map/ppermute | solution.py:683
  454.6 76.9 %collective-permute-start.25 = (bf16[320,1792]{1,0:T(8,128)(2,1)}, bf16[320,1792]{1,0:T(8,128)(2,1)}, u32[]{:S(2)}, u32[]{:S(2)}) collective-permute-start(bf16[320,1792]{1,0:T(8,128)(2,1)} %add.143), channel_id=1, source_target_pairs={{8,0},{12,4},{16,24},{20,28},{9,1},{13,5},{17,25},{21,29},{10,2},{... | collective-permute-start | bytes 3440648 | tf_op jit(solution)/shard_map/ppermute | solution.py:683
  499.8 33.3 %collective-permute-start.34 = (bf16[320,1792]{1,0:T(8,128)(2,1)}, bf16[320,1792]{1,0:T(8,128)(2,1)}, u32[]{:S(2)}, u32[]{:S(2)}) collective-permute-start(bf16[320,1792]{1,0:T(8,128)(2,1)} %add.149), channel_id=1, source_target_pairs={{8,16},{12,20},{16,8},{20,12},{9,17},{13,21},{17,9},{21,13},{10,18... | collective-permute-start | bytes 3440648 | tf_op jit(solution)/shard_map/ppermute | solution.py:683
  525.3 23.1 %collective-permute-start.37 = (bf16[448,1280]{1,0:T(8,128)(2,1)}, bf16[448,1280]{1,0:T(8,128)(2,1)}, u32[]{:S(2)}, u32[]{:S(2)}) collective-permute-start(bf16[448,1280]{1,0:T(8,128)(2,1)} %add.151), channel_id=1, source_target_pairs={{8,16},{12,20},{16,8},{20,12},{9,17},{13,21},{17,9},{21,13},{10,18... | collective-permute-start | bytes 3440648 | tf_op jit(solution)/shard_map/ppermute | solution.py:683
  533.0 19.5 %collective-permute-start.33 = (bf16[320,1792]{1,0:T(8,128)(2,1)S(1)}, bf16[320,1792]{1,0:T(8,128)(2,1)}, u32[]{:S(2)}, u32[]{:S(2)}) collective-permute-start(bf16[320,1792]{1,0:T(8,128)(2,1)S(1)} %broadcast_select_fusion.4.own_ref), channel_id=1, source_target_pairs={{0,4},{4,0},{8,12},{12,8},{16,20},{20,16},{24,28},{28,24},{1,5},{5... | collective-permute-start | bytes 3440648 | tf_op jit(solution)/shard_map/ppermute | solution.py:580
  536.0 30.9 %collective-permute-start.35 = (bf16[320,1792]{1,0:T(8,128)(2,1)}, bf16[320,1792]{1,0:T(8,128)(2,1)}, u32[]{:S(2)}, u32[]{:S(2)}) collective-permute-start(bf16[320,1792]{1,0:T(8,128)(2,1)} %add.150), channel_id=1, source_target_pairs={{8,0},{12,4},{16,24},{20,28},{9,1},{13,5},{17,25},{21,29},{10,2},{... | collective-permute-start | bytes 3440648 | tf_op jit(solution)/shard_map/ppermute | solution.py:683
  547.9 20.5 %collective-permute-start.29 = (bf16[4,176,640]{2,1,0:T(8,128)(2,1)S(1)}, bf16[4,176,640]{2,1,0:T(8,128)(2,1)S(1)}, u32[]{:S(2)}, u32[]{:S(2)}) collective-permute-start(bf16[4,176,640]{2,1,0:T(8,128)(2,1)S(1)} %pad_maximum_fusion.9), channel_id=1, source_target_pairs={{0,4},{4,0},{8,12},{12,8},{16,20},{20,16},{24,28},{28,24},{1,5},{5... | collective-permute-start | bytes 2703368 | tf_op jit(solution)/shard_map/ppermute | solution.py:580
  551.2 40.1 %collective-permute-start.38 = (bf16[448,1280]{1,0:T(8,128)(2,1)}, bf16[448,1280]{1,0:T(8,128)(2,1)}, u32[]{:S(2)}, u32[]{:S(2)}) collective-permute-start(bf16[448,1280]{1,0:T(8,128)(2,1)} %add.152), channel_id=1, source_target_pairs={{8,0},{12,4},{16,24},{20,28},{9,1},{13,5},{17,25},{21,29},{10,2},{... | collective-permute-start | bytes 3440648 | tf_op jit(solution)/shard_map/ppermute | solution.py:683
  568.3 37.4 %collective-permute-start.36 = (bf16[320,1792]{1,0:T(8,128)(2,1)S(1)}, bf16[320,1792]{1,0:T(8,128)(2,1)S(1)}, u32[]{:S(2)}, u32[]{:S(2)}) collective-permute-start(bf16[320,1792]{1,0:T(8,128)(2,1)S(1)} %broadcast_select_fusion.3.own_ref), channel_id=1, source_target_pairs={{0,4},{4,0},{8,12},{12,8},{16,20},{20,16},{24,28},{28,24},{1,5},{5... | collective-permute-start | bytes 3440648 | tf_op jit(solution)/shard_map/ppermute | solution.py:580
  569.5 103.5 %all-reduce.6.cloned.1.call-start = ((), (), s32[]{:S(2)}) async-start(), calls=%async_computation.16 | async-start | bytes 2088960 | tf_op jit(solution)/shard_map/psum | solution.py:680
  593.7 10.2 %collective-permute-start.39 = (bf16[448,1280]{1,0:T(8,128)(2,1)}, bf16[448,1280]{1,0:T(8,128)(2,1)}, u32[]{:S(2)}, u32[]{:S(2)}) collective-permute-start(bf16[448,1280]{1,0:T(8,128)(2,1)} %broadcast_select_fusion), channel_id=1, source_target_pairs={{0,4},{4,0},{8,12},{12,8},{16,20},{20,16},{24,28},{28,24},{1,5},{5... | collective-permute-start | bytes 3440648 | tf_op jit(solution)/shard_map/ppermute | solution.py:580
  597.3 75.8 %collective-permute-start.27 = (bf16[256,1280]{1,0:T(8,128)(2,1)}, bf16[256,1280]{1,0:T(8,128)(2,1)}, u32[]{:S(2)}, u32[]{:S(2)}) collective-permute-start(bf16[256,1280]{1,0:T(8,128)(2,1)} %get-tuple-element.129), channel_id=1, source_target_pairs={{0,0},{8,4},{16,8},{24,12},{28,16},{20,20},{12,24},{4,28},{1,1},{9... | collective-permute-start | bytes 1966088 | tf_op jit(solution)/shard_map/ppermute | solution.py:606
  603.8 69.3 %collective-permute-start.28 = (bf16[256,1280]{1,0:T(8,128)(2,1)S(1)}, bf16[256,1280]{1,0:T(8,128)(2,1)}, u32[]{:S(2)}, u32[]{:S(2)}) collective-permute-start(bf16[256,1280]{1,0:T(8,128)(2,1)S(1)} %get-tuple-element.130), channel_id=1, source_target_pairs={{4,0},{12,4},{20,8},{28,12},{24,16},{16,20},{8,24},{0,28},{5,1},{1... | collective-permute-start | bytes 1966088 | tf_op jit(solution)/shard_map/ppermute | solution.py:606
  675.6 6.9 collective-permute-start.32
  (72 other events, 665.4 us)
Sparse Core Ops, SparseCore 0:
  17.2 31.9 all-gather.4
  60.0 56.0 all-gather.6
  118.5 40.6 all-gather.8
  162.1 61.7 all-gather.10
  247.7 56.0 reduce-scatter.8
  307.3 55.9 reduce-scatter.10
  366.9 55.9 reduce-scatter.12
  425.2 74.7 reduce-scatter.14
  503.6 54.3 reduce-scatter.16
  569.6 29.9 reduce-scatter.18
  604.0 69.0 all-reduce.5

commit v4 on v3

--- a/solution.py
+++ b/solution.py
@@ -786,13 +786,13 @@
     cotangent_rows = moves.balance(late)
     ff_half = gate_weight.shape[1] // fsdp // 2
     ff_core = ff_half * fsdp
-    grown = attend(0, 3, (), queries, all_pairs, info, (own_down, late))
+    grown = attend(0, 3, (), queries, all_pairs, info, (late,))
     full_wide = moves.gather_last(own_wide, wide_arrived, grown[1])
     (whole_out,) = gate((whole_out,), grown[1])
     out_cores = moves.both_cores(whole_out.reshape(fsdp, in_half, model))
     full_out = beside(out_cores)
     attended, log_total = attend(
-        3, 2, grown, queries, all_pairs, info, (cotangent_rows, full_wide)
+        3, 2, grown, queries, all_pairs, info, (cotangent_rows, full_wide, own_down)
     )
     hidden = x + jnp.dot(attended, full_out, preferred_element_type=f32)
     scale_two = rms_scale(hidden)

time: 704 us -> 708 us (level)
  Pallas kernels: 154 us -> 178 us
  waiting for transfers between devices: 248 us -> 234 us
  starting transfers between devices: 73 us -> 63.3 us
    pallas_call x5, Pallas kernels: 72.1 us -> 87.1 us  [attend_back(): pl.pallas_call(ignoring(functools.partial(backward_kernel, keys // half),...]
    all_gather x3, waiting for transfers between devices: 13 us -> 0.01 us  [gather_all(): return lax.all_gather(own, 'fsdp', axis=0, tiled=True)]
    ppermute x9, starting transfers between devices: 38.2 us -> 26.1 us  [along(): lax.ppermute(value, 'ctx', [(2 * a + c, 2 * b + c) for a, b in pairs for...]
    pallas_call x2, Pallas kernels: 40.7 us -> 50.1 us  [attend(): pl.pallas_call(ignoring(functools.partial(forward_kernel, keys // half),...]
    unnamed x145 -> x149, local copies, waits for them, and re-layouts: 32.8 us -> 35 us
  transfers between devices with their start and end apart: 51 -> 51, of which waited for: 18 -> 16; matrix products, arithmetic and copies ran while one was open for 21% -> 21% of each run, Pallas kernels for 22% -> 26%
where the time goes in v4:
time: 708 us; the launch traced here: 698 us
  waiting for transfers between devices  234 us (33%)
  Pallas kernels  178 us (25%)
  matrix products  94.4 us (13%)
  starting transfers between devices  63.3 us (9%)
  other arithmetic  61.3 us (9%)
  local copies, waits for them, and re-layouts  50.7 us (7%)
  between operations  16.2 us (2%)
    ppermute x9, waiting for transfers between devices, along(): lax.ppermute(value, 'ctx', [(2 * a + c, 2 * b + c) for a, b in pairs for...  93.4 us
    pallas_call x5, Pallas kernels, attend_back(): pl.pallas_call(ignoring(functools.partial(backward_kernel, keys // half),...  87.1 us
    psum x1, waiting for transfers between devices, over_line(): return lax.psum(part, 'ctx', axis_index_groups=groups)  63.8 us
    pallas_call x2, Pallas kernels, attend(): pl.pallas_call(ignoring(functools.partial(forward_kernel, keys // half),...  50.1 us
    ppermute x8, waiting for transfers between devices, across(): return lax.ppermute(value, 'fsdp', [(i, i ^ bit) for i in range(self.fsdp)])  42.8 us
    unnamed x149, local copies, waits for them, and re-layouts  35 us
    dot_general x3, matrix products, local(): lax.dot_general(a, b, first, preferred_element_type=f32).astype(bf16)  26.7 us
    ppermute x9, starting transfers between devices, along(): lax.ppermute(value, 'ctx', [(2 * a + c, 2 * b + c) for a, b in pairs for...  26.1 us
  transfers between devices with their start and end apart: 51, of which 16 were waited for; matrix products, arithmetic and copies ran while one was open for 21% of the time, Pallas kernels for 26%

profile of v4, /device:TPU:0, one launch (start us, length us, event | category | flops | bytes accessed | tf_op | source)
XLA Modules:
  0.0 698.3 jit_solution(9797784795028230090)
XLA Ops:
  10.8 3.0 collective-permute-start.3
  24.9 6.3 collective-permute-done.4.refs_3_
  34.8 16.1 %collective-permute-done.1 = bf16[256,1280]{1,0:T(8,128)(2,1)} collective-permute-done((bf16[256,1280]{1,0:T(8,128)(2,1)}, bf16[256,1280]{1,0:T(8,128)(2,1)}, u32[]{:S(2)}, u32[]{:S(2)}) %collective-permute-start.1) | collective-permute-done | bytes 655392 | tf_op jit(solution)/shard_map/ppermute | solution.py:592
  60.0 3.6 split_columns.1.refs_1_.refs_0_
  70.7 3.5 project.3.refs_1_.refs_2_.refs_0_.refs_6_.refs_3_.refs_5_.refs_4_
  79.7 36.2 %collective-permute-done.11.refs_2_ = bf16[320,3584]{1,0:T(8,128)(2,1)} collective-permute-done((bf16[320,3584]{1,0:T(8,128)(2,1)S(1)}, bf16[320,3584]{1,0:T(8,128)(2,1)}, u32[]{:S(2)}, u32[]{:S(2)}) %collective-permute-start.11) | collective-permute-done | bytes 2293792 | tf_op jit(solution)/shard_map/ppermute | solution.py:577
  128.1 6.7 collective-permute-start.8
  134.8 29.7 %attend.2 = (bf16[512,1280]{1,0:T(8,128)(2,1)S(1)}, f32[5,4,512]{2,1,0:T(4,128)S(1)}) custom-call(s32[4]{0:T(128)S(1)} %pad_add_fusion.1.refs_0_, bf16[512,1280]{1,0:T(8,128)(2,1)S(1)} %copy-done.7, bf16[512,1280]{1,0:T(8,128)(2,1)S(1)} %copy-done.1, bf16[4096,640]{1,0:T(8,128)(2,1)} %all-gather.5.cloned.1.call-done.refs_0_.refs_3_.refs_7_.refs_9_.refs_10_.refs_8_), custom_call_target="tpu_custom_call" | custom-call | flops 15572249600 | tf_op jit(solution)/shard_map/attend/pallas_call | solution.py:268
  172.5 4.0 place.3.refs_4_
  178.4 3.1 constant_dynamic-update-slice_fusion.refs_3_
  181.6 20.4 %attend.3 = (bf16[512,1280]{1,0:T(8,128)(2,1)S(1)}, f32[5,4,512]{2,1,0:T(4,128)S(1)}) custom-call(s32[4]{0:T(128)S(1)} %pad_add_fusion.1.refs_0_, bf16[512,1280]{1,0:T(8,128)(2,1)S(1)} %copy-done.33, f32[5,4,512]{2,1,0:T(4,128)S(1)} %copy-done.31, ...), custom_call_target="tpu_custom_call", output_to_operand_aliasing={{0}: (1, {}), {1}: (2, {})} | custom-call | flops 10381500416 | tf_op jit(solution)/shard_map/attend/pallas_call | solution.py:268
  205.2 3.4 multiply_reduce_fusion.2
  213.5 13.1 %fusion.20 = f32[1024,3584]{1,0:T(8,128)} fusion(bf16[1280,3584]{1,0:T(8,128)(2,1)S(1)} %place.3.refs_4_, bf16[512,1280]{1,0:T(8,128)(2,1)S(1)} %collective-permute-done.15, bf16[512,1280]{1,0:T(8,128)(2,1)S(1)} %multiply_convert_fusion.3), kind=kOutput, calls=%fused_computation.72 | convolution fusion | flops 9400483840 | bytes 26476544 | tf_op jit(solution)/shard_map/dot_general | solution.py:805
  226.6 15.1 %multiply_convert_fusion.1 = (bf16[1024,1792]{1,0:T(8,128)(2,1)}, bf16[1024,1792]{1,0:T(8,128)(2,1)S(1)}, bf16[1024,1792]{1,0:T(8,128)(2,1)}) fusion(f32[1024,3584]{1,0:T(8,128)} %fusion.20, bf16[1792,1280]{1,0:T(8,128)(2,1)} %all-gather.11.cloned.1.call-done, bf16[512,1280]{1,0:T(8,128)(2,1)} %collective-permute-done.16, bf16[512,1280]{1,0:T(8,128)(2,1)} %fusion.18), kind=kOutput, calls=%fused_computation.8 | convolution fusion | flops 4730388480 | bytes 32899072 | tf_op jit(solution)/shard_map/dot_general | solution.py:810
  243.6 6.7 convolution_convert_fusion.2.refs_1_
  250.4 10.0 %convolution_convert_fusion.1.refs_2_ = bf16[1280,1792]{1,0:T(8,128)(2,1)} fusion(bf16[1024,1792]{1,0:T(8,128)(2,1)} %get-tuple-element.114, bf16[512,1280]{1,0:T(8,128)(2,1)} %copy-done.64, bf16[512,1280]{1,0:T(8,128)(2,1)} %copy-done.54), kind=kOutput, calls=%fused_computation.1 | convolution fusion | flops 4705157120 | bytes 10878976 | tf_op jit(solution)/shard_map/dot_general | solution.py:815
  260.4 15.1 %fusion = f32[1024,1280]{1,0:T(8,128)S(1)} fusion(bf16[1280,3584]{1,0:T(8,128)(2,1)} %copy-done.6, bf16[1024,1792]{1,0:T(8,128)(2,1)} %get-tuple-element.114, bf16[1024,1792]{1,0:T(8,128)(2,1)} %copy-done.66), kind=kOutput, calls=%fused_computation.3 | convolution fusion | flops 9409921024 | bytes 21757952 | tf_op jit(solution)/shard_map/dot_general | solution.py:816
  276.1 2.7 collective-permute-done.17
  285.6 17.4 %attend_back.5 = (bf16[512,1280]{1,0:T(8,128)(2,1)}, bf16[2048,640]{1,0:T(8,128)(2,1)}, bf16[2048,640]{1,0:T(8,128)(2,1)}) custom-call(s32[4]{0:T(128)S(1)} %pad_add_fusion.1.refs_0_, bf16[1280,1792]{1,0:T(8,128)(2,1)S(1)} %bitcast.81, bf16[1280,1792]{1,0:T(8,128)(2,1)S(1)} %bitcast.79, bf16[512,1280]{1,0:T(8,128)(2,1)S(1)} %copy-done.1, ...), custom_call_target="tpu_custom_call" | custom-call | flops 8305200128 | tf_op jit(solution)/shard_map/attend_back/pallas_call | solution.py:393
  302.9 10.0 %convolution_convert_fusion.refs_4_ = bf16[1792,1280]{1,0:T(8,128)(2,1)} fusion(bf16[1024,1792]{1,0:T(8,128)(2,1)} %gate.10, bf16[512,1280]{1,0:T(8,128)(2,1)} %collective-permute-done.16, bf16[512,1280]{1,0:T(8,128)(2,1)} %fusion.18), kind=kOutput, calls=%fused_computation | convolution fusion | flops 4705157120 | bytes 10878976 | tf_op jit(solution)/shard_map/dot_general | solution.py:815
  313.0 8.3 %fusion.49.refs_4_ = f32[1024,1280]{1,0:T(8,128)S(1)} fusion(bf16[1024,1792]{1,0:T(8,128)(2,1)} %gate.10, bf16[1792,1280]{1,0:T(8,128)(2,1)} %all-gather.11.cloned.1.call-done), kind=kOutput, calls=%fused_computation.139 | convolution fusion | flops 4697620480 | bytes 13500416 | tf_op jit(solution)/shard_map/dot_general | solution.py:839
  321.8 2.7 collective-permute-done.18
  327.9 17.7 %attend_back.6 = (bf16[512,1280]{1,0:T(8,128)(2,1)}, bf16[2048,640]{1,0:T(8,128)(2,1)}, bf16[2048,640]{1,0:T(8,128)(2,1)}) custom-call(s32[4]{0:T(128)S(1)} %pad_add_fusion.1.refs_0_, bf16[512,1280]{1,0:T(8,128)(2,1)} %get-tuple-element.50.refs_0_.refs_1_, ...), custom_call_target="tpu_custom_call", output_to_operand_aliasing={{0}: (1, {}), {1}: (2, {}), {2}: (3, {})} | custom-call | flops 8305200128 | tf_op jit(solution)/shard_map/attend_back/pallas_call | solution.py:393
  345.7 12.3 %collective-permute-start.21 = (bf16[320,1792]{1,0:T(8,128)(2,1)}, bf16[320,1792]{1,0:T(8,128)(2,1)S(1)}, u32[]{:S(2)}, u32[]{:S(2)}) collective-permute-start(bf16[320,1792]{1,0:T(8,128)(2,1)} %reduce-scatter.9.cloned.1.call-done.refs_5_), channel_id=1, source_target_pairs={{0,8},{4,12},{24,16},{28,20},{1,9},{5,13},{25,17},{29,21},{2,10},{... | collective-permute-start | bytes 3440648 | tf_op jit(solution)/shard_map/ppermute | solution.py:683
  364.3 17.4 %attend_back.7 = (bf16[512,1280]{1,0:T(8,128)(2,1)}, bf16[2048,640]{1,0:T(8,128)(2,1)}, bf16[2048,640]{1,0:T(8,128)(2,1)}) custom-call(s32[4]{0:T(128)S(1)} %pad_add_fusion.1.refs_0_, bf16[512,1280]{1,0:T(8,128)(2,1)} %get-tuple-element.53.refs_1_, ...), custom_call_target="tpu_custom_call", output_to_operand_aliasing={{0}: (1, {}), {1}: (2, {}), {2}: (3, {})} | custom-call | flops 8305200128 | tf_op jit(solution)/shard_map/attend_back/pallas_call | solution.py:393
  381.7 17.3 %attend_back.8 = (bf16[512,1280]{1,0:T(8,128)(2,1)}, bf16[2048,640]{1,0:T(8,128)(2,1)}, bf16[2048,640]{1,0:T(8,128)(2,1)}) custom-call(s32[4]{0:T(128)S(1)} %pad_add_fusion.1.refs_0_, bf16[512,1280]{1,0:T(8,128)(2,1)} %get-tuple-element.56.refs_1_, ...), custom_call_target="tpu_custom_call", output_to_operand_aliasing={{0}: (1, {}), {1}: (2, {}), {2}: (3, {})} | custom-call | flops 8305200128 | tf_op jit(solution)/shard_map/attend_back/pallas_call | solution.py:393
  399.0 17.4 %attend_back.9 = (bf16[512,1280]{1,0:T(8,128)(2,1)}, bf16[2048,640]{1,0:T(8,128)(2,1)}, bf16[2048,640]{1,0:T(8,128)(2,1)}) custom-call(s32[4]{0:T(128)S(1)} %pad_add_fusion.1.refs_0_, bf16[512,1280]{1,0:T(8,128)(2,1)} %get-tuple-element.59.refs_1_, ...), custom_call_target="tpu_custom_call", output_to_operand_aliasing={{0}: (1, {}), {1}: (2, {}), {2}: (3, {})} | custom-call | flops 8305200128 | tf_op jit(solution)/shard_map/attend_back/pallas_call | solution.py:393
  416.3 3.3 collective-permute-start.26
  419.7 4.7 collective-permute-done.26
  424.4 4.1 add.144
  431.5 3.2 outer_rows.4
  434.8 3.2 outer_rows.5
  438.7 5.5 collective-permute-done.31
  455.8 3.0 add.143
  460.0 40.9 %collective-permute-done.22.refs_1_ = bf16[320,1792]{1,0:T(8,128)(2,1)S(1)} collective-permute-done((bf16[320,1792]{1,0:T(8,128)(2,1)}, bf16[320,1792]{1,0:T(8,128)(2,1)S(1)}, u32[]{:S(2)}, u32[]{:S(2)}) %collective-permute-start.22) | collective-permute-done | bytes 1146912 | tf_op jit(solution)/shard_map/ppermute | solution.py:683
  504.4 4.8 fusion.50.refs_0_
  509.2 16.2 %collective-permute-done.23.refs_2_ = bf16[448,1280]{1,0:T(8,128)(2,1)} collective-permute-done((bf16[448,1280]{1,0:T(8,128)(2,1)}, bf16[448,1280]{1,0:T(8,128)(2,1)}, u32[]{:S(2)}, u32[]{:S(2)}) %collective-permute-start.23) | collective-permute-done | bytes 1146912 | tf_op jit(solution)/shard_map/ppermute | solution.py:683
  525.4 2.9 add.151
  530.1 4.3 collective-permute-done.25.refs_3_
  535.9 3.1 add.150
  543.0 6.0 fusion.14
  551.2 3.0 add.152
  555.6 4.3 merge_columns.2
  559.8 10.1 %collective-permute-done.35 = bf16[320,1792]{1,0:T(8,128)(2,1)} collective-permute-done((bf16[320,1792]{1,0:T(8,128)(2,1)}, bf16[320,1792]{1,0:T(8,128)(2,1)}, u32[]{:S(2)}, u32[]{:S(2)}) %collective-permute-start.35) | collective-permute-done | bytes 1146912 | tf_op jit(solution)/shard_map/ppermute | solution.py:683
  572.6 21.8 %collective-permute-done.38 = bf16[448,1280]{1,0:T(8,128)(2,1)} collective-permute-done((bf16[448,1280]{1,0:T(8,128)(2,1)}, bf16[448,1280]{1,0:T(8,128)(2,1)}, u32[]{:S(2)}, u32[]{:S(2)}) %collective-permute-start.38) | collective-permute-done | bytes 1146912 | tf_op jit(solution)/shard_map/ppermute | solution.py:683
  600.3 6.5 collective-permute-start.27
  608.7 2.7 merge_columns.3
  613.9 63.8 %all-reduce.6.cloned.1.call-done = (bf16[176,640]{1,0:T(8,128)(2,1)}, bf16[160,2560]{1,0:T(8,128)(2,1)}) async-done(((bf16[176,640]{1,0:T(8,128)(2,1)}, bf16[160,2560]{1,0:T(8,128)(2,1)}), (bf16[176,640]{1,0:T(8,128)(2,1)}, bf16[160,2560]{1,0:T(8,128)(2,1)})) %all-reduce.6.cloned.1.call-update) | async-done | bytes 1044496 | tf_op jit(solution)/shard_map/psum | solution.py:680
  (343 shorter events, 145.4 us)
Async XLA Ops:
  7.2 56.3 %all-gather.7.cloned.1.call-start = ((), (), s32[]{:S(2)}) async-start(), calls=%async_computation.7 | async-start | bytes 2048000 | tf_op jit(solution)/shard_map/all_gather | solution.py:617
  10.8 12.2 %collective-permute-start.3 = (bf16[176,640]{1,0:T(8,128)(2,1)S(1)}, bf16[176,640]{1,0:T(8,128)(2,1)S(1)}, u32[]{:S(2)}, u32[]{:S(2)}) collective-permute-start(bf16[176,640]{1,0:T(8,128)(2,1)S(1)} %fusion.29.refs_0_), channel_id=1, source_target_pairs={{0,2},{1,3},{2,0},{3,1},{4,6},{5,7},{6,4},{7,5},{8,10},{9,11},{10,... | collective-permute-start | bytes 675848 | tf_op jit(solution)/shard_map/ppermute | solution.py:577
  13.8 10.1 %collective-permute-start.2 = (bf16[176,640]{1,0:T(8,128)(2,1)S(1)}, bf16[176,640]{1,0:T(8,128)(2,1)S(1)}, u32[]{:S(2)}, u32[]{:S(2)}) collective-permute-start(bf16[176,640]{1,0:T(8,128)(2,1)S(1)} %fusion.29.refs_0_), channel_id=1, source_target_pairs={{0,1},{1,0},{2,3},{3,2},{4,5},{5,4},{6,7},{7,6},{8,9},{9,8},{10,11... | collective-permute-start | bytes 675848 | tf_op jit(solution)/shard_map/ppermute | solution.py:577
  17.1 105.8 %all-gather.5.cloned.1.call-start = ((), (), s32[]{:S(2)}) async-start(), calls=%async_computation.6 | async-start | bytes 5898240 | tf_op jit(solution)/shard_map/all_gather | solution.py:775
  18.3 16.5 %collective-permute-start = (bf16[256,1280]{1,0:T(8,128)(2,1)}, bf16[256,1280]{1,0:T(8,128)(2,1)S(1)}, u32[]{:S(2)}, u32[]{:S(2)}) collective-permute-start(bf16[256,1280]{1,0:T(8,128)(2,1)} %get-tuple-element.135), channel_id=1, source_target_pairs={{0,0},{4,8},{8,16},{12,24},{16,28},{20,20},{24,12},{28,4},{1,1},{5... | collective-permute-start | bytes 1966088 | tf_op jit(solution)/shard_map/ppermute | solution.py:592
  20.0 30.8 %collective-permute-start.1 = (bf16[256,1280]{1,0:T(8,128)(2,1)}, bf16[256,1280]{1,0:T(8,128)(2,1)}, u32[]{:S(2)}, u32[]{:S(2)}) collective-permute-start(bf16[256,1280]{1,0:T(8,128)(2,1)} %get-tuple-element.136), channel_id=1, source_target_pairs={{0,4},{4,12},{8,20},{12,28},{16,24},{20,16},{24,8},{28,0},{1,5},{5... | collective-permute-start | bytes 1966088 | tf_op jit(solution)/shard_map/ppermute | solution.py:592
  23.0 8.2 %collective-permute-start.5 = (bf16[96,640]{1,0:T(8,128)(2,1)S(1)}, bf16[96,640]{1,0:T(8,128)(2,1)S(1)}, u32[]{:S(2)}, u32[]{:S(2)}) collective-permute-start(bf16[96,640]{1,0:T(8,128)(2,1)S(1)} %slice.161), channel_id=1, source_target_pairs={{0,1},{1,0},{2,3},{3,2},{4,5},{5,4},{6,7},{7,6},{8,9},{9,8},{10,11... | collective-permute-start | bytes 368648 | tf_op jit(solution)/shard_map/ppermute | solution.py:577
  23.9 7.3 %collective-permute-start.4 = (bf16[80,640]{1,0:T(8,128)(2,1)S(1)}, bf16[80,640]{1,0:T(8,128)(2,1)S(1)}, u32[]{:S(2)}, u32[]{:S(2)}) collective-permute-start(bf16[80,640]{1,0:T(8,128)(2,1)S(1)} %slice.160), channel_id=1, source_target_pairs={{0,2},{1,3},{2,0},{3,1},{4,6},{5,7},{6,4},{7,5},{8,10},{9,11},{10,... | collective-permute-start | bytes 307208 | tf_op jit(solution)/shard_map/ppermute | solution.py:577
  33.1 21.2 %collective-permute-start.6 = (bf16[4,160,640]{2,1,0:T(8,128)(2,1)S(1)}, bf16[4,160,640]{2,1,0:T(8,128)(2,1)}, u32[]{:S(2)}, u32[]{:S(2)}) collective-permute-start(bf16[4,160,640]{2,1,0:T(8,128)(2,1)S(1)} %slice.164), channel_id=1, source_target_pairs={{0,4},{4,0},{8,12},{12,8},{16,20},{20,16},{24,28},{28,24},{1,5},{5... | collective-permute-start | bytes 2457608 | tf_op jit(solution)/shard_map/ppermute | solution.py:580
  59.9 106.3 %all-gather.9.cloned.1.call-start = ((), (), s32[]{:S(2)}) async-start(), calls=%async_computation.8 | async-start | bytes 2048000 | tf_op jit(solution)/shard_map/all_gather | solution.py:617
  63.5 3.8 collective-permute-start.7
  65.2 50.8 %collective-permute-start.11 = (bf16[320,3584]{1,0:T(8,128)(2,1)S(1)}, bf16[320,3584]{1,0:T(8,128)(2,1)}, u32[]{:S(2)}, u32[]{:S(2)}) collective-permute-start(bf16[320,3584]{1,0:T(8,128)(2,1)S(1)} %copy-done.2), channel_id=1, source_target_pairs={{0,2},{1,3},{2,0},{3,1},{4,6},{5,7},{6,4},{7,5},{8,10},{9,11},{10,... | collective-permute-start | bytes 6881288 | tf_op jit(solution)/shard_map/ppermute | solution.py:577
  65.7 50.5 %collective-permute-start.10 = (bf16[320,3584]{1,0:T(8,128)(2,1)S(1)}, bf16[320,3584]{1,0:T(8,128)(2,1)}, u32[]{:S(2)}, u32[]{:S(2)}) collective-permute-start(bf16[320,3584]{1,0:T(8,128)(2,1)S(1)} %copy-done.2), channel_id=1, source_target_pairs={{0,1},{1,0},{2,3},{3,2},{4,5},{5,4},{6,7},{7,6},{8,9},{9,8},{10,11... | collective-permute-start | bytes 6881288 | tf_op jit(solution)/shard_map/ppermute | solution.py:577
  78.8 147.8 %all-gather.11.cloned.1.call-start = ((), (), s32[]{:S(2)}) async-start(), calls=%async_computation.9 | async-start | bytes 5734400 | tf_op jit(solution)/shard_map/all_gather | solution.py:617
  120.8 47.8 %collective-permute-start.13 = (bf16[160,3584]{1,0:T(8,128)(2,1)}, bf16[160,3584]{1,0:T(8,128)(2,1)S(1)}, u32[]{:S(2)}, u32[]{:S(2)}) collective-permute-start(bf16[160,3584]{1,0:T(8,128)(2,1)} %slice.134), channel_id=1, source_target_pairs={{0,1},{1,0},{2,3},{3,2},{4,5},{5,4},{6,7},{7,6},{8,9},{9,8},{10,11... | collective-permute-start | bytes 3440648 | tf_op jit(solution)/shard_map/ppermute | solution.py:577
  121.4 47.2 %collective-permute-start.12 = (bf16[160,3584]{1,0:T(8,128)(2,1)}, bf16[160,3584]{1,0:T(8,128)(2,1)}, u32[]{:S(2)}, u32[]{:S(2)}) collective-permute-start(bf16[160,3584]{1,0:T(8,128)(2,1)} %slice.133), channel_id=1, source_target_pairs={{0,2},{1,3},{2,0},{3,1},{4,6},{5,7},{6,4},{7,5},{8,10},{9,11},{10,... | collective-permute-start | bytes 3440648 | tf_op jit(solution)/shard_map/ppermute | solution.py:577
  128.1 50.4 %collective-permute-start.9 = (bf16[256,1280]{1,0:T(8,128)(2,1)}, bf16[256,1280]{1,0:T(8,128)(2,1)}, u32[]{:S(2)}, u32[]{:S(2)}) collective-permute-start(bf16[256,1280]{1,0:T(8,128)(2,1)} %get-tuple-element.133), channel_id=1, source_target_pairs={{0,4},{4,12},{8,20},{12,28},{16,24},{20,16},{24,8},{28,0},{1,5},{5... | collective-permute-start | bytes 1966088 | tf_op jit(solution)/shard_map/ppermute | solution.py:592
  128.1 48.5 %collective-permute-start.8 = (bf16[256,1280]{1,0:T(8,128)(2,1)}, bf16[256,1280]{1,0:T(8,128)(2,1)}, u32[]{:S(2)}, u32[]{:S(2)}) collective-permute-start(bf16[256,1280]{1,0:T(8,128)(2,1)} %get-tuple-element.134), channel_id=1, source_target_pairs={{0,0},{4,8},{8,16},{12,24},{16,28},{20,20},{24,12},{28,4},{1,1},{5... | collective-permute-start | bytes 1966088 | tf_op jit(solution)/shard_map/ppermute | solution.py:592
  166.2 35.8 %collective-permute-start.14 = (bf16[4,160,1280]{2,1,0:T(8,128)(2,1)}, bf16[4,160,1280]{2,1,0:T(8,128)(2,1)}, u32[]{:S(2)}, u32[]{:S(2)}) collective-permute-start(bf16[4,160,1280]{2,1,0:T(8,128)(2,1)} %bitcast.91), channel_id=1, source_target_pairs={{0,4},{4,0},{8,12},{12,8},{16,20},{20,16},{24,28},{28,24},{1,5},{5... | collective-permute-start | bytes 4915208 | tf_op jit(solution)/shard_map/ppermute | solution.py:580
  168.6 177.2 %reduce-scatter.9.cloned.1.call-start = ((), (), s32[]{:S(2)}) async-start(), calls=%async_computation.10 | async-start | bytes 5734400 | tf_op jit(solution)/shard_map/reduce_scatter | solution.py:821
  209.0 3.4 collective-permute-start.15
  211.1 15.5 %collective-permute-start.16 = (bf16[512,1280]{1,0:T(8,128)(2,1)}, bf16[512,1280]{1,0:T(8,128)(2,1)}, u32[]{:S(2)}, u32[]{:S(2)}) collective-permute-start(bf16[512,1280]{1,0:T(8,128)(2,1)} %fusion.18), channel_id=1, source_target_pairs={{0,4},{4,0},{8,12},{12,8},{16,20},{20,16},{24,28},{28,24},{1,5},{5... | collective-permute-start | bytes 3932168 | tf_op jit(solution)/shard_map/ppermute | solution.py:580
  250.3 201.0 %reduce-scatter.11.cloned.1.call-start = ((), (), s32[]{:S(2)}) async-start(), calls=%async_computation.11 | async-start | bytes 5734400 | tf_op jit(solution)/shard_map/reduce_scatter | solution.py:821
  260.4 191.0 %reduce-scatter.13.cloned.1.call-start = ((), (), s32[]{:S(2)}) async-start(), calls=%async_computation.12 | async-start | bytes 5734400 | tf_op jit(solution)/shard_map/reduce_scatter | solution.py:821
  312.9 227.4 %reduce-scatter.15.cloned.1.call-start = ((), (), s32[]{:S(2)}) async-start(), calls=%async_computation.13 | async-start | bytes 3276800 | tf_op jit(solution)/shard_map/reduce_scatter | solution.py:651
  325.1 20.5 %collective-permute-start.20 = (bf16[256,1280]{1,0:T(8,128)(2,1)S(1)}, bf16[256,1280]{1,0:T(8,128)(2,1)S(1)}, u32[]{:S(2)}, u32[]{:S(2)}) collective-permute-start(bf16[256,1280]{1,0:T(8,128)(2,1)S(1)} %get-tuple-element.131), channel_id=1, source_target_pairs={{4,0},{12,4},{20,8},{28,12},{24,16},{16,20},{8,24},{0,28},{5,1},{1... | collective-permute-start | bytes 1966088 | tf_op jit(solution)/shard_map/ppermute | solution.py:606
  327.2 18.4 %collective-permute-start.19 = (bf16[256,1280]{1,0:T(8,128)(2,1)S(1)}, bf16[256,1280]{1,0:T(8,128)(2,1)S(1)}, u32[]{:S(2)}, u32[]{:S(2)}) collective-permute-start(bf16[256,1280]{1,0:T(8,128)(2,1)S(1)} %get-tuple-element.132), channel_id=1, source_target_pairs={{0,0},{8,4},{16,8},{24,12},{28,16},{20,20},{12,24},{4,28},{1,1},{9... | collective-permute-start | bytes 1966088 | tf_op jit(solution)/shard_map/ppermute | solution.py:606
  345.7 53.3 %collective-permute-start.21 = (bf16[320,1792]{1,0:T(8,128)(2,1)}, bf16[320,1792]{1,0:T(8,128)(2,1)S(1)}, u32[]{:S(2)}, u32[]{:S(2)}) collective-permute-start(bf16[320,1792]{1,0:T(8,128)(2,1)} %reduce-scatter.9.cloned.1.call-done.refs_5_), channel_id=1, source_target_pairs={{0,8},{4,12},{24,16},{28,20},{1,9},{5,13},{25,17},{29,21},{2,10},{... | collective-permute-start | bytes 3440648 | tf_op jit(solution)/shard_map/ppermute | solution.py:683
  416.3 8.1 %collective-permute-start.26 = (bf16[2048,640]{1,0:T(8,128)(2,1)}, bf16[2048,640]{1,0:T(8,128)(2,1)S(1)}, u32[]{:S(2)}, u32[]{:S(2)}) collective-permute-start(bf16[2048,640]{1,0:T(8,128)(2,1)} %get-tuple-element.66), channel_id=1, source_target_pairs={{0,4},{4,0},{8,12},{12,8},{16,20},{20,16},{24,28},{28,24},{1,5},{5... | collective-permute-start | bytes 7864328 | tf_op jit(solution)/shard_map/ppermute | solution.py:580
  428.5 178.3 %reduce-scatter.17.cloned.1.call-start = ((), (), s32[]{:S(2)}) async-start(), calls=%async_computation.14 | async-start | bytes 4096000 | tf_op jit(solution)/shard_map/reduce_scatter | solution.py:821
  438.3 5.9 collective-permute-start.31
  446.7 160.2 %reduce-scatter.19.cloned.1.call-start = ((), (), s32[]{:S(2)}) async-start(), calls=%async_computation.15 | async-start | bytes 1126400
  449.6 6.1 collective-permute-start.24
  451.4 49.6 %collective-permute-start.22 = (bf16[320,1792]{1,0:T(8,128)(2,1)}, bf16[320,1792]{1,0:T(8,128)(2,1)S(1)}, u32[]{:S(2)}, u32[]{:S(2)}) collective-permute-start(bf16[320,1792]{1,0:T(8,128)(2,1)} %get-tuple-element.63), channel_id=1, source_target_pairs={{0,8},{4,12},{24,16},{28,20},{1,9},{5,13},{25,17},{29,21},{2,10},{... | collective-permute-start | bytes 3440648 | tf_op jit(solution)/shard_map/ppermute | solution.py:683
  453.1 72.3 %collective-permute-start.23 = (bf16[448,1280]{1,0:T(8,128)(2,1)}, bf16[448,1280]{1,0:T(8,128)(2,1)}, u32[]{:S(2)}, u32[]{:S(2)}) collective-permute-start(bf16[448,1280]{1,0:T(8,128)(2,1)} %get-tuple-element.64), channel_id=1, source_target_pairs={{0,8},{4,12},{24,16},{28,20},{1,9},{5,13},{25,17},{29,21},{2,10},{... | collective-permute-start | bytes 3440648 | tf_op jit(solution)/shard_map/ppermute | solution.py:683
  458.7 75.6 %collective-permute-start.25 = (bf16[320,1792]{1,0:T(8,128)(2,1)}, bf16[320,1792]{1,0:T(8,128)(2,1)}, u32[]{:S(2)}, u32[]{:S(2)}) collective-permute-start(bf16[320,1792]{1,0:T(8,128)(2,1)} %add.143), channel_id=1, source_target_pairs={{8,0},{12,4},{16,24},{20,28},{9,1},{13,5},{17,25},{21,29},{10,2},{... | collective-permute-start | bytes 3440648 | tf_op jit(solution)/shard_map/ppermute | solution.py:683
  502.4 33.5 %collective-permute-start.34 = (bf16[320,1792]{1,0:T(8,128)(2,1)}, bf16[320,1792]{1,0:T(8,128)(2,1)}, u32[]{:S(2)}, u32[]{:S(2)}) collective-permute-start(bf16[320,1792]{1,0:T(8,128)(2,1)} %add.149), channel_id=1, source_target_pairs={{8,16},{12,20},{16,8},{20,12},{9,17},{13,21},{17,9},{21,13},{10,18... | collective-permute-start | bytes 3440648 | tf_op jit(solution)/shard_map/ppermute | solution.py:683
  528.3 22.9 %collective-permute-start.37 = (bf16[448,1280]{1,0:T(8,128)(2,1)}, bf16[448,1280]{1,0:T(8,128)(2,1)}, u32[]{:S(2)}, u32[]{:S(2)}) collective-permute-start(bf16[448,1280]{1,0:T(8,128)(2,1)} %add.151), channel_id=1, source_target_pairs={{8,16},{12,20},{16,8},{20,12},{9,17},{13,21},{17,9},{21,13},{10,18... | collective-permute-start | bytes 3440648 | tf_op jit(solution)/shard_map/ppermute | solution.py:683
  535.8 19.8 %collective-permute-start.33 = (bf16[320,1792]{1,0:T(8,128)(2,1)S(1)}, bf16[320,1792]{1,0:T(8,128)(2,1)}, u32[]{:S(2)}, u32[]{:S(2)}) collective-permute-start(bf16[320,1792]{1,0:T(8,128)(2,1)S(1)} %broadcast_select_fusion.4.own_ref), channel_id=1, source_target_pairs={{0,4},{4,0},{8,12},{12,8},{16,20},{20,16},{24,28},{28,24},{1,5},{5... | collective-permute-start | bytes 3440648 | tf_op jit(solution)/shard_map/ppermute | solution.py:580
  538.9 31.0 %collective-permute-start.35 = (bf16[320,1792]{1,0:T(8,128)(2,1)}, bf16[320,1792]{1,0:T(8,128)(2,1)}, u32[]{:S(2)}, u32[]{:S(2)}) collective-permute-start(bf16[320,1792]{1,0:T(8,128)(2,1)} %add.150), channel_id=1, source_target_pairs={{8,0},{12,4},{16,24},{20,28},{9,1},{13,5},{17,25},{21,29},{10,2},{... | collective-permute-start | bytes 3440648 | tf_op jit(solution)/shard_map/ppermute | solution.py:683
  550.9 20.5 %collective-permute-start.29 = (bf16[4,176,640]{2,1,0:T(8,128)(2,1)S(1)}, bf16[4,176,640]{2,1,0:T(8,128)(2,1)S(1)}, u32[]{:S(2)}, u32[]{:S(2)}) collective-permute-start(bf16[4,176,640]{2,1,0:T(8,128)(2,1)S(1)} %pad_maximum_fusion.9), channel_id=1, source_target_pairs={{0,4},{4,0},{8,12},{12,8},{16,20},{20,16},{24,28},{28,24},{1,5},{5... | collective-permute-start | bytes 2703368 | tf_op jit(solution)/shard_map/ppermute | solution.py:580
  554.3 40.1 %collective-permute-start.38 = (bf16[448,1280]{1,0:T(8,128)(2,1)}, bf16[448,1280]{1,0:T(8,128)(2,1)}, u32[]{:S(2)}, u32[]{:S(2)}) collective-permute-start(bf16[448,1280]{1,0:T(8,128)(2,1)} %add.152), channel_id=1, source_target_pairs={{8,0},{12,4},{16,24},{20,28},{9,1},{13,5},{17,25},{21,29},{10,2},{... | collective-permute-start | bytes 3440648 | tf_op jit(solution)/shard_map/ppermute | solution.py:683
  571.3 37.4 %collective-permute-start.36 = (bf16[320,1792]{1,0:T(8,128)(2,1)S(1)}, bf16[320,1792]{1,0:T(8,128)(2,1)S(1)}, u32[]{:S(2)}, u32[]{:S(2)}) collective-permute-start(bf16[320,1792]{1,0:T(8,128)(2,1)S(1)} %broadcast_select_fusion.3.own_ref), channel_id=1, source_target_pairs={{0,4},{4,0},{8,12},{12,8},{16,20},{20,16},{24,28},{28,24},{1,5},{5... | collective-permute-start | bytes 3440648 | tf_op jit(solution)/shard_map/ppermute | solution.py:580
  572.6 105.2 %all-reduce.6.cloned.1.call-start = ((), (), s32[]{:S(2)}) async-start(), calls=%async_computation.16 | async-start | bytes 2088960 | tf_op jit(solution)/shard_map/psum | solution.py:680
  596.8 10.1 %collective-permute-start.39 = (bf16[448,1280]{1,0:T(8,128)(2,1)}, bf16[448,1280]{1,0:T(8,128)(2,1)}, u32[]{:S(2)}, u32[]{:S(2)}) collective-permute-start(bf16[448,1280]{1,0:T(8,128)(2,1)} %broadcast_select_fusion), channel_id=1, source_target_pairs={{0,4},{4,0},{8,12},{12,8},{16,20},{20,16},{24,28},{28,24},{1,5},{5... | collective-permute-start | bytes 3440648 | tf_op jit(solution)/shard_map/ppermute | solution.py:580
  600.3 77.4 %collective-permute-start.27 = (bf16[256,1280]{1,0:T(8,128)(2,1)}, bf16[256,1280]{1,0:T(8,128)(2,1)}, u32[]{:S(2)}, u32[]{:S(2)}) collective-permute-start(bf16[256,1280]{1,0:T(8,128)(2,1)} %get-tuple-element.129), channel_id=1, source_target_pairs={{0,0},{8,4},{16,8},{24,12},{28,16},{20,20},{12,24},{4,28},{1,1},{9... | collective-permute-start | bytes 1966088 | tf_op jit(solution)/shard_map/ppermute | solution.py:606
  606.9 70.9 %collective-permute-start.28 = (bf16[256,1280]{1,0:T(8,128)(2,1)S(1)}, bf16[256,1280]{1,0:T(8,128)(2,1)}, u32[]{:S(2)}, u32[]{:S(2)}) collective-permute-start(bf16[256,1280]{1,0:T(8,128)(2,1)S(1)} %get-tuple-element.130), channel_id=1, source_target_pairs={{4,0},{12,4},{20,8},{28,12},{24,16},{16,20},{8,24},{0,28},{5,1},{1... | collective-permute-start | bytes 1966088 | tf_op jit(solution)/shard_map/ppermute | solution.py:606
  680.3 6.9 collective-permute-start.32
  (74 other events, 681.9 us)
Sparse Core Ops, SparseCore 0:
  17.2 31.9 all-gather.6
  60.0 56.0 all-gather.4
  118.5 40.6 all-gather.8
  168.7 56.1 all-gather.10
  250.5 56.0 reduce-scatter.8
  310.1 55.9 reduce-scatter.10
  369.7 55.9 reduce-scatter.12
  428.7 72.6 reduce-scatter.14
  504.9 59.9 reduce-scatter.16
  572.7 28.9 reduce-scatter.18
  607.0 70.6 all-reduce.5
